TPU v7x, 32 devices: a whole 2x2x4 slice. The times are simulated.
32 devices in a mesh: dp: 4 (over x, core), seq: 8 (over z, y).
Axes of the slice: x: 2, y: 2, z: 4, core: 2. Of those that a mesh axis runs over, the one named last changes fastest.
Arguments:
- tokens: bfloat16 [8, 1024, 2048], P('dp', 'seq'), may hold values from -6 to 6
- segments: int32 [8, 1024], P('dp'), may hold values from 0 to 5, never falling along the last dimension, each value on 1 to 256 neighbouring positions
- routes: int32 [8, 1024, 8], P('dp', 'seq'), may hold values from 0 to 31, as said below
- cotangent: bfloat16 [8, 1024, 2048], P('dp', 'seq'), may hold values from -6 to 6
- attn_weight: bfloat16 [2048, 4, 2048], P(('dp', 'seq')), may hold values from -0.5 to 0.5
- router_weight: bfloat16 [2048, 32], P(('dp', 'seq')), may hold values from -0.0625 to 0.0625
- norm_gains: bfloat16 [4, 2048], P(None, ('dp', 'seq')), may hold values from 0.5 to 1.5
- expert_in: bfloat16 [32, 2048, 2, 1024], P('seq', 'dp'), may hold values from -0.125 to 0.125
- expert_out: bfloat16 [32, 1024, 2048], P('seq', None, 'dp'), may hold values from -6 to 6
Outputs:
- block_out: bfloat16 [8, 1024, 2048], P('dp', 'seq')
- input_grad: float32 [8, 1024, 2048], P('dp', 'seq')
- attn_grad: float32 [2048, 4, 2048], P(('dp', 'seq'))
- router_grad: float32 [2048, 32], P(('dp', 'seq'))
- gain_grad: float32 [4, 2048], P(None, ('dp', 'seq'))
- expert_in_grad: float32 [32, 2048, 2, 1024], P('seq', 'dp')
- expert_out_grad: float32 [32, 1024, 2048], P('seq', None, 'dp')
Inputs may be any that keep to these rules, and one draw needn't show every extreme that they name: `segments`: block numbers never fall along a sequence; each block has at most 256 positions. `routes`: each token names 8 different experts.
All inputs are finite; a program needn't handle non-finite values.
Results may differ from a plain program's by a relative error of at most 0.02.
Values may be sent and summed in bfloat16 or wider, within the bound.
A program may use at most 384 MiB of HBM per device.

v0:
```python
import math

import jax
import jax.numpy as jnp
from jax import lax
from jax.sharding import PartitionSpec as P

HEADS = 16
HEAD_DIM = 128


NORM_EPS = 1e-05
ROPE_BASE = 10000.0
MASKED_SCORE = -1e30


def rms_factor(values):
    return lax.rsqrt(jnp.mean(values * values, axis=-1, keepdims=True) + NORM_EPS)


def norm_back(values, factor, gain_row, incoming):
    scaled = incoming * gain_row
    gain_part = jnp.sum(incoming * values * factor, axis=0)
    inner = jnp.mean(scaled * values, axis=-1, keepdims=True)
    return (factor * (scaled - values * factor * factor * inner), gain_part)


def rotary(positions):
    half_dim = HEAD_DIM // 2
    freqs = jnp.exp(
        -math.log(ROPE_BASE) * (2.0 * jnp.arange(half_dim, dtype=jnp.float32) / HEAD_DIM)
    )
    angles = positions.astype(jnp.float32)[:, None] * freqs[None, :]
    return (jnp.cos(angles)[:, None, :], jnp.sin(angles)[:, None, :])


def rotate(values, cosine, sine):
    half_dim = values.shape[-1] // 2
    first = values[..., :half_dim]
    second = values[..., half_dim:]
    return jnp.concatenate(
        [first * cosine - second * sine, second * cosine + first * sine], axis=-1
    )


def attend_forward(pieces):
    queries, key_rows, value_rows, seg_ids = pieces
    score_scale = HEAD_DIM ** (-0.5)
    scores = (
        jnp.einsum("qhd,khd->hqk", queries, key_rows, preferred_element_type=jnp.float32)
        * score_scale
    )
    allowed = seg_ids[None, :] <= seg_ids[:, None]
    scores = jnp.where(allowed[None], scores, MASKED_SCORE)
    row_max = jnp.max(scores, axis=-1, keepdims=True)
    exp_scores = jnp.exp(scores - row_max)
    row_sum = jnp.sum(exp_scores, axis=-1, keepdims=True)
    attn_probs = exp_scores / row_sum
    attended = jnp.einsum(
        "hqk,khd->qhd",
        attn_probs.astype(jnp.bfloat16),
        value_rows,
        preferred_element_type=jnp.float32,
    )
    return (attended.astype(jnp.bfloat16), (row_max + jnp.log(row_sum))[..., 0])


def attend_backward(pieces):
    queries, key_rows, value_rows, grad_out, log_norm, seg_ids = pieces
    score_scale = HEAD_DIM ** (-0.5)
    scores = (
        jnp.einsum("qhd,khd->hqk", queries, key_rows, preferred_element_type=jnp.float32)
        * score_scale
    )
    allowed = seg_ids[None, :] <= seg_ids[:, None]
    attn_probs = jnp.where(allowed[None], jnp.exp(scores - log_norm[..., None]), 0.0)
    grad_probs = jnp.einsum(
        "qhd,khd->hqk", grad_out, value_rows, preferred_element_type=jnp.float32
    )
    inner = jnp.sum(attn_probs * grad_probs, axis=-1, keepdims=True)
    grad_scores = (attn_probs * (grad_probs - inner)).astype(jnp.bfloat16)
    grad_query = (
        jnp.einsum("hqk,khd->qhd", grad_scores, key_rows, preferred_element_type=jnp.float32)
        * score_scale
    )
    grad_key = (
        jnp.einsum("hqk,qhd->khd", grad_scores, queries, preferred_element_type=jnp.float32)
        * score_scale
    )
    grad_value = jnp.einsum(
        "hqk,qhd->khd",
        attn_probs.astype(jnp.bfloat16),
        grad_out,
        preferred_element_type=jnp.float32,
    )
    return (
        grad_query.astype(jnp.bfloat16),
        grad_key.astype(jnp.bfloat16),
        grad_value.astype(jnp.bfloat16),
    )


def swiglu(gate_vals, up_vals):
    return jax.nn.silu(gate_vals) * up_vals


def local(
    tokens,
    segments,
    routes,
    cotangent,
    attn_weight,
    router_weight,
    norm_gains,
    expert_in,
    expert_out,
):
    attn_full, router_full, gains_full = (
        lax.all_gather(attn_weight, ("dp", "seq"), axis=0, tiled=True),
        lax.all_gather(router_weight, ("dp", "seq"), axis=0, tiled=True),
        lax.all_gather(norm_gains, ("dp", "seq"), axis=1, tiled=True),
    )
    in_full, out_full = (
        lax.all_gather(expert_in, "dp", axis=1, tiled=True),
        lax.all_gather(expert_out, "dp", axis=2, tiled=True),
    )
    num_seqs, local_len, model_width = tokens.shape
    seq_length = segments.shape[1]
    groups = lax.axis_size("seq")
    heads_here = HEADS // groups
    tok_count = num_seqs * local_len
    gain_rows = gains_full.astype(jnp.float32)
    resid_in = tokens.astype(jnp.float32).reshape(tok_count, model_width)
    factor_attn = rms_factor(resid_in)
    normed_low = (resid_in * factor_attn * gain_rows[0]).astype(jnp.bfloat16)
    projected_rows = jnp.einsum(
        "td,dje->jte", normed_low, attn_full[:, :3], preferred_element_type=jnp.float32
    )
    query_raw = projected_rows[0]
    key_raw = projected_rows[1]
    factor_query = rms_factor(query_raw)
    factor_key = rms_factor(key_raw)
    positions = lax.axis_index("seq") * local_len + jnp.arange(local_len, dtype=jnp.int32)
    cosine, sine = rotary(positions)

    def to_heads(values):
        return values.reshape(num_seqs, local_len, HEADS, HEAD_DIM)

    query_send = (
        rotate(to_heads(query_raw * factor_query * gain_rows[1]), cosine, sine)
        .reshape(num_seqs, local_len, model_width)
        .astype(jnp.bfloat16)
    )
    key_send = (
        rotate(to_heads(key_raw * factor_key * gain_rows[2]), cosine, sine)
        .reshape(num_seqs, local_len, model_width)
        .astype(jnp.bfloat16)
    )
    value_send = projected_rows[2].reshape(num_seqs, local_len, model_width).astype(jnp.bfloat16)
    query_head, key_head, value_head = (
        lax.all_to_all(query_send, "seq", split_axis=2, concat_axis=1, tiled=True),
        lax.all_to_all(key_send, "seq", split_axis=2, concat_axis=1, tiled=True),
        lax.all_to_all(value_send, "seq", split_axis=2, concat_axis=1, tiled=True),
    )
    head_shape = (num_seqs, seq_length, heads_here, HEAD_DIM)
    query_head = query_head.reshape(head_shape)
    key_head = key_head.reshape(head_shape)
    value_head = value_head.reshape(head_shape)
    attended, log_norm = lax.map(attend_forward, (query_head, key_head, value_head, segments))
    attn_tok = lax.all_to_all(
        attended.reshape(num_seqs, seq_length, heads_here * HEAD_DIM),
        "seq",
        split_axis=1,
        concat_axis=2,
        tiled=True,
    )
    attn_flat = attn_tok.reshape(tok_count, model_width)
    middle = resid_in + jnp.dot(attn_flat, attn_full[:, 3], preferred_element_type=jnp.float32)
    factor_ffn = rms_factor(middle)
    ffn_low = (middle * factor_ffn * gain_rows[3]).astype(jnp.bfloat16)
    router_scores = jnp.dot(ffn_low, router_full, preferred_element_type=jnp.float32)
    route_probs = jax.nn.softmax(router_scores, axis=-1)
    experts_all = router_full.shape[1]
    route_width = routes.shape[-1]
    capacity = (9 * tok_count * route_width + 8 * experts_all - 1) // (8 * experts_all)
    route_ids = routes.reshape(tok_count, route_width)
    route_hit = route_ids[:, :, None] == jnp.arange(experts_all, dtype=jnp.int32)[None, None, :]
    expert_hits = jnp.sum(route_hit, axis=1).astype(jnp.bfloat16)
    token_ids = jnp.arange(tok_count, dtype=jnp.int32)
    earlier = (token_ids[:, None] > token_ids[None, :]).astype(jnp.bfloat16)
    earlier_hits = jnp.dot(earlier, expert_hits, preferred_element_type=jnp.float32)
    pair_slot = jnp.sum(jnp.where(route_hit, earlier_hits[:, None, :], 0.0), axis=-1).astype(
        jnp.int32
    )
    kept_pair = pair_slot < capacity
    pair_gate = jnp.where(
        kept_pair, jnp.sum(jnp.where(route_hit, route_probs[:, None, :], 0.0), axis=-1), 0.0
    )
    slot_place = jnp.where(kept_pair, route_ids * capacity + pair_slot, -1)
    safe_place = jnp.where(kept_pair, slot_place, 0).reshape(-1)
    slot_table = (
        slot_place[:, :, None] == jnp.arange(experts_all * capacity, dtype=jnp.int32)[None, None, :]
    )
    slot_owner = jnp.sum(jnp.where(slot_table, token_ids[:, None, None], 0), axis=(0, 1))
    slot_live = jnp.any(slot_table, axis=(0, 1))
    slot_gate = jnp.sum(jnp.where(slot_table, pair_gate[:, :, None], 0.0), axis=(0, 1))
    sent_rows = jnp.where(
        slot_live[:, None], jnp.take(ffn_low, slot_owner, axis=0), jnp.zeros((), jnp.bfloat16)
    )
    received = lax.all_to_all(
        sent_rows.reshape(experts_all, capacity, model_width),
        "seq",
        split_axis=0,
        concat_axis=1,
        tiled=True,
    )
    gate_up = jnp.einsum("erd,edjf->erjf", received, in_full, preferred_element_type=jnp.float32)
    hidden_f, swiglu_pull = jax.vjp(swiglu, gate_up[:, :, 0], gate_up[:, :, 1])
    hidden = hidden_f.astype(jnp.bfloat16)
    expert_res = jnp.einsum(
        "erf,efd->erd", hidden, out_full, preferred_element_type=jnp.float32
    ).astype(jnp.bfloat16)
    returned = lax.all_to_all(expert_res, "seq", split_axis=1, concat_axis=0, tiled=True).reshape(
        experts_all * capacity, model_width
    )
    pair_out = jnp.take(returned, safe_place, axis=0).reshape(tok_count, route_width, model_width)
    mixed = jnp.sum(pair_gate[:, :, None] * pair_out, axis=1)
    block_out = (middle + mixed).astype(jnp.bfloat16).reshape(num_seqs, local_len, model_width)
    cot_low = cotangent.reshape(tok_count, model_width)
    cot_float = cot_low.astype(jnp.float32)
    grad_gate = jnp.where(
        kept_pair,
        jnp.einsum("td,trd->tr", cot_low, pair_out, preferred_element_type=jnp.float32),
        0.0,
    )
    slot_grad = (jnp.take(cot_float, slot_owner, axis=0) * slot_gate[:, None]).astype(jnp.bfloat16)
    grad_res = lax.all_to_all(
        slot_grad.reshape(experts_all, capacity, model_width),
        "seq",
        split_axis=0,
        concat_axis=1,
        tiled=True,
    )
    grad_hidden = jnp.einsum("erd,efd->erf", grad_res, out_full, preferred_element_type=jnp.float32)
    grad_gatev, grad_upv = swiglu_pull(grad_hidden)
    grad_gu = jnp.stack([grad_gatev, grad_upv], axis=2).astype(jnp.bfloat16)
    grad_rows = jnp.einsum(
        "erjf,edjf->erd", grad_gu, in_full, preferred_element_type=jnp.float32
    ).astype(jnp.bfloat16)
    grad_sent = lax.all_to_all(grad_rows, "seq", split_axis=1, concat_axis=0, tiled=True).reshape(
        experts_all * capacity, model_width
    )
    out_term = jnp.einsum("erf,erd->efd", hidden, grad_res, preferred_element_type=jnp.float32)
    in_term = jnp.einsum("erd,erjf->edjf", received, grad_gu, preferred_element_type=jnp.float32)
    expert_in_grad, expert_out_grad = (
        lax.psum_scatter(
            in_term.astype(jnp.bfloat16), "dp", scatter_dimension=1, tiled=True
        ).astype(jnp.float32),
        lax.psum_scatter(
            out_term.astype(jnp.bfloat16), "dp", scatter_dimension=2, tiled=True
        ).astype(jnp.float32),
    )
    grad_pairs = jnp.take(grad_sent, safe_place, axis=0).reshape(
        tok_count, route_width, model_width
    )
    grad_ffn = jnp.sum(
        jnp.where(kept_pair[:, :, None], grad_pairs.astype(jnp.float32), 0.0), axis=1
    )
    grad_prob = jnp.sum(jnp.where(route_hit, grad_gate[:, :, None], 0.0), axis=1)
    grad_logits = (
        route_probs * (grad_prob - jnp.sum(route_probs * grad_prob, axis=-1, keepdims=True))
    ).astype(jnp.bfloat16)
    router_term = jnp.einsum("td,te->de", ffn_low, grad_logits, preferred_element_type=jnp.float32)
    grad_ffn = grad_ffn + jnp.einsum(
        "te,de->td", grad_logits, router_full, preferred_element_type=jnp.float32
    )
    grad_middle, gain_ffn = norm_back(middle, factor_ffn, gain_rows[3], grad_ffn)
    grad_middle = grad_middle + cot_float
    branch_low = grad_middle.astype(jnp.bfloat16)
    out_proj_term = jnp.einsum(
        "td,te->de", attn_flat, branch_low, preferred_element_type=jnp.float32
    )
    grad_attn = jnp.einsum(
        "te,de->td", branch_low, attn_full[:, 3], preferred_element_type=jnp.float32
    ).astype(jnp.bfloat16)
    grad_head = lax.all_to_all(
        grad_attn.reshape(num_seqs, local_len, model_width),
        "seq",
        split_axis=2,
        concat_axis=1,
        tiled=True,
    )
    grad_q, grad_k, grad_v = lax.map(
        attend_backward,
        (query_head, key_head, value_head, grad_head.reshape(head_shape), log_norm, segments),
    )
    flat_shape = (num_seqs, seq_length, heads_here * HEAD_DIM)
    grad_qt, grad_kt, grad_vt = (
        lax.all_to_all(grad_q.reshape(flat_shape), "seq", split_axis=1, concat_axis=2, tiled=True),
        lax.all_to_all(grad_k.reshape(flat_shape), "seq", split_axis=1, concat_axis=2, tiled=True),
        lax.all_to_all(grad_v.reshape(flat_shape), "seq", split_axis=1, concat_axis=2, tiled=True),
    )
    grad_qn = rotate(to_heads(grad_qt.astype(jnp.float32)), cosine, -sine).reshape(
        tok_count, model_width
    )
    grad_kn = rotate(to_heads(grad_kt.astype(jnp.float32)), cosine, -sine).reshape(
        tok_count, model_width
    )
    grad_query_raw, gain_query = norm_back(query_raw, factor_query, gain_rows[1], grad_qn)
    grad_key_raw, gain_key = norm_back(key_raw, factor_key, gain_rows[2], grad_kn)
    grad_stack = jnp.stack(
        [
            grad_query_raw.astype(jnp.bfloat16),
            grad_key_raw.astype(jnp.bfloat16),
            grad_vt.reshape(tok_count, model_width),
        ],
        axis=0,
    )
    qkv_term = jnp.einsum("td,jte->dje", normed_low, grad_stack, preferred_element_type=jnp.float32)
    grad_normed = jnp.einsum(
        "jte,dje->td", grad_stack, attn_full[:, :3], preferred_element_type=jnp.float32
    )
    grad_resid, gain_attn = norm_back(resid_in, factor_attn, gain_rows[0], grad_normed)
    input_grad = (grad_resid + grad_middle).reshape(num_seqs, local_len, model_width)
    attn_term = jnp.concatenate([qkv_term, out_proj_term[:, None, :]], axis=1)
    gain_term = jnp.stack([gain_attn, gain_query, gain_key, gain_ffn], axis=0)
    attn_grad, router_grad, gain_grad = (
        lax.psum_scatter(attn_term, ("dp", "seq"), scatter_dimension=0, tiled=True),
        lax.psum_scatter(router_term, ("dp", "seq"), scatter_dimension=0, tiled=True),
        lax.psum_scatter(gain_term, ("dp", "seq"), scatter_dimension=1, tiled=True),
    )
    return (
        block_out,
        input_grad,
        attn_grad,
        router_grad,
        gain_grad,
        expert_in_grad,
        expert_out_grad,
    )


def solution(mesh):
    in_specs = (
        P("dp", "seq", None),
        P("dp", None),
        P("dp", "seq", None),
        P("dp", "seq", None),
        P(("dp", "seq"), None, None),
        P(("dp", "seq"), None),
        P(None, ("dp", "seq")),
        P("seq", "dp", None, None),
        P("seq", None, "dp"),
    )
    out_specs = (
        P("dp", "seq", None),
        P("dp", "seq", None),
        P(("dp", "seq"), None, None),
        P(("dp", "seq"), None),
        P(None, ("dp", "seq")),
        P("seq", "dp", None, None),
        P("seq", None, "dp"),
    )
    return jax.shard_map(local, mesh=mesh, in_specs=in_specs, out_specs=out_specs, check_vma=False)
```

profile of v0, /device:TPU:0, one launch (start us, length us, event | category | flops | bytes accessed | tf_op | source)
XLA Modules:
  0.0 3736.2 jit_solution(16411563482958224428)
XLA Ops:
  10.1 9.5 copy.277
  20.2 71.0 %all-gather = bf16[32,64,4]{1,2,0:T(4,128)(2,1)S(1)} all-gather(bf16[1,64,4]{1,2,0:T(4,128)(2,1)S(1)} %bitcast.427), channel_id=1, replica_groups=mesh['dp'=4,'seq'=8] {'dp','seq'}, dimensions={0}, use_global_device_ids=true | all-gather | bytes 16896 | tf_op jit(solution)/shard_map/all_gather | solution.py:121
  94.2 115.0 %all-gather.6.cloned.1.call-done = bf16[2048,4,2048]{2,0,1:T(8,128)(2,1)} async-done(((bf16[64,4,2048]{2,0,1:T(8,128)(2,1)}), bf16[2048,4,2048]{2,0,1:T(8,128)(2,1)}) %all-gather.6.cloned.1.call-update) | async-done | bytes 33554448 | tf_op jit(solution)/shard_map/all_gather | solution.py:119
  209.1 13.2 fusion.80
  231.0 4.4 all-to-all-start.2
  237.8 24.1 all-to-all-done.2
  269.3 22.2 all-to-all-done.1
  304.6 16.5 all-to-all-done
  325.5 16.5 while.26
  338.3 3.7 fusion.158
  342.0 3.9 copy.316
  345.9 4.5 all-to-all-start.3
  356.8 19.2 all-to-all-done.3
  378.4 6.3 multiply_reduce_fusion.6
  386.3 9.8 gather_fusion
  396.0 4.9 select_select_fusion
  401.0 209.4 %all_to_all.174 = bf16[32,72,2048]{2,1,0:T(8,128)(2,1)} all-to-all(bf16[32,72,2048]{2,1,0:T(8,128)(2,1)S(1)} %select_select_fusion), channel_id=1, replica_groups=mesh['dp'=4,'seq'=8] {'seq'}, dimensions={0} | all-to-all | bytes 18874368 | tf_op jit(solution)/shard_map/all_to_all | solution.py:210
  610.4 9.4 copy.276
  619.8 28.5 fusion.118
  648.3 10.3 multiply_convert_fusion.3
  658.6 18.8 convolution_convert_fusion.2
  677.3 13.4 copy.279
  690.7 5.2 all-to-all-start.5
  695.9 261.2 %all-gather.1 = bf16[32,64,32]{1,2,0:T(8,128)(2,1)S(1)} all-gather(bf16[1,64,32]{1,2,0:T(8,128)(2,1)S(1)} %bitcast.425), channel_id=1, replica_groups=mesh['dp'=4,'seq'=8] {'dp','seq'}, dimensions={0}, use_global_device_ids=true | all-gather | bytes 135168 | tf_op jit(solution)/shard_map/all_gather | solution.py:120
  959.5 11.7 gather_fusion.1
  971.7 12.8 copy.280
  984.5 21.3 gather_fusion.2
  1005.8 9.2 fusion.72
  1017.9 7.4 multiply_convert_fusion.1
  1025.3 206.5 %all_to_all.175 = bf16[32,72,2048]{2,1,0:T(8,128)(2,1)} all-to-all(bf16[32,72,2048]{2,1,0:T(8,128)(2,1)S(1)} %multiply_convert_fusion.1), channel_id=1, replica_groups=mesh['dp'=4,'seq'=8] {'seq'}, dimensions={0} | all-to-all | bytes 18874368 | tf_op jit(solution)/shard_map/all_to_all | solution.py:237
  1231.8 9.2 copy.283
  1241.0 22.8 fusion.79
  1263.8 27.2 bitcast_convert_fusion
  1291.0 13.4 copy.285
  1304.4 5.4 all-to-all-start.7
  1310.1 203.6 %all-to-all-done.7 = bf16[4,576,2048]{2,0,1:T(4,128)(2,1)} async-done(((bf16[4,576,2048]{2,0,1:T(4,128)(2,1)}), bf16[4,576,2048]{2,0,1:T(4,128)(2,1)}, u32[]{:S(2)}, u32[]{:S(2)}) %all-to-all-start.7) | async-done | bytes 9437216 | tf_op jit(solution)/shard_map/all_to_all | solution.py:250
  1513.7 12.9 copy.286
  1526.6 21.2 gather_fusion.3
  1547.8 20.5 fusion.66
  1571.9 6.5 fusion.87
  1579.3 29.5 all_to_all.176
  1616.3 28.3 while.27
  1644.6 3.8 copy.317
  1654.1 23.6 all-to-all-done.9
  1688.4 19.8 all-to-all-done.10
  1708.3 4.2 all-to-all-start.11
  1719.2 4.2 copy.297
  1726.0 5.4 multiply_subtract_fusion.1
  1733.4 4.2 pad_maximum_fusion.3
  1740.3 4.3 fusion.91
  1748.1 4.6 multiply_reduce_fusion.4
  1752.7 14.4 fusion.98
  1768.6 21.3 convolution_convert_fusion.1
  1790.0 34.9 convolution_convert_fusion
  1826.4 9.8 convolution_bitcast_fusion
  1836.2 21.6 fusion.100
  1857.8 44.3 %pad_maximum_fusion = f32[2048,4,2048]{2,0,1:T(8,128)} fusion(f32[2048,1,2048]{2,0,1:T(8,128)} %convolution_bitcast_fusion, f32[2048,3,2048]{2,0,1:T(8,128)} %fusion.100), kind=kLoop, calls=%fused_computation.70 | loop fusion | flops 16777216 | bytes 134217728 | tf_op jit(solution)/shard_map/concatenate | solution.py:325
  1907.2 50.0 %reduce-scatter.18.cloned.1.call-done = f32[64,4]{1,0:T(8,128)} async-done(((f32[2048,4]{1,0:T(8,128)}), f32[64,4]{1,0:T(8,128)}) %reduce-scatter.18.cloned.1.call-update) | async-done | bytes 1040
  1958.6 123.5 %reduce-scatter.14.cloned.1.call-done = bf16[4,1024,512]{2,1,0:T(8,128)(2,1)} async-done(((bf16[4,1024,2048]{2,1,0:T(8,128)(2,1)}), bf16[4,1024,512]{2,1,0:T(8,128)(2,1)}) %reduce-scatter.14.cloned.1.call-update) | async-done | bytes 4194320 | tf_op jit(solution)/shard_map/reduce_scatter | solution.py:259
  2082.1 6.8 convert_element_type.209
  2088.9 230.9 %reduce-scatter.12.cloned.1.call-done = bf16[4,512,2,1024]{3,1,2,0:T(8,128)(2,1)} async-done(((bf16[4,2048,2,1024]{3,1,2,0:T(8,128)(2,1)}), bf16[4,512,2,1024]{3,1,2,0:T(8,128)(2,1)}) %reduce-scatter.12.cloned.1.call-update) | async-done | bytes 8388624 | tf_op jit(solution)/shard_map/reduce_scatter | solution.py:256
  2319.8 17.7 copy.304
  2337.4 1387.4 %reduce-scatter.10.cloned.1.call-done = f32[64,4,2048]{2,0,1:T(8,128)} async-done(((f32[2048,4,2048]{2,0,1:T(8,128)}), f32[64,4,2048]{2,0,1:T(8,128)}) %reduce-scatter.10.cloned.1.call-update) | async-done | bytes 2097168 | tf_op jit(solution)/shard_map/reduce_scatter | solution.py:328
  3724.8 4.3 copy.303
  (302 shorter events, 154.3 us)
Async XLA Ops:
  7.2 202.0 %all-gather.6.cloned.1.call-start = ((), (), s32[]{:S(2)}) async-start(), calls=%async_computation.17 | async-start | bytes 34603008 | tf_op jit(solution)/shard_map/all_gather | solution.py:119
  10.0 609.8 %all-gather.8.cloned.1.call-start = ((), (), s32[]{:S(2)}) async-start(), calls=%async_computation.18 | async-start | bytes 41943040 | tf_op jit(solution)/shard_map/all_gather | solution.py:124
  19.5 71.9 %copy-start.14 = (bf16[2,128,2048]{2,1,0:T(8,128)(2,1)S(1)}, bf16[2,128,2048]{2,1,0:T(8,128)(2,1)}, u32[]{:S(2)}) copy-start(bf16[2,128,2048]{2,1,0:T(8,128)(2,1)} %param.15) | copy-start | bytes 3145732
  92.6 134.7 %copy-start.33 = (f32[128,64]{1,0:T(8,128)}, f32[128,64]{1,0:T(8,128)S(1)}, u32[]{:S(2)}) copy-start(f32[128,64]{1,0:T(8,128)S(1)} %get-tuple-element.323) | copy-start | bytes 98308
  93.3 133.3 %copy-start.41 = (f32[1,2048]{1,0:T(1,128)}, f32[1,2048]{1,0:T(1,128)S(1)}, u32[]{:S(2)}) copy-start(f32[1,2048]{1,0:T(1,128)S(1)} %get-tuple-element.315) | copy-start | bytes 24580
  93.3 133.7 %copy-start.39 = (f32[1,2048]{1,0:T(1,128)}, f32[1,2048]{1,0:T(1,128)S(1)}, u32[]{:S(2)}) copy-start(f32[1,2048]{1,0:T(1,128)S(1)} %get-tuple-element.314) | copy-start | bytes 24580
  94.2 128.2 %copy-start.18 = (bf16[256,2048]{1,0:T(8,128)(2,1)}, bf16[256,2048]{1,0:T(8,128)(2,1)S(1)}, u32[]{:S(2)}) copy-start(bf16[256,2048]{1,0:T(8,128)(2,1)S(1)} %multiply_convert_fusion.7) | copy-start | bytes 3145732
  231.0 30.9 all-to-all-start.2
  261.9 29.6 all-to-all-start.1
  267.3 28.6 copy-start.38
  291.5 29.6 all-to-all-start
  295.2 363.4 %all-gather.10.cloned.1.call-start = ((), (), s32[]{:S(2)}) async-start(), calls=%async_computation.19 | async-start | bytes 20971520 | tf_op jit(solution)/shard_map/all_gather | solution.py:125
  303.0 22.5 copy-start.36
  342.0 9.2 copy-start.45
  342.0 36.3 copy-start.3
  342.0 36.4 copy-start.5
  342.0 36.4 copy-start.11
  345.9 30.1 all-to-all-start.3
  351.3 33.4 copy-start.29
  356.8 39.3 %copy-start.50 = (pred[32,72]{1,0:T(8,128)(4,1)}, pred[32,72]{1,0:T(8,128)(4,1)S(1)}, u32[]{:S(2)}) copy-start(pred[32,72]{1,0:T(8,128)(4,1)S(1)} %compare_and_fusion) | copy-start | bytes 6916
  378.4 6.3 copy-start.22
  378.4 7.6 copy-start.43
  384.7 11.3 copy-start.54
  386.3 584.9 %copy-start = (bf16[256,2048]{1,0:T(8,128)(2,1)}, bf16[256,2048]{1,0:T(8,128)(2,1)S(1)}, u32[]{:S(2)}) copy-start(bf16[256,2048]{1,0:T(8,128)(2,1)S(1)} %multiply_convert_fusion.6) | copy-start | bytes 3145732
  690.7 5.2 copy-start.59
  690.7 281.0 %all-to-all-start.5 = ((bf16[4,576,2048]{2,0,1:T(4,128)(2,1)}), bf16[4,576,2048]{2,0,1:T(4,128)(2,1)}, u32[]{:S(2)}, u32[]{:S(2)}) async-start(bf16[4,576,2048]{2,0,1:T(4,128)(2,1)} %copy.279), calls=%async_computation.5 | async-start | bytes 18874368 | tf_op jit(solution)/shard_map/all_to_all | solution.py:223
  957.5 13.7 copy-start.31
  984.5 21.3 copy-start.21
  1005.8 9.3 copy-start.53
  1005.8 9.5 copy-start.30
  1005.8 12.1 copy-start.51
  1304.4 209.3 %all-to-all-start.7 = ((bf16[4,576,2048]{2,0,1:T(4,128)(2,1)}), bf16[4,576,2048]{2,0,1:T(4,128)(2,1)}, u32[]{:S(2)}, u32[]{:S(2)}) async-start(bf16[4,576,2048]{2,0,1:T(4,128)(2,1)} %copy.285), calls=%async_computation.7 | async-start | bytes 18874368 | tf_op jit(solution)/shard_map/all_to_all | solution.py:250
  1547.8 20.5 copy-start.10
  1547.8 20.5 copy-start.32
  1547.8 20.5 copy-start.44
  1547.8 20.5 copy-start.55
  1571.9 6.5 copy-start.7
  1608.8 7.5 copy-start.4
  1608.8 7.5 copy-start.6
  1608.8 7.5 copy-start.12
  1608.8 7.5 copy-start.37
  1608.8 7.5 copy-start.46
  1644.6 7.4 copy-start.28
  1644.6 36.6 copy-start.1
  1648.4 29.2 all-to-all-start.9
  1677.6 8.8 copy-start.23
  1677.6 30.6 all-to-all-start.10
  1681.2 220.9 %reduce-scatter.16.cloned.1.call-start = ((), (), s32[]{:S(2)}) async-start(), calls=%async_computation.23 | async-start | bytes 1081344
  1708.3 36.4 all-to-all-start.11
  1712.5 244.7 %reduce-scatter.18.cloned.1.call-start = ((), (), s32[]{:S(2)}) async-start(), calls=%async_computation.24 | async-start | bytes 1081344
  1719.2 6.8 copy-start.34
  1719.2 6.8 copy-start.35
  1733.4 6.9 copy-start.40
  1733.4 6.9 copy-start.42
  1744.6 3.5 copy-start.20
  1744.6 3.5 copy-start.60
  1748.0 4.7 copy-start.16
  1748.0 4.6 copy-start.48
  1748.1 4.6 copy-start.57
  1752.7 14.4 copy-start.52
  1768.6 313.6 %reduce-scatter.14.cloned.1.call-start = ((), (), s32[]{:S(2)}) async-start(), calls=%async_computation.22 | async-start | bytes 20971520 | tf_op jit(solution)/shard_map/reduce_scatter | solution.py:259
  1789.9 529.9 %reduce-scatter.12.cloned.1.call-start = ((), (), s32[]{:S(2)}) async-start(), calls=%async_computation.21 | async-start | bytes 41943040 | tf_op jit(solution)/shard_map/reduce_scatter | solution.py:256
  1824.8 11.3 copy-start.19
  1824.8 1900.0 %reduce-scatter.10.cloned.1.call-start = ((), (), s32[]{:S(2)}) async-start(), calls=%async_computation.20 | async-start | bytes 69206016 | tf_op jit(solution)/shard_map/reduce_scatter | solution.py:328
  (22 other events, 39.5 us)
Sparse Core Ops, SparseCore 0:
  11.7 197.4 all-gather.5
  211.3 199.6 all-gather.7
  412.6 105.9 all-gather.9
  1684.0 136.8 reduce-scatter.15
  1823.1 134.0 reduce-scatter.17
  1959.7 122.4 reduce-scatter.13
  2084.9 234.8 reduce-scatter.11
  2322.2 1402.5 reduce-scatter.9
where the time goes:
time: 3750 us; the launch traced here: 3740 us
  waiting for transfers between devices  2240 us (60%)
  blocking collectives  778 us (21%)
  matrix products  268 us (7%)
  local copies, waits for them, and re-layouts  248 us (7%)
  other arithmetic  151 us (4%)
  starting transfers between devices  38.6 us (1%)
    reduce_scatter x1, waiting for transfers between devices, local(): lax.psum_scatter(attn_term, ('dp', 'seq'), scatter_dimension=0, tiled=True)  1390 us
    all_gather x1, blocking collectives, local(): lax.all_gather(router_weight, ('dp', 'seq'), axis=0, tiled=True)  261 us
    reduce_scatter x1, waiting for transfers between devices, local(): lax.psum_scatter(in_term.astype(jnp.bfloat16), 'dp', scatter_dimension=1,...  231 us
    all_to_all x1, blocking collectives, local(): lax.all_to_all(sent_rows.reshape(experts_all, capacity, model_width), 'se...  209 us
    all_to_all x1, blocking collectives, local(): lax.all_to_all(slot_grad.reshape(experts_all, capacity, model_width), 'se...  207 us
    all_to_all x1, waiting for transfers between devices, local(): lax.all_to_all(grad_rows, 'seq', split_axis=1, concat_axis=0, tiled=True)  204 us
    reduce_scatter x1, waiting for transfers between devices, local(): lax.psum_scatter(out_term.astype(jnp.bfloat16), 'dp', scatter_dimension=2...  123 us
    all_gather x1, waiting for transfers between devices, local(): lax.all_gather(attn_weight, ('dp', 'seq'), axis=0, tiled=True)  115 us
  transfers between devices with their start and end apart: 17, of which 12 were waited for; matrix products, arithmetic and copies ran while one was open for 10% of the time, Pallas kernels for 0%

commit v1 on v0

v1 whole, which is shorter than its diff:
```python
import math

import jax
import jax.numpy as jnp
from jax import lax
from jax.experimental import pallas as pl
from jax.experimental.pallas import tpu as pltpu
from jax.sharding import PartitionSpec as P

HEADS = 16
HEAD_DIM = 128
NORM_EPS = 1e-05
ROPE_BASE = 10000.0
MASKED_SCORE = -1e30
BF = jnp.bfloat16
F32 = jnp.float32
MESH = pl.DeviceIdType.MESH
VMEM_MOST = 60 << 20


def grid_of(seq_size):
    lines = 4 if seq_size % 4 == 0 else 1
    return lines, seq_size // lines


def greet(targets):
    barrier = pltpu.get_barrier_semaphore()
    count = 0
    for cond, device in targets:

        @pl.when(cond)
        def _(device=device):
            pl.semaphore_signal(barrier, 1, device_id=device, device_id_type=MESH)

        count = count + cond.astype(jnp.int32)
    pl.semaphore_wait(barrier, count)


def neighbours(dp, z, y, nz, ny):
    return {
        ("z", 1): (z < nz - 1, (dp, (z + 1) * ny + y)),
        ("z", -1): (z > 0, (dp, (z - 1) * ny + y)),
        ("y", 1): (y < ny - 1, (dp, z * ny + y + 1)),
        ("y", -1): (y > 0, (dp, z * ny + y - 1)),
    }


def seq_gather(block, collective_id, pieces=2):
    rows, width = block.shape
    seq = lax.axis_size("seq")
    nz, ny = grid_of(seq)
    part = rows // pieces

    def kernel(x_ref, o_ref, send_sem, recv_sem, local_sem):
        dp, me = lax.axis_index("dp"), lax.axis_index("seq")
        z, y = lax.div(me, ny), lax.rem(me, ny)
        near = neighbours(dp, z, y, nz, ny)
        greet(list(near.values()))
        own = pltpu.make_async_copy(x_ref, o_ref.at[me], local_sem)
        own.start()
        sent = []
        names = list(near)

        def cut(h):
            return pl.ds(h * part, part)

        def copy(src, origin, h, name):
            return pltpu.make_async_remote_copy(
                src_ref=src,
                dst_ref=o_ref.at[origin, cut(h)],
                send_sem=send_sem.at[origin, h, names.index(name)],
                recv_sem=recv_sem.at[origin, h],
                device_id=near[name][1],
                device_id_type=MESH,
            )

        def send(src, origin, h, name, cond):
            ok = jnp.logical_and(cond, near[name][0])
            pl.when(ok)(lambda: copy(src, origin, h, name).start())
            sent.append((ok, src, origin, h, name))

        def arrive(origin, h, cond):
            @pl.when(cond)
            def _():
                copy(o_ref.at[origin, cut(h)], origin, h, names[0]).wait_recv()

        always = z >= 0
        for h in range(pieces):
            for name in names:
                send(x_ref.at[cut(h)], me, h, name, always)
        for far in range(1, nz):
            for h in range(pieces):
                for sign in (1, -1):
                    zz = z - sign * far
                    cond = jnp.logical_and(zz >= 0, zz < nz)
                    origin = lax.select(cond, zz * ny + y, me)
                    arrive(origin, h, cond)
                    for name in (("z", sign), ("y", 1), ("y", -1)):
                        send(o_ref.at[origin, cut(h)], origin, h, name, cond)
        for side in range(1, ny):
            for far in range(nz):
                for h in range(pieces):
                    for sign in (1, -1) if far else (1,):
                        zz = z - sign * far
                        for turn in (1, -1):
                            yy = y - turn * side
                            cond = (zz >= 0) & (zz < nz) & (yy >= 0) & (yy < ny)
                            origin = lax.select(cond, zz * ny + yy, me)
                            arrive(origin, h, cond)
                            if side < ny - 1:
                                send(o_ref.at[origin, cut(h)], origin, h, ("y", turn), cond)
        for ok, src, origin, h, name in sent:
            pl.when(ok)(lambda: copy(src, origin, h, name).wait_send())
        own.wait()

    return pl.pallas_call(
        kernel,
        out_shape=jax.ShapeDtypeStruct((seq, rows, width), block.dtype),
        in_specs=[pl.BlockSpec(memory_space=pl.ANY)],
        out_specs=pl.BlockSpec(memory_space=pl.ANY),
        scratch_shapes=[
            pltpu.SemaphoreType.DMA((seq, pieces, 4)),
            pltpu.SemaphoreType.DMA((seq, pieces)),
            pltpu.SemaphoreType.DMA,
        ],
        compiler_params=pltpu.CompilerParams(collective_id=collective_id, has_side_effects=True),
        name="seq_gather",
    )(block)


def seq_reduce(terms, collective_id, pieces=2):
    seq, rows, width = terms.shape
    nz, ny = grid_of(seq)
    part = rows // pieces
    sides = 1 if ny == 2 else 2
    strip = 16

    def kernel(p_ref, o_ref, acc, from_y, from_z, send_sem, ysem, zsem):
        dp, me = lax.axis_index("dp"), lax.axis_index("seq")
        z, y = lax.div(me, ny), lax.rem(me, ny)
        near = neighbours(dp, z, y, nz, ny)
        names = list(near)
        greet(list(near.values()))
        sent = []

        def cut(h):
            return pl.ds(h * part, part)

        def lane(turn):
            return 0 if sides == 1 else (0 if turn == 1 else 1)

        def copy(src, dest, h, name):
            if name[0] == "y":
                dst, sem = from_y.at[lane(name[1]), dest, cut(h)], ysem.at[lane(name[1]), dest, h]
            else:
                side = 0 if name[1] == 1 else 1
                zz = lax.div(dest, ny)
                dst, sem = from_z.at[side, zz, cut(h)], zsem.at[side, zz, h]
            return pltpu.make_async_remote_copy(
                src_ref=src,
                dst_ref=dst,
                send_sem=send_sem.at[dest, h],
                recv_sem=sem,
                device_id=near[name][1],
                device_id_type=MESH,
            )

        def send(src, dest, h, name, ok):
            pl.when(ok)(lambda: copy(src, dest, h, name).start())
            sent.append((ok, src, dest, h, name))

        def add_up(refs, out, h):
            def body(i, carry):
                at = pl.ds(h * part + i * strip, strip)
                total = refs[0][at, :].astype(F32)
                for ref in refs[1:]:
                    total = total + ref[at, :].astype(F32)
                out[at, :] = total.astype(out.dtype)
                return carry

            lax.fori_loop(0, part // strip, body, 0)

        def order():
            for far in range(nz - 1, -1, -1):
                for sign in (1, -1) if far else (1,):
                    zz = z + sign * far
                    yield far, sign, zz, (zz >= 0) & (zz < nz)

        for side in range(ny - 1, 0, -1):
            for far, sign, zz, ok in order():
                for h in range(pieces):
                    for turn in (1, -1):
                        yy = y + turn * side
                        go = ok & (yy >= 0) & (yy < ny)
                        dest = lax.select(go, zz * ny + yy, me)
                        behind = near[("y", -turn)][0]
                        if ny == 2:
                            send(p_ref.at[dest, cut(h)], dest, h, ("y", turn), go)
                        else:

                            @pl.when(go & behind)
                            def _():
                                copy(p_ref.at[dest, cut(h)], dest, h, ("y", turn)).wait_recv()
                                add_up([p_ref.at[dest], from_y.at[lane(turn), dest]], acc.at[dest], h)

                            @pl.when(go & jnp.logical_not(behind))
                            def _():
                                add_up([p_ref.at[dest]], acc.at[dest], h)

                            send(acc.at[dest, cut(h)], dest, h, ("y", turn), go)
        for far, sign, zz, ok in order():
            dest = lax.select(ok, zz * ny + y, me)
            for h in range(pieces):
                for turn in (1, -1):

                    @pl.when(ok & near[("y", -turn)][0])
                    def _():
                        copy(p_ref.at[dest, cut(h)], dest, h, ("y", turn)).wait_recv()

                if ny == 2:

                    @pl.when(ok)
                    def _():
                        add_up([p_ref.at[dest], from_y.at[0, dest]], acc.at[dest], h)

                else:

                    @pl.when(ok)
                    def _():
                        add_up([p_ref.at[dest]], acc.at[dest], h)

                    for turn in (1, -1):

                        @pl.when(ok & near[("y", -turn)][0])
                        def _():
                            add_up([acc.at[dest], from_y.at[lane(turn), dest]], acc.at[dest], h)

                if far:
                    name = ("z", sign)
                    behind = near[("z", -sign)][0]
                    side = 0 if sign == 1 else 1

                    @pl.when(ok & behind)
                    def _():
                        copy(acc.at[dest, cut(h)], dest, h, name).wait_recv()
                        add_up([acc.at[dest], from_z.at[side, zz]], acc.at[dest], h)

                    send(acc.at[dest, cut(h)], dest, h, name, ok)
                else:
                    below, above = near[("z", -1)][0], near[("z", 1)][0]
                    for sign2, cond in ((1, below), (-1, above)):

                        @pl.when(cond)
                        def _():
                            copy(acc.at[me, cut(h)], me, h, ("z", sign2)).wait_recv()

                    lower, upper = from_z.at[0, z], from_z.at[1, z]

                    @pl.when(below & above)
                    def _():
                        add_up([acc.at[me], lower, upper], o_ref, h)

                    @pl.when(below & jnp.logical_not(above))
                    def _():
                        add_up([acc.at[me], lower], o_ref, h)

                    @pl.when(jnp.logical_not(below) & above)
                    def _():
                        add_up([acc.at[me], upper], o_ref, h)

        for ok, src, dest, h, name in sent:
            pl.when(ok)(lambda: copy(src, dest, h, name).wait_send())

    return pl.pallas_call(
        kernel,
        out_shape=jax.ShapeDtypeStruct((rows, width), F32),
        in_specs=[pl.BlockSpec(memory_space=pltpu.VMEM)],
        out_specs=pl.BlockSpec(memory_space=pltpu.VMEM),
        scratch_shapes=[
            pltpu.VMEM((seq, rows, width), BF),
            pltpu.VMEM((sides, seq, rows, width), BF),
            pltpu.VMEM((2, nz, rows, width), BF),
            pltpu.SemaphoreType.DMA((seq, pieces)),
            pltpu.SemaphoreType.DMA((sides, seq, pieces)),
            pltpu.SemaphoreType.DMA((2, nz, pieces)),
        ],
        compiler_params=pltpu.CompilerParams(
            collective_id=collective_id, has_side_effects=True, vmem_limit_bytes=VMEM_MOST
        ),
        name="seq_reduce",
    )(terms)


def small_exchange(arrays, axes, collective_id):
    sizes = [lax.axis_size(axis) for axis in axes]
    peers = math.prod(sizes)
    seq = lax.axis_size("seq")
    count = len(arrays)

    def kernel(*refs):
        ins, outs, (send_sem, recv_sem) = refs[:count], refs[count : 2 * count], refs[2 * count :]
        dp, sq = lax.axis_index("dp"), lax.axis_index("seq")
        me = sq if len(axes) == 1 else dp * seq + sq

        def device(peer):
            return (dp, peer) if len(axes) == 1 else (lax.div(peer, seq), lax.rem(peer, seq))

        barrier = pltpu.get_barrier_semaphore()
        for step in range(1, peers):
            pl.semaphore_signal(
                barrier, 1, device_id=device(lax.rem(me + step, peers)), device_id_type=MESH
            )
        pl.semaphore_wait(barrier, peers - 1)

        def copy(i, peer, src_slot):
            src = ins[i].at[0] if arrays[i].shape[0] == 1 else ins[i].at[peer]
            return pltpu.make_async_remote_copy(
                src_ref=src,
                dst_ref=outs[i].at[src_slot],
                send_sem=send_sem.at[i, peer],
                recv_sem=recv_sem.at[i, src_slot],
                device_id=device(peer),
                device_id_type=MESH,
            )

        for step in range(1, peers):
            for i in range(count):
                copy(i, lax.rem(me + step, peers), me).start()
        for i in range(count):
            outs[i][me] = ins[i][0] if arrays[i].shape[0] == 1 else ins[i][me]
        for step in range(1, peers):
            for i in range(count):
                copy(i, lax.rem(me + step, peers), me).wait_send()
                source = lax.rem(me + peers - step, peers)
                copy(i, source, source).wait_recv()

    return pl.pallas_call(
        kernel,
        out_shape=[jax.ShapeDtypeStruct((peers,) + a.shape[1:], a.dtype) for a in arrays],
        in_specs=[pl.BlockSpec(memory_space=pltpu.VMEM)] * count,
        out_specs=[pl.BlockSpec(memory_space=pltpu.VMEM)] * count,
        scratch_shapes=[
            pltpu.SemaphoreType.DMA((count, peers)),
            pltpu.SemaphoreType.DMA((count, peers)),
        ],
        compiler_params=pltpu.CompilerParams(collective_id=collective_id, has_side_effects=True),
        name="small_exchange",
    )(*arrays)


def packed_rows(parts, sublanes):
    flat = jnp.concatenate(parts, axis=1)
    fill = -flat.shape[1] % (sublanes * 128)
    return jnp.pad(flat, ((0, 0), (0, fill))).reshape(flat.shape[0], -1, 128)


def rms_factor(values):
    return lax.rsqrt(jnp.mean(values * values, axis=-1, keepdims=True) + NORM_EPS)


def norm_back(values, factor, gain_row, incoming):
    scaled = incoming * gain_row
    gain_part = jnp.sum(incoming * values * factor, axis=0)
    inner = jnp.mean(scaled * values, axis=-1, keepdims=True)
    return (factor * (scaled - values * factor * factor * inner), gain_part)


def rotary(positions):
    half_dim = HEAD_DIM // 2
    freqs = jnp.exp(
        -math.log(ROPE_BASE) * (2.0 * jnp.arange(half_dim, dtype=F32) / HEAD_DIM)
    )
    angles = positions.astype(F32)[:, None] * freqs[None, :]
    return (jnp.cos(angles)[:, None, :], jnp.sin(angles)[:, None, :])


def rotate(values, cosine, sine):
    half_dim = values.shape[-1] // 2
    first = values[..., :half_dim]
    second = values[..., half_dim:]
    return jnp.concatenate(
        [first * cosine - second * sine, second * cosine + first * sine], axis=-1
    )


def attend_forward(pieces):
    queries, key_rows, value_rows, seg_ids = pieces
    score_scale = HEAD_DIM ** (-0.5)
    scores = jnp.einsum("qhd,khd->hqk", queries, key_rows, preferred_element_type=F32) * score_scale
    allowed = seg_ids[None, :] <= seg_ids[:, None]
    scores = jnp.where(allowed[None], scores, MASKED_SCORE)
    row_max = jnp.max(scores, axis=-1, keepdims=True)
    exp_scores = jnp.exp(scores - row_max)
    row_sum = jnp.sum(exp_scores, axis=-1, keepdims=True)
    attn_probs = exp_scores / row_sum
    attended = jnp.einsum(
        "hqk,khd->qhd", attn_probs.astype(BF), value_rows, preferred_element_type=F32
    )
    return (attended.astype(BF), (row_max + jnp.log(row_sum))[..., 0])


def attend_backward(pieces):
    queries, key_rows, value_rows, grad_out, log_norm, seg_ids = pieces
    score_scale = HEAD_DIM ** (-0.5)
    scores = jnp.einsum("qhd,khd->hqk", queries, key_rows, preferred_element_type=F32) * score_scale
    allowed = seg_ids[None, :] <= seg_ids[:, None]
    attn_probs = jnp.where(allowed[None], jnp.exp(scores - log_norm[..., None]), 0.0)
    grad_probs = jnp.einsum("qhd,khd->hqk", grad_out, value_rows, preferred_element_type=F32)
    inner = jnp.sum(attn_probs * grad_probs, axis=-1, keepdims=True)
    grad_scores = (attn_probs * (grad_probs - inner)).astype(BF)
    grad_query = (
        jnp.einsum("hqk,khd->qhd", grad_scores, key_rows, preferred_element_type=F32) * score_scale
    )
    grad_key = (
        jnp.einsum("hqk,qhd->khd", grad_scores, queries, preferred_element_type=F32) * score_scale
    )
    grad_value = jnp.einsum(
        "hqk,qhd->khd", attn_probs.astype(BF), grad_out, preferred_element_type=F32
    )
    return (grad_query.astype(BF), grad_key.astype(BF), grad_value.astype(BF))


def swiglu(gate_vals, up_vals):
    return jax.nn.silu(gate_vals) * up_vals


def local(
    tokens,
    segments,
    routes,
    cotangent,
    attn_weight,
    router_weight,
    norm_gains,
    expert_in,
    expert_out,
):
    num_seqs, local_len, width = tokens.shape
    seq_length = segments.shape[1]
    seq, ndp = lax.axis_size("seq"), lax.axis_size("dp")
    me = lax.axis_index("seq")
    devices = seq * ndp
    heads_here = HEADS // seq
    cols = heads_here * HEAD_DIM
    tok = num_seqs * local_len
    group = tok * seq
    own_rows = attn_weight.shape[0]
    experts_all = router_weight.shape[1]
    experts = experts_all // seq
    top = routes.shape[-1]
    capacity = (9 * tok * top + 8 * experts_all - 1) // (8 * experts_all)

    in_full = lax.all_gather(expert_in, "dp", axis=1, tiled=True)
    out_full = lax.all_gather(expert_out, "dp", axis=2, tiled=True)

    n_router, n_gain = own_rows * experts_all, 4 * own_rows
    (small_all,) = small_exchange(
        [packed_rows([router_weight.reshape(1, -1), norm_gains.reshape(1, -1)], 16)], ("dp", "seq"), 1
    )
    small_all = small_all.reshape(devices, -1)
    router_full = small_all[:, :n_router].reshape(width, experts_all)
    gain_rows = (
        small_all[:, n_router : n_router + n_gain]
        .reshape(devices, 4, own_rows)
        .transpose(1, 0, 2)
        .reshape(4, width)
        .astype(F32)
    )
    (routes_all,) = small_exchange([routes.reshape(1, -1, 128)], ("seq",), 2)
    routes_all = routes_all.reshape(seq, tok, top)

    qkv_send = (
        attn_weight[:, :3].reshape(own_rows, 3, seq, cols).transpose(2, 1, 0, 3)
    )
    qkv_got = lax.all_to_all(qkv_send, "seq", split_axis=0, concat_axis=0, tiled=True)
    qkv_full = lax.all_gather(qkv_got, "dp", axis=0, tiled=True)
    qkv_weight = qkv_full.transpose(1, 0, 2, 3).reshape(3, width, cols)
    spread = seq // ndp
    out_rows = lax.all_gather(attn_weight[:, 3], "dp", axis=0, tiled=False)
    out_send = jnp.repeat(out_rows, spread, axis=0)
    out_got = lax.all_to_all(out_send, "seq", split_axis=0, concat_axis=0, tiled=True)
    proj_weight = lax.dynamic_slice_in_dim(
        out_got, lax.rem(me, spread) * ndp, ndp, axis=0
    ).reshape(cols, width)

    resid_in = tokens.astype(F32).reshape(tok, width)
    factor_attn = rms_factor(resid_in)
    normed_low = (resid_in * factor_attn * gain_rows[0]).astype(BF)
    normed_all = seq_gather(normed_low, 3).reshape(group, width)
    raw = jnp.einsum("td,jde->jte", normed_all, qkv_weight, preferred_element_type=F32)
    squares = jnp.sum(raw[:2] * raw[:2], axis=-1).reshape(1, -1, 128)
    (sums,) = small_exchange([squares], ("seq",), 4)
    factors = lax.rsqrt(jnp.sum(sums, axis=0).reshape(2, group, 1) / width + NORM_EPS)
    head_gains = lax.dynamic_slice_in_dim(gain_rows, me * cols, cols, axis=1)

    position = (
        jnp.arange(seq, dtype=jnp.int32)[:, None, None] * local_len
        + jnp.zeros((1, num_seqs, 1), jnp.int32)
        + jnp.arange(local_len, dtype=jnp.int32)[None, None, :]
    ).reshape(group)
    cosine, sine = rotary(position)

    def to_heads(values):
        return values.reshape(group, heads_here, HEAD_DIM)

    def by_sequence(values):
        return (
            values.reshape(seq, num_seqs, local_len, heads_here, HEAD_DIM)
            .transpose(1, 0, 2, 3, 4)
            .reshape(num_seqs, seq_length, heads_here, HEAD_DIM)
        )

    def by_source(values):
        return (
            values.reshape(num_seqs, seq, local_len, cols).transpose(1, 0, 2, 3).reshape(group, cols)
        )

    qn = raw[0] * factors[0] * head_gains[1]
    kn = raw[1] * factors[1] * head_gains[2]
    query_head = by_sequence(rotate(to_heads(qn), cosine, sine).astype(BF))
    key_head = by_sequence(rotate(to_heads(kn), cosine, sine).astype(BF))
    value_head = by_sequence(raw[2].astype(BF))
    attended, log_norm = lax.map(attend_forward, (query_head, key_head, value_head, segments))
    o_head = by_source(attended.reshape(num_seqs, seq_length, cols))
    z_terms = jnp.dot(o_head, proj_weight, preferred_element_type=F32).astype(BF)
    z = seq_reduce(z_terms.reshape(seq, tok, width), 5)

    middle = resid_in + z
    factor_ffn = rms_factor(middle)
    ffn_low = (middle * factor_ffn * gain_rows[3]).astype(BF)
    ffn_all = seq_gather(ffn_low, 6)
    cot_low = cotangent.reshape(tok, width)
    cot_all = seq_gather(cot_low, 7)

    logits_all = jnp.einsum("std,de->ste", ffn_all, router_full, preferred_element_type=F32)
    probs_all = jax.nn.softmax(logits_all, axis=-1)
    here = me * experts + jnp.arange(experts, dtype=jnp.int32)
    hits = jnp.any(routes_all[:, :, :, None] == here, axis=2)
    token_ids = jnp.arange(tok, dtype=jnp.int32)
    earlier = (token_ids[:, None] > token_ids[None, :]).astype(BF)
    slot = jnp.einsum("tu,sue->ste", earlier, hits.astype(BF), preferred_element_type=F32)
    slot = jnp.where(hits, slot, float(tok + 1)).astype(jnp.int32)
    place = slot.transpose(2, 0, 1)[:, :, None, :] == jnp.arange(capacity, dtype=jnp.int32)[
        None, None, :, None
    ]
    place_low = place.astype(BF)
    probs_here = lax.dynamic_slice_in_dim(probs_all, me * experts, experts, axis=2).transpose(2, 0, 1)
    place_gate = jnp.where(place, probs_here[:, :, None, :], 0.0)
    slot_gate = jnp.sum(place_gate, axis=-1)
    slots = seq * capacity
    rows = (
        jnp.einsum("esjt,std->esjd", place_low, ffn_all, preferred_element_type=F32)
        .astype(BF)
        .reshape(experts, slots, width)
    )
    cot_rows = jnp.einsum("esjt,std->esjd", place_low, cot_all, preferred_element_type=F32).reshape(
        experts, slots, width
    )

    gate_up = jnp.einsum("erd,edjf->erjf", rows, in_full, preferred_element_type=F32)
    hidden_f, swiglu_pull = jax.vjp(swiglu, gate_up[:, :, 0], gate_up[:, :, 1])
    hidden = hidden_f.astype(BF)
    expert_res = jnp.einsum("erf,efd->erd", hidden, out_full, preferred_element_type=F32).astype(BF)
    mixed_terms = jnp.einsum(
        "esjt,esjd->std",
        place_gate.astype(BF),
        expert_res.reshape(experts, seq, capacity, width),
        preferred_element_type=F32,
    ).astype(BF)
    mixed = seq_reduce(mixed_terms, 8)
    block_out = (middle + mixed).astype(BF).reshape(num_seqs, local_len, width)

    slot_dgate = jnp.sum(cot_rows * expert_res.astype(F32), axis=-1).reshape(experts, seq, capacity)
    grad_prob_here = jnp.sum(jnp.where(place, slot_dgate[..., None], 0.0), axis=2)
    grad_res = (cot_rows * slot_gate.reshape(experts, slots, 1)).astype(BF)
    grad_hidden = jnp.einsum("erd,efd->erf", grad_res, out_full, preferred_element_type=F32)
    grad_gatev, grad_upv = swiglu_pull(grad_hidden)
    grad_gu = jnp.stack([grad_gatev, grad_upv], axis=2).astype(BF)
    grad_rows = jnp.einsum("erjf,edjf->erd", grad_gu, in_full, preferred_element_type=F32).astype(BF)
    out_term = jnp.einsum("erf,erd->efd", hidden, grad_res, preferred_element_type=F32).astype(BF)
    in_term = jnp.einsum("erd,erjf->edjf", rows, grad_gu, preferred_element_type=F32).astype(BF)
    expert_out_grad = lax.psum_scatter(out_term, "dp", scatter_dimension=2, tiled=True).astype(F32)
    expert_in_grad = lax.psum_scatter(in_term, "dp", scatter_dimension=1, tiled=True).astype(F32)
    dffn_terms = jnp.einsum(
        "esjt,esjd->std",
        place_low,
        grad_rows.reshape(experts, seq, capacity, width),
        preferred_element_type=F32,
    ).astype(BF)
    grad_ffn = seq_reduce(dffn_terms, 9)
    (grad_prob,) = small_exchange(
        [grad_prob_here.transpose(1, 0, 2).reshape(seq, -1, 128)], ("seq",), 10
    )
    grad_prob = grad_prob.reshape(experts_all, tok).T

    route_probs = jax.nn.softmax(
        jnp.dot(ffn_low, router_full, preferred_element_type=F32), axis=-1
    )
    grad_logits = (
        route_probs * (grad_prob - jnp.sum(route_probs * grad_prob, axis=-1, keepdims=True))
    ).astype(BF)
    router_term = jnp.einsum("td,te->de", ffn_low, grad_logits, preferred_element_type=F32)
    grad_ffn = grad_ffn + jnp.einsum(
        "te,de->td", grad_logits, router_full, preferred_element_type=F32
    )
    grad_middle, gain_ffn = norm_back(middle, factor_ffn, gain_rows[3], grad_ffn)
    grad_middle = grad_middle + cot_low.astype(F32)

    dz_all = seq_gather(grad_middle.astype(BF), 11).reshape(group, width)
    grad_o = jnp.einsum("te,de->td", dz_all, proj_weight, preferred_element_type=F32).astype(BF)
    proj_term = jnp.einsum("td,te->de", o_head, dz_all, preferred_element_type=F32).astype(BF)
    grad_q, grad_k, grad_v = lax.map(
        attend_backward,
        (query_head, key_head, value_head, by_sequence(grad_o), log_norm, segments),
    )
    flat = (num_seqs, seq_length, cols)
    grad_qn = rotate(to_heads(by_source(grad_q.reshape(flat)).astype(F32)), cosine, -sine).reshape(
        group, cols
    )
    grad_kn = rotate(to_heads(by_source(grad_k.reshape(flat)).astype(F32)), cosine, -sine).reshape(
        group, cols
    )
    grad_n = jnp.stack([grad_qn, grad_kn])
    scaled = grad_n * head_gains[1:3, None, :]
    inner = jnp.sum(scaled * raw[:2], axis=-1).reshape(1, -1, 128)
    (inners,) = small_exchange([inner], ("seq",), 12)
    inner = jnp.sum(inners, axis=0).reshape(2, group, 1) / width
    gain_heads = jnp.sum(grad_n * raw[:2] * factors, axis=1)
    grad_raw = factors * (scaled - raw[:2] * factors * factors * inner)
    grad_stack = jnp.concatenate(
        [grad_raw.astype(BF), by_source(grad_v.reshape(flat))[None]], axis=0
    )
    dn_terms = jnp.einsum("jte,jde->td", grad_stack, qkv_weight, preferred_element_type=F32).astype(BF)
    grad_normed = seq_reduce(dn_terms.reshape(seq, tok, width), 13)
    qkv_term = jnp.einsum("td,jte->jde", normed_all, grad_stack, preferred_element_type=F32).astype(BF)
    grad_resid, gain_attn = norm_back(resid_in, factor_attn, gain_rows[0], grad_normed)
    input_grad = (grad_resid + grad_middle).reshape(num_seqs, local_len, width)

    qkv_part = lax.psum_scatter(qkv_term, "dp", scatter_dimension=1, tiled=True)
    qkv_out = lax.all_to_all(
        qkv_part.reshape(3, seq, own_rows, cols).transpose(1, 0, 2, 3),
        "seq",
        split_axis=0,
        concat_axis=0,
        tiled=True,
    )
    qkv_grad = qkv_out.transpose(2, 1, 0, 3).reshape(own_rows, 3, width)
    proj_part = lax.psum_scatter(proj_term, "dp", scatter_dimension=0, tiled=True)
    proj_grad = lax.ppermute(
        proj_part,
        ("dp", "seq"),
        [(i * seq + s, s * ndp + i) for i in range(ndp) for s in range(seq)],
    )
    attn_grad = jnp.concatenate([qkv_grad, proj_grad[:, None, :]], axis=1).astype(F32)
    zero_heads = jnp.zeros((2, width), F32)
    gain_heads = lax.dynamic_update_slice_in_dim(zero_heads, gain_heads, me * cols, axis=1)
    gain_term = jnp.concatenate([gain_attn[None], gain_heads, gain_ffn[None]], axis=0)
    gain_send = gain_term.reshape(4, devices, own_rows).transpose(1, 0, 2)
    (terms,) = small_exchange(
        [packed_rows([router_term.reshape(devices, -1), gain_send.reshape(devices, -1)], 8)],
        ("dp", "seq"),
        14,
    )
    total = jnp.sum(terms, axis=0).reshape(-1)
    router_grad = total[:n_router].reshape(own_rows, experts_all)
    gain_grad = total[n_router : n_router + n_gain].reshape(4, own_rows)
    return (
        block_out,
        input_grad,
        attn_grad,
        router_grad,
        gain_grad,
        expert_in_grad,
        expert_out_grad,
    )


def solution(mesh):
    in_specs = (
        P("dp", "seq", None),
        P("dp", None),
        P("dp", "seq", None),
        P("dp", "seq", None),
        P(("dp", "seq"), None, None),
        P(("dp", "seq"), None),
        P(None, ("dp", "seq")),
        P("seq", "dp", None, None),
        P("seq", None, "dp"),
    )
    out_specs = (
        P("dp", "seq", None),
        P("dp", "seq", None),
        P(("dp", "seq"), None, None),
        P(("dp", "seq"), None),
        P(None, ("dp", "seq")),
        P("seq", "dp", None, None),
        P("seq", None, "dp"),
    )
    return jax.shard_map(local, mesh=mesh, in_specs=in_specs, out_specs=out_specs, check_vma=False)
```

time: 3750 us -> 1510 us (0.40)
  waiting for transfers between devices: 2240 us -> 124 us
  Pallas kernels: 0 us -> 828 us
  blocking collectives: 778 us -> 27.2 us
  local copies, waits for them, and re-layouts: 248 us -> 139 us
  other arithmetic: 151 us -> 68.3 us
    reduce_scatter x3 -> x4, waiting for transfers between devices: 1740 us -> 123 us  [the longest x1 123 us: local(): lax.psum_scatter(in_term, 'dp', scatter_dimension=1, tiled=True).astype(F32)]
    pallas_call x0 -> x14, Pallas kernels: none -> 828 us  [the longest x4 382 us: seq_gather(): pl.pallas_call(kernel, out_shape=jax.ShapeDtypeStruct((seq, rows, width),...]
    all_to_all x3 -> x1, blocking collectives: 445 us -> 27.2 us  [local(): lax.all_to_all(qkv_send, 'seq', split_axis=0, concat_axis=0, tiled=True)]
    all_gather x2 -> x0, blocking collectives: 332 us -> none  [the longest x1 261 us: local(): lax.all_gather(router_weight, ('dp', 'seq'), axis=0, tiled=True)]
    all_to_all x9 -> x2, waiting for transfers between devices: 329 us -> 0.01 us  [the longest x1 0.01 us: local(): lax.all_to_all(out_send, 'seq', split_axis=0, concat_axis=0, tiled=True)]
    all_gather x3 -> x4, waiting for transfers between devices: 115 us -> 0.03 us  [the longest x1 0.02 us: local(): in_full = lax.all_gather(expert_in, 'dp', axis=1, tiled=True)]
    gather x4 -> x0, local copies, waits for them, and re-layouts: 64 us -> none  [the longest x1 21.3 us: local(): jnp.take(returned, safe_place, axis=0)]
    all_to_all x16 -> x1, local copies, waits for them, and re-layouts: 54.8 us -> 0.96 us  [local(): lax.all_to_all(qkv_send, 'seq', split_axis=0, concat_axis=0, tiled=True)]
  transfers between devices with their start and end apart: 17 -> 11, of which waited for: 12 -> 1; matrix products, arithmetic and copies ran while one was open for 10% -> 19% of each run, Pallas kernels for 0% -> 42%
where the time goes in v1:
time: 1510 us; the launch traced here: 1500 us
  Pallas kernels  828 us (55%)
  matrix products  286 us (19%)
  local copies, waits for them, and re-layouts  139 us (9%)
  waiting for transfers between devices  124 us (8%)
  other arithmetic  68.3 us (5%)
  blocking collectives  27.2 us (2%)
  between operations  15.6 us (1%)
    pallas_call x4, Pallas kernels, seq_gather(): pl.pallas_call(kernel, out_shape=jax.ShapeDtypeStruct((seq, rows, width),...  382 us
    pallas_call x4, Pallas kernels, seq_reduce(): pl.pallas_call(kernel, out_shape=jax.ShapeDtypeStruct((rows, width), F32)...  371 us
    reduce_scatter x1, waiting for transfers between devices, local(): lax.psum_scatter(in_term, 'dp', scatter_dimension=1, tiled=True).astype(F32)  123 us
    pallas_call x6, Pallas kernels, small_exchange(): pl.pallas_call(kernel, out_shape=[jax.ShapeDtypeStruct((peers,) + a.shape...  74.5 us
    unnamed x147, local copies, waits for them, and re-layouts  48.7 us
    dot_general x1, matrix products, local(): jnp.einsum('erd,erjf->edjf', rows, grad_gu, preferred_element_type=F32)  34.7 us
  transfers between devices with their start and end apart: 11, of which 1 were waited for; matrix products, arithmetic and copies ran while one was open for 19% of the time, Pallas kernels for 42%

profile of v1, /device:TPU:0, one launch (start us, length us, event | category | flops | bytes accessed | tf_op | source)
XLA Modules:
  0.0 1499.1 jit_solution(10304591318187165609)
XLA Ops:
  10.0 2.6 reshape.538
  12.7 27.2 %all_to_all.15 = bf16[8,3,64,256]{3,2,1,0:T(8,128)(2,1)S(1)} all-to-all(bf16[8,3,64,256]{3,2,1,0:T(8,128)(2,1)S(1)} %copy.238), channel_id=1, replica_groups=mesh['dp'=4,'seq'=8] {'seq'}, dimensions={0} | all-to-all | bytes 1572864 | tf_op jit(solution)/shard_map/all_to_all | solution.py:475
  41.0 9.4 copy.257
  52.2 7.9 small_exchange.8
  60.8 13.2 small_exchange.6
  77.7 3.1 broadcast_in_dim.110
  80.7 3.8 all-to-all-start.1
  92.3 111.0 %seq_gather.4 = bf16[8,256,2048]{2,1,0:T(8,128)(2,1)} custom-call(bf16[256,2048]{1,0:T(8,128)(2,1)} %fusion.91.x_ref), custom_call_target="tpu_custom_call" | custom-call | tf_op jit(solution)/shard_map/seq_gather/pallas_call | solution.py:116
  203.4 93.9 %seq_gather.6 = bf16[8,256,2048]{2,1,0:T(8,128)(2,1)} custom-call(bf16[256,2048]{1,0:T(8,128)(2,1)} %bitcast.388), custom_call_target="tpu_custom_call" | custom-call | tf_op jit(solution)/shard_map/seq_gather/pallas_call | solution.py:116
  297.2 5.2 fusion.76
  302.5 6.8 copy.260
  310.1 2.8 fusion.113
  314.1 10.4 convolution_bitcast_fusion
  328.1 18.2 %small_exchange.7 = f32[8,32,128]{2,1,0:T(8,128)} custom-call(f32[1,32,128]{2,1,0:T(8,128)} %reshape.492.refs_0_), custom_call_target="tpu_custom_call" | custom-call | tf_op jit(solution)/shard_map/small_exchange/pallas_call | solution.py:337
  349.4 2.6 copy.241
  352.0 2.5 fusion.128
  375.3 17.0 %while.26 = (s32[]{:T(128)}, bf16[2,1024,2,128]{1,3,2,0:T(8,128)(2,1)}, f32[2,2,1024]{2,1,0:T(2,128)S(1)}, bf16[2,1024,2,128]{3,1,2,0:T(8,128)(2,1)S(1)}, s32[2,...) while((s32[]{:T(128)}, ...), condition=%wide.region_6.7_spmd, body=%wide.region_3.6_spmd.sunk | while | flops 1100216320 | bytes 39925916 | solution.py:523
  379.8 3.0 fusion.179
  388.3 3.0 fusion.179
  392.3 3.3 copy.303
  397.2 7.3 convolution_convert_fusion.2
  404.6 95.7 %seq_reduce.4 = f32[256,2048]{1,0:T(8,128)} custom-call(bf16[8,256,2048]{2,1,0:T(8,128)(2,1)} %bitcast.374), custom_call_target="tpu_custom_call" | custom-call | tf_op jit(solution)/shard_map/seq_reduce/pallas_call | solution.py:274
  504.8 90.4 %seq_gather.5 = bf16[8,256,2048]{2,1,0:T(8,128)(2,1)} custom-call(bf16[256,2048]{1,0:T(8,128)(2,1)} %multiply_convert_fusion.7.x_ref), custom_call_target="tpu_custom_call" | custom-call | tf_op jit(solution)/shard_map/seq_gather/pallas_call | solution.py:116
  595.2 8.5 convert_bitcast_fusion
  603.8 9.2 copy.256
  613.5 6.0 fusion.130
  619.6 28.6 %fusion.132 = f32[4,576,2,1024]{3,1,2,0:T(8,128)} fusion(bf16[4,576,2048,1]{2,1,3,0:T(8,128)(2,1)} %bitcast.389, bf16[4,2048,2,1024]{3,1,2,0:T(8,128)(2,1)} %all-gather.8.cloned.1.call-done), kind=kOutput, calls=%fused_computation.222 | convolution fusion | flops 19327352832 | bytes 61865984 | tf_op jit(solution)/shard_map/erd,edjf->erjf/dot_general | solution.py:560
  648.2 10.1 multiply_convert_fusion.3
  658.3 20.1 %multiply_reduce_fusion.1 = (f32[4,576]{1,0:T(4,128)S(1)}, bf16[4,576,2048]{2,1,0:T(8,128)(2,1)}) fusion(f32[4,576,2048]{2,1,0:T(8,128)} %bitcast.377, bf16[4,576,1024]{2,1,0:T(8,128)(2,1)} %multiply_convert_fusion.3, bf16[4,1024,2048]{2,1,0:T(8,128)(2,1)} %all-gather.10.cloned.1.call-done), kind=kOutput, calls=%fused_computation.70 | convolution fusion | flops 9682548736 | bytes 49816576 | tf_op jit(solution)/shard_map/erf,efd->erd/dot_general | solution.py:563
  680.6 8.4 small_exchange.9
  689.9 26.0 %fusion.86 = (bf16[4,576,1,1024]{3,1,0,2:T(8,128)(2,1)}, bf16[4,576,1,1024]{3,1,0,2:T(8,128)(2,1)}) fusion(f32[4,576,2,1024]{3,1,2,0:T(8,128)} %fusion.132, bf16[4,1024,2048]{2,1,0:T(8,128)(2,1)} %all-gather.10.cloned.1.call-done, f32[4,576,2048]{2,1,0:T(8,128)} %bitcast.378, f32[4,576]{1,0:T(4,128)S(1)} %mul.670), kind=kOutput, calls=%fused_computation.101 | convolution fusion | flops 9706143744 | bytes 63972352 | tf_op jit(solution)/shard_map/erd,efd->erf/dot_general | solution.py:576
  716.0 27.5 %bitcast_convert_fusion = bf16[4,576,2048]{2,1,0:T(8,128)(2,1)} fusion(bf16[4,2048,2,1024]{3,1,2,0:T(8,128)(2,1)} %all-gather.8.cloned.1.call-done, bf16[4,576,1,1024]{3,1,0,2:T(8,128)(2,1)} %get-tuple-element.241, bf16[4,576,1,1024]{3,1,0,2:T(8,128)(2,1)} %get-tuple-element.240), kind=kOutput, calls=%fused_computation.69 | convolution fusion | flops 19336790016 | bytes 52428800 | tf_op jit(solution)/shard_map/erjf,edjf->erd/dot_general | solution.py:579
  743.5 10.5 bitcast_convert_fusion.2.p_ref
  754.0 92.7 %seq_reduce.6 = f32[256,2048]{1,0:T(8,128)} custom-call(bf16[8,256,2048]{2,1,0:T(8,128)(2,1)} %bitcast_convert_fusion.2.p_ref), custom_call_target="tpu_custom_call" | custom-call | tf_op jit(solution)/shard_map/seq_reduce/pallas_call | solution.py:274
  846.7 3.1 multiply_reduce_fusion.5
  852.9 87.1 %seq_gather.7 = bf16[8,256,2048]{2,1,0:T(8,128)(2,1)} custom-call(bf16[256,2048]{1,0:T(8,128)(2,1)} %fusion.126.x_ref), custom_call_target="tpu_custom_call" | custom-call | tf_op jit(solution)/shard_map/seq_gather/pallas_call | solution.py:116
  940.0 6.7 convolution_convert_fusion.6
  955.0 27.9 %while.27 = (s32[]{:T(128)}, bf16[2,1024,2,128]{1,3,2,0:T(8,128)(2,1)}, bf16[2,1024,2,128]{1,3,2,0:T(8,128)(2,1)}, bf16[2,1024,2,128]{1,3,2,0:T(8,128)(2,1)}, bf...) while((s32[]{:T(128)}, ...), condition=%wide.region_20.21_spmd, body=%wide.region_18.20_spmd.sunk | while | flops 2718169088 | bytes 101786952 | solution.py:612
  957.3 2.6 fusion.191
  959.9 2.8 multiply_reduce_fusion.9
  962.7 2.7 multiply_convert_fusion.11
  971.2 2.6 fusion.191
  973.9 2.8 multiply_reduce_fusion.9
  976.6 2.7 multiply_convert_fusion.11
  990.5 2.7 reshape.522
  995.5 2.7 reshape.523
  998.2 2.9 multiply_subtract_fusion.1
  1004.5 8.1 small_exchange.10
  1013.6 3.5 multiply_convert_fusion.4
  1018.4 10.4 fusion.88
  1029.1 6.7 convolution_convert_fusion.5
  1035.8 21.6 %convolution_convert_fusion.1 = bf16[4,1024,2048]{2,1,0:T(8,128)(2,1)} fusion(bf16[4,576,1024]{2,1,0:T(8,128)(2,1)} %multiply_convert_fusion.3, f32[4,576,2048]{2,1,0:T(8,128)} %bitcast.379, f32[4,576]{1,0:T(4,128)S(1)} %copy-done.68), kind=kOutput, calls=%fused_computation.76 | convolution fusion | flops 9681502208 | bytes 40379392 | tf_op jit(solution)/shard_map/erf,erd->efd/dot_general | solution.py:580
  1057.5 34.7 %convolution_convert_fusion = bf16[4,2048,2,1024]{3,1,2,0:T(8,128)(2,1)} fusion(bf16[4,576,2048,1]{2,1,3,0:T(8,128)(2,1)} %bitcast.390, bf16[4,576,1,1024]{3,1,0,2:T(8,128)(2,1)} %get-tuple-element.241, bf16[4,576,1,1024]{3,1,0,2:T(8,128)(2,1)} %get-tuple-element.240), kind=kOutput, calls=%fused_computation.68 | convolution fusion | flops 19348848640 | bytes 52428800 | tf_op jit(solution)/shard_map/erd,erjf->edjf/dot_general | solution.py:581
  1093.8 11.0 bitcast_convert_fusion.1
  1104.8 89.2 %seq_reduce.7 = f32[256,2048]{1,0:T(8,128)} custom-call(bf16[8,256,2048]{2,1,0:T(8,128)(2,1)} %bitcast.391), custom_call_target="tpu_custom_call" | custom-call | tf_op jit(solution)/shard_map/seq_reduce/pallas_call | solution.py:274
  1196.2 10.7 bitcast_convert_fusion.3.p_ref
  1209.3 4.7 all-to-all-start.2
  1215.5 93.6 %seq_reduce.5 = f32[256,2048]{1,0:T(8,128)} custom-call(bf16[8,256,2048]{2,1,0:T(8,128)(2,1)} %bitcast_convert_fusion.3.p_ref), custom_call_target="tpu_custom_call" | custom-call | tf_op jit(solution)/shard_map/seq_reduce/pallas_call | solution.py:274
  1309.2 6.3 fusion.95
  1320.2 18.6 %small_exchange.11 = f32[32,24,128]{2,1,0:T(8,128)} custom-call(f32[32,24,128]{2,1,0:T(8,128)} %bitcast.415), custom_call_target="tpu_custom_call" | custom-call | tf_op jit(solution)/shard_map/small_exchange/pallas_call | solution.py:337
  1341.5 2.7 copy.276
  1344.2 6.8 convert_element_type.293
  1351.0 123.2 %reduce-scatter.9.cloned.1.call-done = bf16[4,512,2,1024]{3,1,2,0:T(8,128)(2,1)} async-done(((bf16[4,2048,2,1024]{3,1,2,0:T(8,128)(2,1)}), bf16[4,512,2,1024]{3,1,2,0:T(8,128)(2,1)}) %reduce-scatter.9.cloned.1.call-update) | async-done | bytes 8388624 | tf_op jit(solution)/shard_map/reduce_scatter | solution.py:583
  1474.2 17.7 %copy.278 = f32[4,512,2,1024]{3,2,1,0:T(2,128)} copy(bf16[4,512,2,1024]{3,1,2,0:T(8,128)(2,1)} %reduce-scatter.9.cloned.1.call-done) | data formatting | bytes 25165824
  (341 shorter events, 121.2 us)
Async XLA Ops:
  7.2 70.5 %all-gather.12.cloned.1.call-start = ((), (), s32[]{:S(2)}) async-start(), calls=%async_computation.14 | async-start | bytes 1310720 | tf_op jit(solution)/shard_map/all_gather | solution.py:479
  9.9 304.1 %all-gather.6.cloned.1.call-start = ((), (), s32[]{:S(2)}) async-start(), calls=%async_computation.7 | async-start | bytes 3932160 | tf_op jit(solution)/shard_map/all_gather | solution.py:476
  40.9 578.6 %all-gather.8.cloned.1.call-start = ((), (), s32[]{:S(2)}) async-start(), calls=%async_computation.8 | async-start | bytes 41943040 | tf_op jit(solution)/shard_map/all_gather | solution.py:453
  50.5 607.8 %all-gather.10.cloned.1.call-start = ((), (), s32[]{:S(2)}) async-start(), calls=%async_computation.9 | async-start | bytes 20971520 | tf_op jit(solution)/shard_map/all_gather | solution.py:454
  75.2 5.5 copy-start.45
  77.0 13.7 copy-start.8
  80.7 232.2 %all-to-all-start.1 = ((bf16[8,64,2048]{2,1,0:T(8,128)(2,1)}), bf16[8,64,2048]{2,1,0:T(8,128)(2,1)S(1)}, u32[]{:S(2)}, u32[]{:S(2)}) async-start(bf16[8,64,2048]{2,1,0:T(8,128)(2,1)} %bitcast.45), calls=%async_computation.1 | async-start | bytes 4194304 | tf_op jit(solution)/shard_map/all_to_all | solution.py:481
  84.5 1122.3 %reduce-scatter.5.cloned.1.call-start = ((), (), s32[]{:S(2)}) async-start(), calls=%async_computation.10 | async-start | bytes 3932160 | tf_op jit(solution)/shard_map/reduce_scatter | solution.py:639
  88.5 114.8 %copy-start.54 = (f32[2048]{0:T(1024)}, f32[2048]{0:T(1024)S(1)}, u32[]{:S(2)}) copy-start(f32[2048]{0:T(1024)S(1)} %mul.626) | copy-start | bytes 24580
  90.7 652.8 %copy-start.43 = (s32[4,8,256]{2,0,1:T(4,128)}, s32[4,8,256]{2,0,1:T(4,128)S(1)}, u32[]{:S(2)}) copy-start(s32[4,8,256]{2,0,1:T(4,128)S(1)} %copy.254) | copy-start | bytes 98308
  91.0 112.4 %copy-start.65 = (f32[256]{0:T(256)}, f32[256]{0:T(256)S(1)}, u32[]{:S(2)}) copy-start(f32[256]{0:T(256)S(1)} %rsqrt_bitcast_fusion) | copy-start | bytes 3076
  312.9 42.0 %copy-start.23 = (f32[2048,64]{0,1:T(8,128)}, f32[2048,64]{0,1:T(8,128)S(1)}, u32[]{:S(2)}) copy-start(f32[2048,64]{0,1:T(8,128)S(1)} %get-tuple-element.264) | copy-start | bytes 1572868
  357.4 7.3 copy-start.38
  357.4 10.7 copy-start.37
  368.4 6.9 copy-start.49
  392.3 12.3 copy-start.4
  392.3 12.3 copy-start.6
  392.3 12.3 copy-start.58
  397.2 7.4 copy-start.15
  404.6 95.7 %copy-start.9 = (bf16[2,128,2048]{2,1,0:T(8,128)(2,1)S(1)}, bf16[2,128,2048]{2,1,0:T(8,128)(2,1)}, u32[]{:S(2)}) copy-start(bf16[2,128,2048]{2,1,0:T(8,128)(2,1)} %param.13) | copy-start | bytes 3145732
  500.3 3.3 copy-start.46
  603.8 9.2 copy-start.13
  603.8 9.2 copy-start.21
  619.5 59.0 %copy-start.56 = (f32[4,8,256]{2,0,1:T(4,128)}, f32[4,8,256]{2,0,1:T(4,128)S(1)}, u32[]{:S(2)}) copy-start(f32[4,8,256]{2,0,1:T(4,128)S(1)} %fusion.117) | copy-start | bytes 98308
  689.8 156.9 %copy-start.52 = (bf16[256,32]{0,1:T(8,128)(2,1)}, bf16[256,32]{0,1:T(8,128)(2,1)S(1)}, u32[]{:S(2)}) copy-start(bf16[256,32]{0,1:T(8,128)(2,1)S(1)} %fusion.116) | copy-start | bytes 49156
  689.9 26.0 %copy-start.67 = (f32[4,576]{1,0:T(4,128)}, f32[4,576]{1,0:T(4,128)S(1)}, u32[]{:S(2)}) copy-start(f32[4,576]{1,0:T(4,128)S(1)} %mul.670) | copy-start | bytes 27652
  754.0 92.7 %copy-start.1 = (f32[256,2048]{1,0:T(8,128)S(1)}, f32[256,2048]{1,0:T(8,128)}, u32[]{:S(2)}) copy-start(f32[256,2048]{1,0:T(8,128)} %copy-done) | copy-start | bytes 6291460
  754.0 92.7 %copy-start.22 = (bf16[2048,32]{1,0:T(8,128)(2,1)S(1)}, bf16[2048,32]{1,0:T(8,128)(2,1)}, u32[]{:S(2)}) copy-start(bf16[2048,32]{1,0:T(8,128)(2,1)} %reshape.500) | copy-start | bytes 393220
  754.0 92.7 %copy-start.47 = (f32[2048]{0:T(1024)S(1)}, f32[2048]{0:T(1024)}, u32[]{:S(2)}) copy-start(f32[2048]{0:T(1024)} %mul.664) | copy-start | bytes 24580
  754.0 92.7 %copy-start.62 = (f32[256]{0:T(256)S(1)}, f32[256]{0:T(256)}, u32[]{:S(2)}) copy-start(f32[256]{0:T(256)} %copy-done.61) | copy-start | bytes 3076
  846.7 4.4 copy-start.20
  849.8 90.2 %copy-start.69 = (f32[256]{0:T(256)}, f32[256]{0:T(256)S(1)}, u32[]{:S(2)}) copy-start(f32[256]{0:T(256)S(1)} %broadcast_multiply_fusion.2) | copy-start | bytes 3076
  852.9 87.2 %copy-start.35 = (bf16[4,64,2048]{2,1,0:T(8,128)(2,1)S(1)}, bf16[4,64,2048]{2,1,0:T(8,128)(2,1)}, u32[]{:S(2)}) copy-start(bf16[4,64,2048]{2,1,0:T(8,128)(2,1)} %constant_dynamic-slice_fusion.2) | copy-start | bytes 3145732
  946.8 8.2 copy-start.5
  946.8 8.2 copy-start.7
  946.8 8.2 copy-start.18
  946.8 8.2 copy-start.50
  946.8 8.2 copy-start.59
  982.9 5.2 copy-start.30
  988.8 4.3 copy-start.27
  993.9 4.3 copy-start.24
  993.9 4.3 copy-start.39
  998.2 3.5 slice-start
  998.2 4.1 slice-start.1
  1013.6 4.8 copy-start.42
  1018.4 10.6 copy-start.16
  1028.8 7.0 copy-start.68
  1028.8 286.8 %reduce-scatter.7.cloned.1.call-start = ((), (), s32[]{:S(2)}) async-start(), calls=%async_computation.11 | async-start | bytes 1310720 | tf_op jit(solution)/shard_map/reduce_scatter | solution.py:648
  1035.8 308.4 %reduce-scatter.11.cloned.1.call-start = ((), (), s32[]{:S(2)}) async-start(), calls=%async_computation.13 | async-start | bytes 20971520 | tf_op jit(solution)/shard_map/reduce_scatter | solution.py:582
  1057.4 416.8 %reduce-scatter.9.cloned.1.call-start = ((), (), s32[]{:S(2)}) async-start(), calls=%async_computation.12 | async-start | bytes 41943040 | tf_op jit(solution)/shard_map/reduce_scatter | solution.py:583
  1104.8 89.2 %copy-start.10 = (bf16[2,128,2048]{2,1,0:T(8,128)(2,1)S(1)}, bf16[2,128,2048]{2,1,0:T(8,128)(2,1)}, u32[]{:S(2)}) copy-start(bf16[2,128,2048]{2,1,0:T(8,128)(2,1)} %param.13) | copy-start | bytes 3145732
  1104.8 89.2 %copy-start.55 = (f32[2048]{0:T(1024)S(1)}, f32[2048]{0:T(1024)}, u32[]{:S(2)}) copy-start(f32[2048]{0:T(1024)} %copy-done.54) | copy-start | bytes 24580
  1104.8 89.2 %copy-start.66 = (f32[256]{0:T(256)S(1)}, f32[256]{0:T(256)}, u32[]{:S(2)}) copy-start(f32[256]{0:T(256)} %copy-done.65) | copy-start | bytes 3076
  1104.8 91.4 %copy-start.44 = (s32[4,8,256]{2,0,1:T(4,128)S(1)}, s32[4,8,256]{2,0,1:T(4,128)}, u32[]{:S(2)}) copy-start(s32[4,8,256]{2,0,1:T(4,128)} %copy-done.43) | copy-start | bytes 98308
  1104.8 91.4 %copy-start.57 = (f32[4,8,256]{2,0,1:T(4,128)S(1)}, f32[4,8,256]{2,0,1:T(4,128)}, u32[]{:S(2)}) copy-start(f32[4,8,256]{2,0,1:T(4,128)} %copy-done.56) | copy-start | bytes 98308
  1206.8 7.2 copy-start.14
  1206.8 7.2 copy-start.53
  1209.3 131.9 %all-to-all-start.2 = ((bf16[8,3,64,256]{3,2,1,0:T(8,128)(2,1)}), bf16[8,3,64,256]{3,2,1,0:T(8,128)(2,1)S(1)}, u32[]{:S(2)}, u32[]{:S(2)}) async-start(bf16[8,3,64,256]{3,2,1,0:T(8,128)(2,1)} %copy.271), calls=%async_computation.3 | async-start | bytes 1572864 | tf_op jit(solution)/shard_map/all_to_all | solution.py:640
  1215.5 93.7 %copy-start.2 = (f32[256,2048]{1,0:T(8,128)S(1)}, f32[256,2048]{1,0:T(8,128)}, u32[]{:S(2)}) copy-start(f32[256,2048]{1,0:T(8,128)} %copy-done) | copy-start | bytes 6291460
  1215.5 93.7 %copy-start.48 = (f32[2048]{0:T(1024)S(1)}, f32[2048]{0:T(1024)}, u32[]{:S(2)}) copy-start(f32[2048]{0:T(1024)} %mul.664) | copy-start | bytes 24580
  1215.5 93.7 %copy-start.63 = (f32[256]{0:T(256)S(1)}, f32[256]{0:T(256)}, u32[]{:S(2)}) copy-start(f32[256]{0:T(256)} %copy-done.61) | copy-start | bytes 3076
  1215.5 93.7 %copy-start.70 = (f32[256]{0:T(256)S(1)}, f32[256]{0:T(256)}, u32[]{:S(2)}) copy-start(f32[256]{0:T(256)} %copy-done.69) | copy-start | bytes 3076
  1309.2 9.7 copy-start.60
  1315.6 25.8 %collective-permute-start = (bf16[64,2048]{1,0:T(8,128)(2,1)}, bf16[64,2048]{1,0:T(8,128)(2,1)S(1)}, u32[]{:S(2)}, u32[]{:S(2)}) collective-permute-start(bf16[64,2048]{1,0:T(8,128)(2,1)} %reduce-scatter.7.cloned.1.call-done), channel_id=1, source_target_pairs={{0,0},{1,4},{2,8},{3,12},{4,16},{5,20},{6,24},{7,28},{8,1},{9,5},{... | collective-permute-start | bytes 786440 | tf_op jit(solution)/shard_map/ppermute | solution.py:649
  (32 other events, 50.4 us)
Sparse Core Ops, SparseCore 0:
  10.1 19.4 all-gather.11
  41.1 28.1 all-gather.5
  70.9 202.9 all-gather.7
  275.3 105.9 all-gather.9
  1028.9 38.7 reduce-scatter.4
  1070.2 24.8 reduce-scatter.6
  1098.3 126.1 reduce-scatter.10
  1227.3 246.8 reduce-scatter.8

commit v2 on v1

--- a/solution.py
+++ b/solution.py
@@ -18,9 +18,50 @@
 VMEM_MOST = 60 << 20
 
 
+class Line:
+    def __init__(self, size, place, device):
+        self.size, self.place, self.device = size, place, device
+
+    def has(self, turn):
+        return self.place < self.size - 1 if turn > 0 else self.place > 0
+
+    def inside(self, place):
+        return (place >= 0) & (place < self.size)
+
+
 def grid_of(seq_size):
     lines = 4 if seq_size % 4 == 0 else 1
     return lines, seq_size // lines
+
+
+def seq_lines():
+    dp, me = lax.axis_index("dp"), lax.axis_index("seq")
+    nz, ny = grid_of(lax.axis_size("seq"))
+    along = Line(nz, lax.div(me, ny), lambda turn: (dp, me + turn * ny))
+    across = Line(ny, lax.rem(me, ny), lambda turn: (dp, me + turn))
+    return along, across, me, lambda z, y: z * ny + y
+
+
+def dp_lines():
+    dp, me = lax.axis_index("dp"), lax.axis_index("seq")
+    along = Line(lax.axis_size("dp") // 2, lax.div(dp, 2), lambda turn: (dp + 2 * turn, me))
+    across = Line(2, lax.rem(dp, 2), lambda turn: (dp + turn, me))
+    return along, across, dp, lambda x, core: 2 * x + core
+
+
+def cost_of(microseconds):
+    return pl.CostEstimate(flops=0, bytes_accessed=microseconds * 3_600_000, transcendentals=0)
+
+
+def send_to(src, dst, send_sem, recv_sem, device):
+    return pltpu.make_async_remote_copy(
+        src_ref=src,
+        dst_ref=dst,
+        send_sem=send_sem,
+        recv_sem=recv_sem,
+        device_id=device,
+        device_id_type=MESH,
+    )
 
 
 def greet(targets):
@@ -36,81 +77,155 @@
     pl.semaphore_wait(barrier, count)
 
 
-def neighbours(dp, z, y, nz, ny):
-    return {
-        ("z", 1): (z < nz - 1, (dp, (z + 1) * ny + y)),
-        ("z", -1): (z > 0, (dp, (z - 1) * ny + y)),
-        ("y", 1): (y < ny - 1, (dp, z * ny + y + 1)),
-        ("y", -1): (y > 0, (dp, z * ny + y - 1)),
-    }
-
-
-def seq_gather(block, collective_id, pieces=2):
+def greet_lines(*lines):
+    greet([(line.has(turn), line.device(turn)) for line in lines for turn in (1, -1)])
+
+
+def cuts_of(rows, ny):
+    unit = rows // 16
+    late = max(1, unit * 3 // 16) if ny == 2 else unit // 2
+    early = unit - late
+    half = (early + 1) // 2
+    firsts = [(0, half * 16)] + ([(half * 16, (early - half) * 16)] if early > half else [])
+    return firsts, [(early * 16, late * 16)]
+
+
+class Gather:
+    def __init__(self, first, second, me, flat, pieces, own, slot, send_sem, recv_sem, ready=None):
+        self.first, self.second, self.me, self.flat = first, second, me, flat
+        self.pieces, self.own, self.slot = pieces, own, slot
+        self.send_sem, self.recv_sem, self.ready = send_sem, recv_sem, ready
+        self.sent = []
+
+    def _copy(self, src, origin, h, line, turn):
+        way = (0 if line is self.first else 2) + (turn > 0)
+        return send_to(
+            src,
+            self.slot(origin, h),
+            self.send_sem.at[origin, h, way],
+            self.recv_sem.at[origin, h],
+            line.device(turn),
+        )
+
+    def _send(self, src, origin, h, line, turn, cond):
+        ok = cond & line.has(turn)
+        pl.when(ok)(lambda: self._copy(src, origin, h, line, turn).start())
+        self.sent.append((ok, src, origin, h, line, turn))
+
+    def start(self):
+        for h in range(self.pieces):
+            if self.ready is not None:
+                self.ready(h)
+            for line in (self.first, self.second):
+                for turn in (1, -1):
+                    self._send(self.own(h), self.me, h, line, turn, self.me >= 0)
+
+    def _arrive(self, place, side, h, sends):
+        first, second = self.first, self.second
+        cond = first.inside(place) & second.inside(side)
+        origin = lax.select(cond, self.flat(place, side), self.me)
+
+        @pl.when(cond)
+        def _():
+            self._copy(self.slot(origin, h), origin, h, first, 1).wait_recv()
+
+        for line, turn in sends:
+            self._send(self.slot(origin, h), origin, h, line, turn, cond)
+
+    def steps(self):
+        first, second = self.first, self.second
+        listed = []
+        for far in range(1, first.size):
+            for h in range(self.pieces):
+                for sign in (1, -1):
+                    listed.append(
+                        (
+                            far,
+                            lambda far=far, h=h, sign=sign: self._arrive(
+                                first.place - sign * far,
+                                second.place,
+                                h,
+                                [(first, sign), (second, 1), (second, -1)],
+                            ),
+                        )
+                    )
+        for step in range(1, second.size):
+            for far in range(first.size):
+                for h in range(self.pieces):
+                    for sign in (1, -1) if far else (1,):
+                        for turn in (1, -1):
+                            listed.append(
+                                (
+                                    far + step + 0.5,
+                                    lambda far=far, step=step, h=h, sign=sign, turn=turn: self._arrive(
+                                        first.place - sign * far,
+                                        second.place - turn * step,
+                                        h,
+                                        [(second, turn)] if step < second.size - 1 else [],
+                                    ),
+                                )
+                            )
+        return listed
+
+    def finish(self):
+        for ok, src, origin, h, line, turn in self.sent:
+            pl.when(ok)(lambda: self._copy(src, origin, h, line, turn).wait_send())
+
+
+def run_steps(*programs):
+    for _, step in sorted((s for p in programs for s in p.steps()), key=lambda s: s[0]):
+        step()
+
+
+def seq_gathers(block_ref, out_ref, sems):
+    along, across, me, flat = seq_lines()
+    early, late = cuts_of(block_ref.shape[0], across.size)
+    made = []
+    for cuts, first, second, index, (send_sem, recv_sem) in (
+        (early, along, across, flat, sems[0:2]),
+        (late, across, along, lambda y, z: flat(z, y), sems[2:4]),
+    ):
+        made.append(
+            Gather(
+                first,
+                second,
+                me,
+                index,
+                len(cuts),
+                lambda h, cuts=cuts: block_ref.at[pl.ds(*cuts[h])],
+                lambda origin, h, cuts=cuts: out_ref.at[origin, pl.ds(*cuts[h])],
+                send_sem,
+                recv_sem,
+            )
+        )
+    return made
+
+
+def gather_sems(seq, rows):
+    early, late = cuts_of(rows, grid_of(seq)[1])
+    return [
+        pltpu.SemaphoreType.DMA((seq, len(early), 4)),
+        pltpu.SemaphoreType.DMA((seq, len(early))),
+        pltpu.SemaphoreType.DMA((seq, len(late), 4)),
+        pltpu.SemaphoreType.DMA((seq, len(late))),
+    ]
+
+
+def seq_gather(block, collective_id):
     rows, width = block.shape
     seq = lax.axis_size("seq")
-    nz, ny = grid_of(seq)
-    part = rows // pieces
-
-    def kernel(x_ref, o_ref, send_sem, recv_sem, local_sem):
-        dp, me = lax.axis_index("dp"), lax.axis_index("seq")
-        z, y = lax.div(me, ny), lax.rem(me, ny)
-        near = neighbours(dp, z, y, nz, ny)
-        greet(list(near.values()))
+
+    def kernel(x_ref, o_ref, local_sem, *sems):
+        along, across, me, _ = seq_lines()
+        greet_lines(along, across)
         own = pltpu.make_async_copy(x_ref, o_ref.at[me], local_sem)
         own.start()
-        sent = []
-        names = list(near)
-
-        def cut(h):
-            return pl.ds(h * part, part)
-
-        def copy(src, origin, h, name):
-            return pltpu.make_async_remote_copy(
-                src_ref=src,
-                dst_ref=o_ref.at[origin, cut(h)],
-                send_sem=send_sem.at[origin, h, names.index(name)],
-                recv_sem=recv_sem.at[origin, h],
-                device_id=near[name][1],
-                device_id_type=MESH,
-            )
-
-        def send(src, origin, h, name, cond):
-            ok = jnp.logical_and(cond, near[name][0])
-            pl.when(ok)(lambda: copy(src, origin, h, name).start())
-            sent.append((ok, src, origin, h, name))
-
-        def arrive(origin, h, cond):
-            @pl.when(cond)
-            def _():
-                copy(o_ref.at[origin, cut(h)], origin, h, names[0]).wait_recv()
-
-        always = z >= 0
-        for h in range(pieces):
-            for name in names:
-                send(x_ref.at[cut(h)], me, h, name, always)
-        for far in range(1, nz):
-            for h in range(pieces):
-                for sign in (1, -1):
-                    zz = z - sign * far
-                    cond = jnp.logical_and(zz >= 0, zz < nz)
-                    origin = lax.select(cond, zz * ny + y, me)
-                    arrive(origin, h, cond)
-                    for name in (("z", sign), ("y", 1), ("y", -1)):
-                        send(o_ref.at[origin, cut(h)], origin, h, name, cond)
-        for side in range(1, ny):
-            for far in range(nz):
-                for h in range(pieces):
-                    for sign in (1, -1) if far else (1,):
-                        zz = z - sign * far
-                        for turn in (1, -1):
-                            yy = y - turn * side
-                            cond = (zz >= 0) & (zz < nz) & (yy >= 0) & (yy < ny)
-                            origin = lax.select(cond, zz * ny + yy, me)
-                            arrive(origin, h, cond)
-                            if side < ny - 1:
-                                send(o_ref.at[origin, cut(h)], origin, h, ("y", turn), cond)
-        for ok, src, origin, h, name in sent:
-            pl.when(ok)(lambda: copy(src, origin, h, name).wait_send())
+        programs = seq_gathers(x_ref, o_ref, sems)
+        for program in programs:
+            program.start()
+        run_steps(*programs)
+        for program in programs:
+            program.finish()
         own.wait()
 
     return pl.pallas_call(
@@ -118,177 +233,377 @@
         out_shape=jax.ShapeDtypeStruct((seq, rows, width), block.dtype),
         in_specs=[pl.BlockSpec(memory_space=pl.ANY)],
         out_specs=pl.BlockSpec(memory_space=pl.ANY),
-        scratch_shapes=[
-            pltpu.SemaphoreType.DMA((seq, pieces, 4)),
-            pltpu.SemaphoreType.DMA((seq, pieces)),
-            pltpu.SemaphoreType.DMA,
-        ],
+        scratch_shapes=[pltpu.SemaphoreType.DMA] + gather_sems(seq, rows),
         compiler_params=pltpu.CompilerParams(collective_id=collective_id, has_side_effects=True),
         name="seq_gather",
+        cost_estimate=cost_of(80),
     )(block)
 
 
-def seq_reduce(terms, collective_id, pieces=2):
-    seq, rows, width = terms.shape
-    nz, ny = grid_of(seq)
-    part = rows // pieces
-    sides = 1 if ny == 2 else 2
-    strip = 16
-
-    def kernel(p_ref, o_ref, acc, from_y, from_z, send_sem, ysem, zsem):
-        dp, me = lax.axis_index("dp"), lax.axis_index("seq")
-        z, y = lax.div(me, ny), lax.rem(me, ny)
-        near = neighbours(dp, z, y, nz, ny)
-        names = list(near)
-        greet(list(near.values()))
-        sent = []
-
-        def cut(h):
-            return pl.ds(h * part, part)
-
-        def lane(turn):
-            return 0 if sides == 1 else (0 if turn == 1 else 1)
-
-        def copy(src, dest, h, name):
-            if name[0] == "y":
-                dst, sem = from_y.at[lane(name[1]), dest, cut(h)], ysem.at[lane(name[1]), dest, h]
-            else:
-                side = 0 if name[1] == 1 else 1
-                zz = lax.div(dest, ny)
-                dst, sem = from_z.at[side, zz, cut(h)], zsem.at[side, zz, h]
-            return pltpu.make_async_remote_copy(
-                src_ref=src,
-                dst_ref=dst,
-                send_sem=send_sem.at[dest, h],
-                recv_sem=sem,
-                device_id=near[name][1],
-                device_id_type=MESH,
-            )
-
-        def send(src, dest, h, name, ok):
-            pl.when(ok)(lambda: copy(src, dest, h, name).start())
-            sent.append((ok, src, dest, h, name))
-
-        def add_up(refs, out, h):
+class Reduce:
+    def __init__(self, first, second, me, flat, cuts, terms, acc, out, from_first, from_second, sems):
+        self.first, self.second, self.me, self.flat, self.cuts = first, second, me, flat, cuts
+        self.terms, self.acc, self.out = terms, acc, out
+        self.from_first, self.from_second = from_first, from_second
+        self.send_sem, self.first_sem, self.second_sem = sems
+        self.base = cuts[0][0]
+        self.sent = []
+
+    @staticmethod
+    def scratch(rows_of, first_size, second_size, width):
+        seq, rows, pieces = first_size * second_size, sum(r for _, r in rows_of), len(rows_of)
+        lanes = 1 if first_size == 2 else 2
+        return [
+            pltpu.VMEM((lanes, seq, rows, width), BF),
+            pltpu.VMEM((2, second_size, rows, width), BF),
+            pltpu.SemaphoreType.DMA((seq, pieces)),
+            pltpu.SemaphoreType.DMA((lanes, seq, pieces)),
+            pltpu.SemaphoreType.DMA((2, second_size, pieces)),
+        ]
+
+    def _lane(self, turn):
+        return 0 if self.first.size == 2 or turn > 0 else 1
+
+    def _cut(self, h):
+        return pl.ds(*self.cuts[h])
+
+    def _inner(self, h):
+        return pl.ds(self.cuts[h][0] - self.base, self.cuts[h][1])
+
+    def _copy(self, src, dest, spot, h, line, turn):
+        if line is self.first:
+            lane = self._lane(turn)
+            dst, sem = self.from_first.at[lane, dest, self._inner(h)], self.first_sem.at[lane, dest, h]
+        else:
+            side = 0 if turn > 0 else 1
+            dst, sem = self.from_second.at[side, spot, self._inner(h)], self.second_sem.at[side, spot, h]
+        return send_to(src, dst, self.send_sem.at[dest, h], sem, line.device(turn))
+
+    def _send(self, src, dest, spot, h, line, turn, ok):
+        pl.when(ok)(lambda: self._copy(src, dest, spot, h, line, turn).start())
+        self.sent.append((ok, src, dest, spot, h, line, turn))
+
+    def _add(self, cond, whole, parts, out, h):
+        first, count = self.cuts[h]
+
+        @pl.when(cond)
+        def _():
             def body(i, carry):
-                at = pl.ds(h * part + i * strip, strip)
-                total = refs[0][at, :].astype(F32)
-                for ref in refs[1:]:
-                    total = total + ref[at, :].astype(F32)
+                at = pl.ds(pl.multiple_of(first + i * 16, 16), 16)
+                inner = pl.ds(pl.multiple_of(first - self.base + i * 16, 16), 16)
+                total = None
+                for ref in whole:
+                    total = ref[at, :].astype(F32) if total is None else total + ref[at, :].astype(F32)
+                for ref in parts:
+                    total = total + ref[inner, :].astype(F32)
                 out[at, :] = total.astype(out.dtype)
                 return carry
 
-            lax.fori_loop(0, part // strip, body, 0)
-
-        def order():
-            for far in range(nz - 1, -1, -1):
-                for sign in (1, -1) if far else (1,):
-                    zz = z + sign * far
-                    yield far, sign, zz, (zz >= 0) & (zz < nz)
-
-        for side in range(ny - 1, 0, -1):
-            for far, sign, zz, ok in order():
-                for h in range(pieces):
+            lax.fori_loop(0, count // 16, body, 0)
+
+    def _spread(self):
+        for far in range(self.second.size - 1, -1, -1):
+            for sign in (1, -1) if far else (1,):
+                spot = self.second.place + sign * far
+                yield far, sign, spot, self.second.inside(spot)
+
+    def outward(self):
+        first = self.first
+        for step in range(first.size - 1, 0, -1):
+            for far, sign, spot, ok in self._spread():
+                for h in range(len(self.cuts)):
                     for turn in (1, -1):
-                        yy = y + turn * side
-                        go = ok & (yy >= 0) & (yy < ny)
-                        dest = lax.select(go, zz * ny + yy, me)
-                        behind = near[("y", -turn)][0]
-                        if ny == 2:
-                            send(p_ref.at[dest, cut(h)], dest, h, ("y", turn), go)
-                        else:
-
-                            @pl.when(go & behind)
-                            def _():
-                                copy(p_ref.at[dest, cut(h)], dest, h, ("y", turn)).wait_recv()
-                                add_up([p_ref.at[dest], from_y.at[lane(turn), dest]], acc.at[dest], h)
-
-                            @pl.when(go & jnp.logical_not(behind))
-                            def _():
-                                add_up([p_ref.at[dest]], acc.at[dest], h)
-
-                            send(acc.at[dest, cut(h)], dest, h, ("y", turn), go)
-        for far, sign, zz, ok in order():
-            dest = lax.select(ok, zz * ny + y, me)
-            for h in range(pieces):
-                for turn in (1, -1):
-
-                    @pl.when(ok & near[("y", -turn)][0])
-                    def _():
-                        copy(p_ref.at[dest, cut(h)], dest, h, ("y", turn)).wait_recv()
-
-                if ny == 2:
-
-                    @pl.when(ok)
-                    def _():
-                        add_up([p_ref.at[dest], from_y.at[0, dest]], acc.at[dest], h)
-
-                else:
-
-                    @pl.when(ok)
-                    def _():
-                        add_up([p_ref.at[dest]], acc.at[dest], h)
-
-                    for turn in (1, -1):
-
-                        @pl.when(ok & near[("y", -turn)][0])
-                        def _():
-                            add_up([acc.at[dest], from_y.at[lane(turn), dest]], acc.at[dest], h)
-
-                if far:
-                    name = ("z", sign)
-                    behind = near[("z", -sign)][0]
-                    side = 0 if sign == 1 else 1
-
-                    @pl.when(ok & behind)
-                    def _():
-                        copy(acc.at[dest, cut(h)], dest, h, name).wait_recv()
-                        add_up([acc.at[dest], from_z.at[side, zz]], acc.at[dest], h)
-
-                    send(acc.at[dest, cut(h)], dest, h, name, ok)
-                else:
-                    below, above = near[("z", -1)][0], near[("z", 1)][0]
-                    for sign2, cond in ((1, below), (-1, above)):
-
-                        @pl.when(cond)
-                        def _():
-                            copy(acc.at[me, cut(h)], me, h, ("z", sign2)).wait_recv()
-
-                    lower, upper = from_z.at[0, z], from_z.at[1, z]
-
-                    @pl.when(below & above)
-                    def _():
-                        add_up([acc.at[me], lower, upper], o_ref, h)
-
-                    @pl.when(below & jnp.logical_not(above))
-                    def _():
-                        add_up([acc.at[me], lower], o_ref, h)
-
-                    @pl.when(jnp.logical_not(below) & above)
-                    def _():
-                        add_up([acc.at[me], upper], o_ref, h)
-
-        for ok, src, dest, h, name in sent:
-            pl.when(ok)(lambda: copy(src, dest, h, name).wait_send())
+                        yield lambda a=(step, spot, ok, h, turn): self._pass_on(*a)
+
+    def _pass_on(self, step, spot, ok, h, turn):
+        first = self.first
+        goal = first.place + turn * step
+        go = ok & first.inside(goal)
+        dest = lax.select(go, self.flat(goal, spot), self.me)
+        if first.size == 2:
+            self._send(self.terms.at[dest, self._cut(h)], dest, spot, h, first, turn, go)
+            return
+        behind = first.has(-turn)
+        self._await(go & behind, dest, spot, h, first, turn)
+        self._add(go & behind, [self.terms.at[dest]], [self.from_first.at[self._lane(turn), dest]], self.acc.at[dest], h)
+        self._add(go & jnp.logical_not(behind), [self.terms.at[dest]], [], self.acc.at[dest], h)
+        self._send(self.acc.at[dest, self._cut(h)], dest, spot, h, first, turn, go)
+
+    def _await(self, cond, dest, spot, h, line, turn):
+        @pl.when(cond)
+        def _():
+            self._copy(self.acc.at[dest, self._cut(h)], dest, spot, h, line, turn).wait_recv()
+
+    def inward(self):
+        for far, sign, spot, ok in self._spread():
+            for h in range(len(self.cuts)):
+                yield lambda a=(far, sign, spot, ok, h): self._collect(*a)
+
+    def _collect(self, far, sign, spot, ok, h):
+        first, second, acc = self.first, self.second, self.acc
+        dest = lax.select(ok, self.flat(first.place, spot), self.me)
+        for turn in (1, -1):
+            self._await(ok & first.has(-turn), dest, spot, h, first, turn)
+        if first.size == 2:
+            self._add(ok, [self.terms.at[dest]], [self.from_first.at[0, dest]], acc.at[dest], h)
+        else:
+            low, high = first.has(-1), first.has(1)
+            lows, highs = self.from_first.at[self._lane(1), dest], self.from_first.at[self._lane(-1), dest]
+            self._add(ok & low & high, [self.terms.at[dest]], [lows, highs], acc.at[dest], h)
+            self._add(ok & low & jnp.logical_not(high), [self.terms.at[dest]], [lows], acc.at[dest], h)
+            self._add(ok & high & jnp.logical_not(low), [self.terms.at[dest]], [highs], acc.at[dest], h)
+        if far:
+            behind = second.has(-sign)
+            side = 0 if sign > 0 else 1
+            self._await(ok & behind, dest, spot, h, second, sign)
+            self._add(ok & behind, [acc.at[dest]], [self.from_second.at[side, spot]], acc.at[dest], h)
+            self._send(acc.at[dest, self._cut(h)], dest, spot, h, second, sign, ok)
+            return
+        low, high = second.has(-1), second.has(1)
+        self._await(low, dest, spot, h, second, 1)
+        self._await(high, dest, spot, h, second, -1)
+        lows, highs = self.from_second.at[0, spot], self.from_second.at[1, spot]
+        self._add(low & high, [acc.at[dest]], [lows, highs], self.out, h)
+        self._add(low & jnp.logical_not(high), [acc.at[dest]], [lows], self.out, h)
+        self._add(high & jnp.logical_not(low), [acc.at[dest]], [highs], self.out, h)
+
+    def finish(self):
+        for ok, src, dest, spot, h, line, turn in self.sent:
+            pl.when(ok)(lambda: self._copy(src, dest, spot, h, line, turn).wait_send())
+
+
+def woven(*lists):
+    keyed = [((i + 1) / len(entries), n, entry) for n, entries in enumerate(map(list, lists)) for i, entry in enumerate(entries)]
+    return [entry for _, _, entry in sorted(keyed, key=lambda k: k[:2])]
+
+
+def seq_reduces(terms, acc, out, scratch):
+    along, across, me, flat = seq_lines()
+    early, late = cuts_of(terms.shape[1], across.size)
+    return [
+        Reduce(across, along, me, lambda y, z: flat(z, y), early, terms, acc, out, *scratch[0:2], scratch[2:5]),
+        Reduce(along, across, me, flat, late, terms, acc, out, *scratch[5:7], scratch[7:10]),
+    ]
+
+
+def reduce_scratch(seq, rows, width):
+    nz, ny = grid_of(seq)
+    early, late = cuts_of(rows, ny)
+    return (
+        [pltpu.VMEM((seq, rows, width), BF)]
+        + Reduce.scratch(early, ny, nz, width)
+        + Reduce.scratch(late, nz, ny, width)
+    )
+
+
+def seq_reduce(terms, collective_id):
+    seq, rows, width = terms.shape
+
+    def kernel(p_ref, o_ref, acc, *scratch):
+        along, across, _, _ = seq_lines()
+        greet_lines(along, across)
+        programs = seq_reduces(p_ref, acc, o_ref, scratch)
+        for step in woven(*[p.outward() for p in programs]):
+            step()
+        for step in woven(*[p.inward() for p in programs]):
+            step()
+        for program in programs:
+            program.finish()
 
     return pl.pallas_call(
         kernel,
         out_shape=jax.ShapeDtypeStruct((rows, width), F32),
         in_specs=[pl.BlockSpec(memory_space=pltpu.VMEM)],
         out_specs=pl.BlockSpec(memory_space=pltpu.VMEM),
-        scratch_shapes=[
-            pltpu.VMEM((seq, rows, width), BF),
-            pltpu.VMEM((sides, seq, rows, width), BF),
-            pltpu.VMEM((2, nz, rows, width), BF),
-            pltpu.SemaphoreType.DMA((seq, pieces)),
-            pltpu.SemaphoreType.DMA((sides, seq, pieces)),
-            pltpu.SemaphoreType.DMA((2, nz, pieces)),
-        ],
+        scratch_shapes=reduce_scratch(seq, rows, width),
         compiler_params=pltpu.CompilerParams(
             collective_id=collective_id, has_side_effects=True, vmem_limit_bytes=VMEM_MOST
         ),
         name="seq_reduce",
+        cost_estimate=cost_of(80),
     )(terms)
+
+
+def first_transfers(tokens, qkv_rows, proj_rows, packed, routes, collective_id):
+    seq, ndp = lax.axis_size("seq"), lax.axis_size("dp")
+    devices = seq * ndp
+    rows, width = tokens.shape
+
+    def kernel(x_ref, qkv_ref, proj_ref, packed_ref, routes_ref, x_out, qkv_out, proj_out, packed_out, routes_out, *sems):
+        (local_sem, part_send, part_recv, own_sem, qkv_send, qkv_recv, proj_send, proj_recv, proj_fwd) = sems[:9]
+        (small_send, small_recv, routes_send, routes_recv) = sems[9:13]
+        along, across, me, _ = seq_lines()
+        x_line, core_line, dp, dp_flat = dp_lines()
+        rank = dp * seq + me
+        barrier = pltpu.get_barrier_semaphore()
+
+        def device(peer):
+            return (lax.div(peer, seq), lax.rem(peer, seq))
+
+        def meet(step, carry):
+            pl.semaphore_signal(
+                barrier, 1, device_id=device(lax.rem(rank + step, devices)), device_id_type=MESH
+            )
+            return carry
+
+        lax.fori_loop(1, devices, meet, 0)
+        pl.semaphore_wait(barrier, devices - 1)
+
+        own_x = pltpu.make_async_copy(x_ref, x_out.at[me], local_sem.at[0])
+        own_qkv = pltpu.make_async_copy(qkv_ref.at[me], qkv_out.at[dp, me], own_sem)
+        own_x.start()
+        own_qkv.start()
+
+        def part(peer, origin):
+            return send_to(
+                qkv_ref.at[peer], qkv_out.at[dp, origin], part_send.at[peer], part_recv.at[origin], (dp, peer)
+            )
+
+        for step in range(1, seq):
+            part(lax.rem(me + step, seq), me).start()
+
+        goal = lax.div(rank, ndp)
+        place = lax.rem(rank, ndp)
+
+        def proj_first(slot):
+            return send_to(proj_ref, proj_out.at[slot], proj_send, proj_recv.at[slot], (dp, goal))
+
+        stays = goal == me
+        own_proj = pltpu.make_async_copy(proj_ref, proj_out.at[place], local_sem.at[1])
+        pl.when(stays)(own_proj.start)
+        pl.when(jnp.logical_not(stays))(lambda: proj_first(place).start())
+
+        def small(peer, origin):
+            return send_to(
+                packed_ref, packed_out.at[origin], small_send.at[peer], small_recv.at[origin], device(peer)
+            )
+
+        def small_start(step, carry):
+            small(lax.rem(rank + step, devices), rank).start()
+            return carry
+
+        lax.fori_loop(1, devices, small_start, 0)
+
+        def route(peer, origin):
+            return send_to(
+                routes_ref, routes_out.at[origin], routes_send.at[peer], routes_recv.at[origin], (dp, peer)
+            )
+
+        for step in range(1, seq):
+            route(lax.rem(me + step, seq), me).start()
+        packed_out[rank] = packed_ref[...]
+        routes_out[me] = routes_ref[...]
+
+        gathers = seq_gathers(x_ref, x_out, sems[13:])
+        for program in gathers:
+            program.start()
+
+        def ready(h):
+            @pl.when(h == me)
+            def _():
+                own_qkv.wait()
+
+            @pl.when(h != me)
+            def _():
+                part(h, h).wait_recv()
+
+        spread = Gather(
+            x_line,
+            core_line,
+            dp,
+            dp_flat,
+            seq,
+            lambda h: qkv_out.at[dp, h],
+            lambda origin, h: qkv_out.at[origin, h],
+            qkv_send,
+            qkv_recv,
+            ready,
+        )
+        spread.start()
+        root = lax.div(me * ndp, seq)
+        root_x, root_core = lax.div(root, 2), lax.rem(root, 2)
+        on_line = core_line.place == root_core
+        ways = [
+            (on_line & (x_line.place >= root_x) & x_line.has(1), x_line.device(1), 0),
+            (on_line & (x_line.place <= root_x) & x_line.has(-1), x_line.device(-1), 1),
+            (on_line & core_line.has(1), core_line.device(1), 2),
+            (on_line & core_line.has(-1), core_line.device(-1), 3),
+        ]
+
+        def onward(slot, way, target):
+            return send_to(
+                proj_out.at[slot], proj_out.at[slot], proj_fwd.at[slot, way], proj_recv.at[slot], target
+            )
+
+        for slot in range(ndp):
+            held = (dp == root) & (lax.rem(me * ndp + slot, seq) == me)
+
+            @pl.when(held)
+            def _():
+                own_proj.wait()
+
+            @pl.when(jnp.logical_not(held))
+            def _():
+                onward(slot, 0, x_line.device(1)).wait_recv()
+
+            for cond, target, way in ways:
+                pl.when(cond)(lambda: onward(slot, way, target).start())
+        run_steps(*gathers, spread)
+
+        for program in (*gathers, spread):
+            program.finish()
+        for slot in range(ndp):
+            for cond, target, way in ways:
+                pl.when(cond)(lambda: onward(slot, way, target).wait_send())
+        pl.when(jnp.logical_not(stays))(lambda: proj_first(place).wait_send())
+        for step in range(1, seq):
+            part(lax.rem(me + step, seq), me).wait_send()
+            route(lax.rem(me + step, seq), me).wait_send()
+            source = lax.rem(me + seq - step, seq)
+            route(source, source).wait_recv()
+
+        def small_end(step, carry):
+            small(lax.rem(rank + step, devices), rank).wait_send()
+            source = lax.rem(rank + devices - step, devices)
+            small(source, source).wait_recv()
+            return carry
+
+        lax.fori_loop(1, devices, small_end, 0)
+        own_x.wait()
+
+    dma = pltpu.SemaphoreType.DMA
+    hbm, vmem = pl.BlockSpec(memory_space=pl.ANY), pl.BlockSpec(memory_space=pltpu.VMEM)
+    return pl.pallas_call(
+        kernel,
+        out_shape=[
+            jax.ShapeDtypeStruct((seq, rows, width), BF),
+            jax.ShapeDtypeStruct((ndp,) + qkv_rows.shape, BF),
+            jax.ShapeDtypeStruct((ndp,) + proj_rows.shape, BF),
+            jax.ShapeDtypeStruct((devices,) + packed.shape, BF),
+            jax.ShapeDtypeStruct((seq,) + routes.shape, jnp.int32),
+        ],
+        in_specs=[hbm, hbm, hbm, vmem, vmem],
+        out_specs=[hbm, hbm, hbm, vmem, vmem],
+        scratch_shapes=[
+            dma((2,)),
+            dma((seq,)),
+            dma((seq,)),
+            dma,
+            dma((ndp, seq, 4)),
+            dma((ndp, seq)),
+            dma,
+            dma((ndp,)),
+            dma((ndp, 4)),
+            dma((devices,)),
+            dma((devices,)),
+            dma((seq,)),
+            dma((seq,)),
+        ]
+        + gather_sems(seq, rows),
+        compiler_params=pltpu.CompilerParams(collective_id=collective_id, has_side_effects=True),
+        name="first_transfers",
+        cost_estimate=cost_of(120),
+    )(tokens, qkv_rows, proj_rows, packed, routes)
 
 
 def small_exchange(arrays, axes, collective_id):
@@ -345,7 +660,175 @@
         ],
         compiler_params=pltpu.CompilerParams(collective_id=collective_id, has_side_effects=True),
         name="small_exchange",
+        cost_estimate=cost_of(8),
     )(*arrays)
+
+
+def last_transfers(terms, qkv_terms, proj_terms, packed, collective_id):
+    seq, ndp = lax.axis_size("seq"), lax.axis_size("dp")
+    devices = seq * ndp
+    _, rows, width = terms.shape
+    part_rows, cols = qkv_terms.shape[1] // seq, qkv_terms.shape[2]
+    proj_rows = proj_terms.shape[1]
+    n_scratch = len(reduce_scratch(seq, rows, width))
+    n_reduce = 5
+
+    def kernel(p_ref, qkv_ref, proj_ref, packed_ref, o_ref, qkv_out, proj_out, sum_out, acc, *scratch):
+        seq_scratch, rest = scratch[: n_scratch - 1], scratch[n_scratch - 1 :]
+        qkv_acc, qkv_sum, proj_acc, proj_sum, got = rest[:5]
+        qkv_scratch, proj_scratch = rest[5 : 5 + n_reduce], rest[5 + n_reduce : 5 + 2 * n_reduce]
+        (part_send, part_recv, move_send, move_recv, small_send, small_recv, own_sem) = rest[5 + 2 * n_reduce :]
+        _, _, me, _ = seq_lines()
+        x_line, core_line, dp, dp_flat = dp_lines()
+        rank = dp * seq + me
+        barrier = pltpu.get_barrier_semaphore()
+
+        def device(peer):
+            return (lax.div(peer, seq), lax.rem(peer, seq))
+
+        def meet(step, carry):
+            pl.semaphore_signal(
+                barrier, 1, device_id=device(lax.rem(rank + step, devices)), device_id_type=MESH
+            )
+            return carry
+
+        lax.fori_loop(1, devices, meet, 0)
+        pl.semaphore_wait(barrier, devices - 1)
+
+        programs = seq_reduces(p_ref, acc, o_ref, seq_scratch)
+
+        def over_dp(refs, total, out, buffers):
+            return Reduce(
+                core_line,
+                x_line,
+                dp,
+                lambda core, x: dp_flat(x, core),
+                [(0, refs.shape[1])],
+                refs,
+                total,
+                out,
+                *buffers[0:2],
+                buffers[2:5],
+            )
+
+        owners = [
+            over_dp(qkv_ref, qkv_acc, qkv_sum, qkv_scratch),
+            over_dp(proj_ref, proj_acc, proj_sum, proj_scratch),
+        ]
+        for owner in owners:
+            for step in owner.outward():
+                step()
+        for step in woven(*[p.outward() for p in programs]):
+            step()
+
+        def small(peer, origin):
+            return send_to(
+                packed_ref.at[peer], got.at[origin], small_send.at[peer], small_recv.at[origin], device(peer)
+            )
+
+        def small_start(step, carry):
+            small(lax.rem(rank + step, devices), rank).start()
+            return carry
+
+        lax.fori_loop(1, devices, small_start, 0)
+        inner = [list(owner.inward()) for owner in owners]
+        for steps in inner:
+            for step in steps[:-1]:
+                step()
+
+        def part(peer, origin):
+            return send_to(
+                qkv_sum.at[pl.ds(pl.multiple_of(peer * part_rows, 16), part_rows)],
+                qkv_out.at[origin],
+                part_send.at[peer],
+                part_recv.at[origin],
+                (dp, peer),
+            )
+
+        own_part = pltpu.make_async_copy(
+            qkv_sum.at[pl.ds(pl.multiple_of(me * part_rows, 16), part_rows)], qkv_out.at[me], own_sem.at[0]
+        )
+        goal = me * ndp + dp
+        stays = goal == rank
+        own_move = pltpu.make_async_copy(proj_sum, proj_out, own_sem.at[1])
+
+        def move():
+            return send_to(proj_sum, proj_out, move_send, move_recv, device(goal))
+
+        steps = woven(*[p.inward() for p in programs])
+        half = len(steps) // 2
+        for step in steps[:half]:
+            step()
+        for owner_steps in inner:
+            owner_steps[-1]()
+        own_part.start()
+        for step in range(1, seq):
+            part(lax.rem(me + step, seq), me).start()
+        pl.when(stays)(own_move.start)
+        pl.when(jnp.logical_not(stays))(lambda: move().start())
+        for step in steps[half:]:
+            step()
+
+        got[rank] = packed_ref[rank]
+
+        def small_end(step, carry):
+            small(lax.rem(rank + step, devices), rank).wait_send()
+            source = lax.rem(rank + devices - step, devices)
+            small(source, source).wait_recv()
+            return carry
+
+        lax.fori_loop(1, devices, small_end, 0)
+        sum_out[...] = jnp.sum(got[...], axis=0)
+        for program in (*programs, *owners):
+            program.finish()
+        for step in range(1, seq):
+            part(lax.rem(me + step, seq), me).wait_send()
+            source = lax.rem(me + seq - step, seq)
+            part(source, source).wait_recv()
+        own_part.wait()
+
+        @pl.when(stays)
+        def _():
+            own_move.wait()
+
+        @pl.when(jnp.logical_not(stays))
+        def _():
+            move().wait_send()
+            move().wait_recv()
+
+    dma = pltpu.SemaphoreType.DMA
+    vmem = pl.BlockSpec(memory_space=pltpu.VMEM)
+
+    def over_dp_scratch(array):
+        return Reduce.scratch([(0, array.shape[1])], 2, ndp // 2, array.shape[2])
+
+    return pl.pallas_call(
+        kernel,
+        out_shape=[
+            jax.ShapeDtypeStruct((rows, width), F32),
+            jax.ShapeDtypeStruct((seq, part_rows, cols), BF),
+            jax.ShapeDtypeStruct((proj_rows, width), BF),
+            jax.ShapeDtypeStruct(packed.shape[1:], F32),
+        ],
+        in_specs=[vmem] * 4,
+        out_specs=[vmem] * 4,
+        scratch_shapes=reduce_scratch(seq, rows, width)
+        + [
+            pltpu.VMEM(qkv_terms.shape, BF),
+            pltpu.VMEM(qkv_terms.shape[1:], BF),
+            pltpu.VMEM(proj_terms.shape, BF),
+            pltpu.VMEM(proj_terms.shape[1:], BF),
+            pltpu.VMEM(packed.shape, F32),
+        ]
+        + over_dp_scratch(qkv_terms)
+        + over_dp_scratch(proj_terms)
+        + [dma((seq,)), dma((seq,)), dma, dma, dma((devices,)), dma((devices,)), dma((2,))],
+        compiler_params=pltpu.CompilerParams(
+            collective_id=collective_id, has_side_effects=True, vmem_limit_bytes=VMEM_MOST
+        ),
+        name="last_transfers",
+        cost_estimate=cost_of(100),
+    )(terms, qkv_terms, proj_terms, packed)
 
 
 def packed_rows(parts, sublanes):
@@ -450,13 +933,19 @@
     top = routes.shape[-1]
     capacity = (9 * tok * top + 8 * experts_all - 1) // (8 * experts_all)
 
+    n_router, n_gain = own_rows * experts_all, 4 * own_rows
+    token_rows = tokens.reshape(tok, width)
+    x_all, qkv_got, proj_got, small_all, routes_all = first_transfers(
+        token_rows,
+        attn_weight[:, :3].reshape(own_rows, 3, seq, cols).transpose(2, 1, 0, 3),
+        attn_weight[:, 3],
+        packed_rows([router_weight.reshape(1, -1), norm_gains.reshape(1, -1)], 16)[0],
+        routes.reshape(-1, 128),
+        1,
+    )
+    expert_in, expert_out, small_all = lax.optimization_barrier((expert_in, expert_out, small_all))
     in_full = lax.all_gather(expert_in, "dp", axis=1, tiled=True)
     out_full = lax.all_gather(expert_out, "dp", axis=2, tiled=True)
-
-    n_router, n_gain = own_rows * experts_all, 4 * own_rows
-    (small_all,) = small_exchange(
-        [packed_rows([router_weight.reshape(1, -1), norm_gains.reshape(1, -1)], 16)], ("dp", "seq"), 1
-    )
     small_all = small_all.reshape(devices, -1)
     router_full = small_all[:, :n_router].reshape(width, experts_all)
     gain_rows = (
@@ -466,27 +955,14 @@
         .reshape(4, width)
         .astype(F32)
     )
-    (routes_all,) = small_exchange([routes.reshape(1, -1, 128)], ("seq",), 2)
     routes_all = routes_all.reshape(seq, tok, top)
-
-    qkv_send = (
-        attn_weight[:, :3].reshape(own_rows, 3, seq, cols).transpose(2, 1, 0, 3)
-    )
-    qkv_got = lax.all_to_all(qkv_send, "seq", split_axis=0, concat_axis=0, tiled=True)
-    qkv_full = lax.all_gather(qkv_got, "dp", axis=0, tiled=True)
-    qkv_weight = qkv_full.transpose(1, 0, 2, 3).reshape(3, width, cols)
-    spread = seq // ndp
-    out_rows = lax.all_gather(attn_weight[:, 3], "dp", axis=0, tiled=False)
-    out_send = jnp.repeat(out_rows, spread, axis=0)
-    out_got = lax.all_to_all(out_send, "seq", split_axis=0, concat_axis=0, tiled=True)
-    proj_weight = lax.dynamic_slice_in_dim(
-        out_got, lax.rem(me, spread) * ndp, ndp, axis=0
-    ).reshape(cols, width)
-
-    resid_in = tokens.astype(F32).reshape(tok, width)
+    qkv_weight = qkv_got.transpose(2, 0, 1, 3, 4).reshape(3, width, cols)
+    proj_weight = proj_got.reshape(cols, width)
+
+    resid_in = token_rows.astype(F32)
     factor_attn = rms_factor(resid_in)
-    normed_low = (resid_in * factor_attn * gain_rows[0]).astype(BF)
-    normed_all = seq_gather(normed_low, 3).reshape(group, width)
+    group_in = x_all.reshape(group, width).astype(F32)
+    normed_all = (group_in * rms_factor(group_in) * gain_rows[0]).astype(BF)
     raw = jnp.einsum("td,jde->jte", normed_all, qkv_weight, preferred_element_type=F32)
     squares = jnp.sum(raw[:2] * raw[:2], axis=-1).reshape(1, -1, 128)
     (sums,) = small_exchange([squares], ("seq",), 4)
@@ -579,6 +1055,7 @@
     grad_rows = jnp.einsum("erjf,edjf->erd", grad_gu, in_full, preferred_element_type=F32).astype(BF)
     out_term = jnp.einsum("erf,erd->efd", hidden, grad_res, preferred_element_type=F32).astype(BF)
     in_term = jnp.einsum("erd,erjf->edjf", rows, grad_gu, preferred_element_type=F32).astype(BF)
+    out_term, in_term, grad_rows = lax.optimization_barrier((out_term, in_term, grad_rows))
     expert_out_grad = lax.psum_scatter(out_term, "dp", scatter_dimension=2, tiled=True).astype(F32)
     expert_in_grad = lax.psum_scatter(in_term, "dp", scatter_dimension=1, tiled=True).astype(F32)
     dffn_terms = jnp.einsum(
@@ -631,37 +1108,27 @@
         [grad_raw.astype(BF), by_source(grad_v.reshape(flat))[None]], axis=0
     )
     dn_terms = jnp.einsum("jte,jde->td", grad_stack, qkv_weight, preferred_element_type=F32).astype(BF)
-    grad_normed = seq_reduce(dn_terms.reshape(seq, tok, width), 13)
-    qkv_term = jnp.einsum("td,jte->jde", normed_all, grad_stack, preferred_element_type=F32).astype(BF)
-    grad_resid, gain_attn = norm_back(resid_in, factor_attn, gain_rows[0], grad_normed)
-    input_grad = (grad_resid + grad_middle).reshape(num_seqs, local_len, width)
-
-    qkv_part = lax.psum_scatter(qkv_term, "dp", scatter_dimension=1, tiled=True)
-    qkv_out = lax.all_to_all(
-        qkv_part.reshape(3, seq, own_rows, cols).transpose(1, 0, 2, 3),
-        "seq",
-        split_axis=0,
-        concat_axis=0,
-        tiled=True,
-    )
-    qkv_grad = qkv_out.transpose(2, 1, 0, 3).reshape(own_rows, 3, width)
-    proj_part = lax.psum_scatter(proj_term, "dp", scatter_dimension=0, tiled=True)
-    proj_grad = lax.ppermute(
-        proj_part,
-        ("dp", "seq"),
-        [(i * seq + s, s * ndp + i) for i in range(ndp) for s in range(seq)],
-    )
-    attn_grad = jnp.concatenate([qkv_grad, proj_grad[:, None, :]], axis=1).astype(F32)
-    zero_heads = jnp.zeros((2, width), F32)
-    gain_heads = lax.dynamic_update_slice_in_dim(zero_heads, gain_heads, me * cols, axis=1)
+    qkv_term = jnp.einsum("td,jte->jde", normed_all, grad_stack, preferred_element_type=F32)
+    gain_attn = jnp.sum(qkv_term * qkv_weight.astype(F32), axis=(0, 2)) / gain_rows[0]
+
+    gain_heads = lax.dynamic_update_slice_in_dim(jnp.zeros((2, width), F32), gain_heads, me * cols, axis=1)
     gain_term = jnp.concatenate([gain_attn[None], gain_heads, gain_ffn[None]], axis=0)
     gain_send = gain_term.reshape(4, devices, own_rows).transpose(1, 0, 2)
-    (terms,) = small_exchange(
-        [packed_rows([router_term.reshape(devices, -1), gain_send.reshape(devices, -1)], 8)],
-        ("dp", "seq"),
+    grad_normed, qkv_out, proj_grad, total = last_transfers(
+        dn_terms.reshape(seq, tok, width),
+        qkv_term.astype(BF)
+        .reshape(3, ndp, seq, own_rows, cols)
+        .transpose(1, 2, 0, 3, 4)
+        .reshape(ndp, seq * 3 * own_rows, cols),
+        proj_term.reshape(ndp, own_rows, width),
+        packed_rows([router_term.reshape(devices, -1), gain_send.reshape(devices, -1)], 8),
         14,
     )
-    total = jnp.sum(terms, axis=0).reshape(-1)
+    grad_resid, _ = norm_back(resid_in, factor_attn, gain_rows[0], grad_normed)
+    input_grad = (grad_resid + grad_middle).reshape(num_seqs, local_len, width)
+    qkv_grad = qkv_out.reshape(seq, 3, own_rows, cols).transpose(2, 1, 0, 3).reshape(own_rows, 3, width)
+    attn_grad = jnp.concatenate([qkv_grad, proj_grad[:, None, :]], axis=1).astype(F32)
+    total = total.reshape(-1)
     router_grad = total[:n_router].reshape(own_rows, experts_all)
     gain_grad = total[n_router : n_router + n_gain].reshape(4, own_rows)
     return (

time: 1510 us -> 1340 us (0.89)
  waiting for transfers between devices: 124 us -> 1.28 us
  Pallas kernels: 828 us -> 790 us
  other arithmetic: 68.3 us -> 97.6 us
  blocking collectives: 27.2 us -> 0 us
    pallas_call x0 -> x2, Pallas kernels: none -> 240 us  [the longest x1 121 us: first_transfers(): pl.pallas_call(kernel, out_shape=[jax.ShapeDtypeStruct((seq, rows, width)...]
    pallas_call x4 -> x3, Pallas kernels: 382 us -> 245 us  [seq_gather(): pl.pallas_call(kernel, out_shape=jax.ShapeDtypeStruct((seq, rows, width),...]
    reduce_scatter x1, waiting for transfers between devices: 123 us -> 0.01 us  [local(): lax.psum_scatter(in_term, 'dp', scatter_dimension=1, tiled=True).astype(F32)]
    pallas_call x4 -> x3, Pallas kernels: 371 us -> 269 us  [seq_reduce(): pl.pallas_call(kernel, out_shape=jax.ShapeDtypeStruct((rows, width), F32)...]
    pallas_call x6 -> x3, Pallas kernels: 74.5 us -> 35.5 us  [small_exchange(): pl.pallas_call(kernel, out_shape=[jax.ShapeDtypeStruct((peers,) + a.shape...]
    all_to_all x1 -> x0, blocking collectives: 27.2 us -> none  [local(): lax.all_to_all(qkv_send, 'seq', split_axis=0, concat_axis=0, tiled=True)]
    convert_element_type x1 -> x2, other arithmetic: 1.28 us -> 21.7 us  [local(): normed_all = (group_in * rms_factor(group_in) * gain_rows[0]).astype(BF)]
    unnamed x147 -> x161, local copies, waits for them, and re-layouts: 48.7 us -> 36.7 us
  transfers between devices with their start and end apart: 11 -> 4, of which waited for: 1 -> 0; matrix products, arithmetic and copies ran while one was open for 19% -> 26% of each run, Pallas kernels for 42% -> 50%
where the time goes in v2:
time: 1340 us; the launch traced here: 1330 us
  Pallas kernels  790 us (59%)
  matrix products  286 us (21%)
  local copies, waits for them, and re-layouts  138 us (10%)
  other arithmetic  97.6 us (7%)
  between operations  15.4 us (1%)
    pallas_call x3, Pallas kernels, seq_reduce(): pl.pallas_call(kernel, out_shape=jax.ShapeDtypeStruct((rows, width), F32)...  269 us
    pallas_call x3, Pallas kernels, seq_gather(): pl.pallas_call(kernel, out_shape=jax.ShapeDtypeStruct((seq, rows, width),...  245 us
    pallas_call x1, Pallas kernels, first_transfers(): pl.pallas_call(kernel, out_shape=[jax.ShapeDtypeStruct((seq, rows, width)...  121 us
    pallas_call x1, Pallas kernels, last_transfers(): pl.pallas_call(kernel, out_shape=[jax.ShapeDtypeStruct((rows, width), F32...  119 us
    unnamed x161, local copies, waits for them, and re-layouts  36.7 us
    pallas_call x3, Pallas kernels, small_exchange(): pl.pallas_call(kernel, out_shape=[jax.ShapeDtypeStruct((peers,) + a.shape...  35.5 us
    dot_general x1, matrix products, local(): jnp.einsum('erd,erjf->edjf', rows, grad_gu, preferred_element_type=F32)  34.6 us
    dot_general x1, matrix products, local(): jnp.einsum('erd,edjf->erjf', rows, in_full, preferred_element_type=F32)  28.6 us
  transfers between devices with their start and end apart: 4, of which 0 were waited for; matrix products, arithmetic and copies ran while one was open for 26% of the time, Pallas kernels for 50%

profile of v2, /device:TPU:0, one launch (start us, length us, event | category | flops | bytes accessed | tf_op | source)
XLA Modules:
  0.0 1329.3 jit_solution(2671157444191122523)
XLA Ops:
  9.1 2.6 reshape.570
  15.3 121.1 %first_transfers.1 = (bf16[8,256,2048]{2,1,0:T(8,128)(2,1)}, bf16[4,8,3,64,256]{4,3,2,1,0:T(8,128)(2,1)}, bf16[4,64,2048]{2,1,0:T(8,128)(2,1)}, bf16[32,32,128]{2,1,0:T(8,128)(2,1)}, s32[8,16,128]{2,1,0:T(8,128)}) custom-call(bf16[256,2048]{1,0:T(8,128)(2,1)} %bitcast.382, bf16[8,3,64,256]{3,2,1,0:T(8,128)(2,1)} %bitcast.417, bf16[64,2048]{1,0:T(8,128)(2,1)} %bitcast.423, ...), custom_call_target="tpu_custom_call" | custom-call | bytes 432000000 | tf_op jit(solution)/shard_map/first_transfers/pallas_call | solution.py:576
  136.5 9.4 copy.267
  150.2 6.2 multiply_reduce_fusion.2
  157.1 9.5 multiply_convert_fusion.2
  166.5 10.8 convolution_bitcast_fusion
  177.5 4.0 copy-done.3
  182.5 19.7 %small_exchange.3 = f32[8,32,128]{2,1,0:T(8,128)} custom-call(f32[1,32,128]{2,1,0:T(8,128)} %reshape.522.refs_0_), custom_call_target="tpu_custom_call" | custom-call | bytes 28800000 | tf_op jit(solution)/shard_map/small_exchange/pallas_call | solution.py:652
  203.5 2.7 fusion.112
  206.2 2.7 fusion.128
  224.8 2.6 copy.253
  232.4 16.9 %while.26 = (s32[]{:T(128)}, bf16[2,1024,2,128]{1,3,2,0:T(8,128)(2,1)}, f32[2,2,1024]{2,1,0:T(2,128)S(1)}, bf16[2,1024,2,128]{3,1,2,0:T(8,128)(2,1)S(1)}, s32[2,...) while((s32[]{:T(128)}, ...), condition=%wide.region_6.7_spmd, body=%wide.region_3.6_spmd.sunk | while | flops 1100216320 | bytes 31537244 | solution.py:999
  237.4 3.7 fusion.178
  245.7 3.7 fusion.178
  249.4 3.3 copy.313
  254.3 7.3 convolution_convert_fusion.2
  261.7 90.7 %seq_reduce.3 = f32[256,2048]{1,0:T(8,128)} custom-call(bf16[8,256,2048]{2,1,0:T(8,128)(2,1)} %bitcast.379), custom_call_target="tpu_custom_call" | custom-call | bytes 288000000 | tf_op jit(solution)/shard_map/seq_reduce/pallas_call | solution.py:413
  356.9 84.5 %seq_gather.3 = bf16[8,256,2048]{2,1,0:T(8,128)(2,1)} custom-call(bf16[256,2048]{1,0:T(8,128)(2,1)} %multiply_convert_fusion.8.x_ref), custom_call_target="tpu_custom_call" | custom-call | bytes 288000000 | tf_op jit(solution)/shard_map/seq_gather/pallas_call | solution.py:231
  443.1 8.7 convert_bitcast_fusion
  451.8 9.1 copy.266
  461.0 82.9 %seq_gather.4 = bf16[8,256,2048]{2,1,0:T(8,128)(2,1)} custom-call(bf16[256,2048]{1,0:T(8,128)(2,1)} %bitcast.399), custom_call_target="tpu_custom_call" | custom-call | bytes 288000000 | tf_op jit(solution)/shard_map/seq_gather/pallas_call | solution.py:231
  543.9 5.0 fusion.80
  548.9 6.8 copy.270
  555.7 6.0 fusion.130
  561.8 28.6 %fusion.132 = f32[4,576,2,1024]{3,1,2,0:T(8,128)} fusion(bf16[4,576,2048,1]{2,1,3,0:T(8,128)(2,1)} %bitcast.400, bf16[4,2048,2,1024]{3,1,2,0:T(8,128)(2,1)} %all-gather.3.cloned.1.call-done), kind=kOutput, calls=%fused_computation.229 | convolution fusion | flops 19327352832 | bytes 61865984 | tf_op jit(solution)/shard_map/erd,edjf->erjf/dot_general | solution.py:1036
  590.4 10.1 multiply_convert_fusion.4
  600.5 20.1 %multiply_reduce_fusion.1 = (f32[4,576]{1,0:T(4,128)S(1)}, bf16[4,576,2048]{2,1,0:T(8,128)(2,1)}) fusion(f32[4,576,2048]{2,1,0:T(8,128)} %bitcast.383, bf16[4,576,1024]{2,1,0:T(8,128)(2,1)} %multiply_convert_fusion.4, bf16[4,1024,2048]{2,1,0:T(8,128)(2,1)} %all-gather.5.cloned.1.call-done), kind=kOutput, calls=%fused_computation.70 | convolution fusion | flops 9682548736 | bytes 49816576 | tf_op jit(solution)/shard_map/erf,efd->erd/dot_general | solution.py:1039
  622.7 20.3 %convolution_convert_fusion.1 = bf16[4,1024,2048]{2,1,0:T(8,128)(2,1)} fusion(bf16[4,576,1024]{2,1,0:T(8,128)(2,1)} %multiply_convert_fusion.4, f32[4,576,2048]{2,1,0:T(8,128)} %bitcast.384, f32[4,576]{1,0:T(4,128)S(1)} %mul.682), kind=kOutput, calls=%fused_computation.81 | convolution fusion | flops 9681502208 | bytes 40379392 | tf_op jit(solution)/shard_map/erf,erd->efd/dot_general | solution.py:1056
  643.0 26.5 %fusion.91 = (bf16[4,576,1,1024]{3,1,0,2:T(8,128)(2,1)}, bf16[4,576,1,1024]{3,1,0,2:T(8,128)(2,1)}) fusion(f32[4,576,2,1024]{3,1,2,0:T(8,128)} %fusion.132, bf16[4,1024,2048]{2,1,0:T(8,128)(2,1)} %all-gather.5.cloned.1.call-done, f32[4,576,2048]{2,1,0:T(8,128)} %bitcast.385, f32[4,576]{1,0:T(4,128)S(1)} %mul.682), kind=kOutput, calls=%fused_computation.111 | convolution fusion | flops 9706143744 | bytes 63972352 | tf_op jit(solution)/shard_map/erd,efd->erf/dot_general | solution.py:1052
  669.4 34.6 %convolution_convert_fusion = bf16[4,2048,2,1024]{3,1,2,0:T(8,128)(2,1)} fusion(bf16[4,576,2048,1]{2,1,3,0:T(8,128)(2,1)} %bitcast.401, bf16[4,576,1,1024]{3,1,0,2:T(8,128)(2,1)} %get-tuple-element.269, bf16[4,576,1,1024]{3,1,0,2:T(8,128)(2,1)} %get-tuple-element.268), kind=kOutput, calls=%fused_computation.68 | convolution fusion | flops 19348848640 | bytes 52428800 | tf_op jit(solution)/shard_map/erd,erjf->edjf/dot_general | solution.py:1057
  704.1 27.4 %bitcast_convert_fusion = bf16[4,576,2048]{2,1,0:T(8,128)(2,1)} fusion(bf16[4,2048,2,1024]{3,1,2,0:T(8,128)(2,1)} %all-gather.3.cloned.1.call-done, bf16[4,576,1,1024]{3,1,0,2:T(8,128)(2,1)} %get-tuple-element.269, bf16[4,576,1,1024]{3,1,0,2:T(8,128)(2,1)} %get-tuple-element.268), kind=kOutput, calls=%fused_computation.69 | convolution fusion | flops 19336790016 | bytes 52428800 | tf_op jit(solution)/shard_map/erjf,edjf->erd/dot_general | solution.py:1055
  734.3 5.0 copy.284
  741.4 12.3 fusion.62
  754.3 7.8 small_exchange.4
  762.9 11.2 bitcast_convert_fusion.2.p_ref
  774.1 83.2 %seq_reduce.5 = f32[256,2048]{1,0:T(8,128)} custom-call(bf16[8,256,2048]{2,1,0:T(8,128)(2,1)} %bitcast_convert_fusion.2.p_ref), custom_call_target="tpu_custom_call" | custom-call | bytes 288000000 | tf_op jit(solution)/shard_map/seq_reduce/pallas_call | solution.py:413
  857.5 3.1 multiply_reduce_fusion.6
  863.5 78.0 %seq_gather.5 = bf16[8,256,2048]{2,1,0:T(8,128)(2,1)} custom-call(bf16[256,2048]{1,0:T(8,128)(2,1)} %fusion.126.x_ref), custom_call_target="tpu_custom_call" | custom-call | bytes 288000000 | tf_op jit(solution)/shard_map/seq_gather/pallas_call | solution.py:231
  941.6 7.0 convolution_convert_fusion.5
  948.6 2.4 reshape.538
  951.0 2.5 copy.276
  956.9 28.4 %while.27 = (s32[]{:T(128)}, bf16[2,1024,2,128]{1,3,2,0:T(8,128)(2,1)}, bf16[2,1024,2,128]{1,3,2,0:T(8,128)(2,1)}, bf16[2,1024,2,128]{1,3,2,0:T(8,128)(2,1)}, bf...) while((s32[]{:T(128)}, ...), condition=%wide.region_21.22_spmd, body=%wide.region_19.21_spmd.sunk | while | flops 2718169088 | bytes 93398280 | solution.py:1089
  958.8 2.8 multiply_reduce_fusion.11
  961.6 2.7 multiply_convert_fusion.12
  967.7 3.4 fusion.190
  973.0 2.8 multiply_reduce_fusion.11
  975.8 2.7 multiply_convert_fusion.12
  981.9 3.4 fusion.190
  988.9 2.9 reshape.553
  994.1 2.7 reshape.554
  996.8 2.9 multiply_subtract_fusion.1
  1003.3 8.0 small_exchange.5
  1017.0 3.5 multiply_convert_fusion.5
  1020.5 11.4 bitcast_convert_fusion.4
  1035.5 3.2 copy.281
  1040.6 6.9 convolution_convert_fusion.4
  1047.5 9.0 bitcast_convert_fusion.1
  1056.5 118.5 %last_transfers.1 = (f32[256,2048]{1,0:T(8,128)}, bf16[8,192,256]{2,1,0:T(8,128)(2,1)}, bf16[64,2048]{1,0:T(8,128)(2,1)}, f32[24,128]{1,0:T(8,128)}) custom-call(bf16[8,256,2048]{2,1,0:T(8,128)(2,1)} %bitcast.403, bf16[4,1536,256]{2,1,0:T(8,128)(2,1)} %bitcast.398, bf16[4,64,2048]{2,1,0:T(8,128)(2,1)} %bitcast.410, f32[32,24,128]{2,1,0:T(8,128)} %bitcast.421), custom_call_target="tpu_custom_call" | custom-call | bytes 360000000 | tf_op jit(solution)/shard_map/last_transfers/pallas_call | solution.py:805
  1179.4 2.7 copy.287
  1182.1 10.5 bitcast_convert_fusion.3.p_ref
  1192.7 95.6 %seq_reduce.4 = f32[256,2048]{1,0:T(8,128)} custom-call(bf16[8,256,2048]{2,1,0:T(8,128)(2,1)} %bitcast_convert_fusion.3.p_ref), custom_call_target="tpu_custom_call" | custom-call | bytes 288000000 | tf_op jit(solution)/shard_map/seq_reduce/pallas_call | solution.py:413
  1291.7 6.2 fusion.97
  1297.9 6.8 convert_element_type.317
  1304.6 17.7 %copy.289 = f32[4,512,2,1024]{3,2,1,0:T(2,128)} copy(bf16[4,512,2,1024]{3,1,2,0:T(8,128)(2,1)} %reduce-scatter.3.cloned.1.call-done) | data formatting | bytes 25165824
  (323 shorter events, 104.2 us)
Async XLA Ops:
  7.2 6.4 copy-start.73
  7.2 7.2 copy-start.74
  7.2 7.4 copy-start.76
  7.2 554.6 %all-gather.3.cloned.1.call-start = ((), (), s32[]{:S(2)}) async-start(), calls=%async_computation.2 | async-start | bytes 41943040 | tf_op jit(solution)/shard_map/all_gather | solution.py:947
  145.9 454.6 %all-gather.5.cloned.1.call-start = ((), (), s32[]{:S(2)}) async-start(), calls=%async_computation.3 | async-start | bytes 20971520 | tf_op jit(solution)/shard_map/all_gather | solution.py:948
  146.7 1151.2 %reduce-scatter.5.cloned.1.call-start = ((), (), s32[]{:S(2)}) async-start(), calls=%async_computation.5 | async-start | bytes 20971520 | tf_op jit(solution)/shard_map/reduce_scatter | solution.py:1059
  147.9 9.1 copy-start.43
  150.2 16.3 %copy-start.20 = (bf16[3,4,8,64,256]{4,3,2,1,0:T(8,128)(2,1)}, bf16[3,4,8,64,256]{4,3,2,1,0:T(8,128)(2,1)S(1)}, u32[]{:S(2)}) copy-start(bf16[3,4,8,64,256]{4,3,2,1,0:T(8,128)(2,1)S(1)} %copy.251) | copy-start | bytes 9437188
  177.3 4.2 copy-start.3
  202.3 6.6 copy-start.63
  203.5 5.4 copy-start.54
  224.8 7.6 copy-start.49
  249.4 3.3 copy-start.17
  249.4 12.3 copy-start.4
  249.4 12.3 copy-start.6
  249.4 12.3 copy-start.59
  254.3 7.4 copy-start.15
  261.6 90.8 %copy-start.8 = (bf16[2,128,2048]{2,1,0:T(8,128)(2,1)S(1)}, bf16[2,128,2048]{2,1,0:T(8,128)(2,1)}, u32[]{:S(2)}) copy-start(bf16[2,128,2048]{2,1,0:T(8,128)(2,1)} %param.13) | copy-start | bytes 3145732
  352.4 89.0 %copy-start.46 = (f32[2048]{0:T(1024)}, f32[2048]{0:T(1024)S(1)}, u32[]{:S(2)}) copy-start(f32[2048]{0:T(1024)S(1)} %mul.674) | copy-start | bytes 24580
  356.9 84.9 %copy-start.61 = (s32[8,16,128]{2,1,0:T(8,128)S(1)}, s32[8,16,128]{2,1,0:T(8,128)}, u32[]{:S(2)}) copy-start(s32[8,16,128]{2,1,0:T(8,128)} %get-tuple-element.120) | copy-start | bytes 196612
  441.8 113.9 %copy-start.24 = (bf16[2048,32]{1,0:T(8,128)(2,1)}, bf16[2048,32]{1,0:T(8,128)(2,1)S(1)}, u32[]{:S(2)}) copy-start(bf16[2048,32]{1,0:T(8,128)(2,1)S(1)} %reshape.528) | copy-start | bytes 393220
  443.1 177.6 %copy-start.39 = (s32[4,8,256]{2,0,1:T(4,128)}, s32[4,8,256]{2,0,1:T(4,128)S(1)}, u32[]{:S(2)}) copy-start(s32[4,8,256]{2,0,1:T(4,128)S(1)} %copy.264) | copy-start | bytes 98308
  561.7 59.0 %copy-start.56 = (f32[4,8,256]{2,0,1:T(4,128)}, f32[4,8,256]{2,0,1:T(4,128)S(1)}, u32[]{:S(2)}) copy-start(f32[4,8,256]{2,0,1:T(4,128)S(1)} %fusion.116) | copy-start | bytes 98308
  731.5 573.2 %reduce-scatter.3.cloned.1.call-start = ((), (), s32[]{:S(2)}) async-start(), calls=%async_computation.4 | async-start | bytes 41943040 | tf_op jit(solution)/shard_map/reduce_scatter | solution.py:1060
  732.2 7.1 copy-start.66
  732.2 7.2 copy-start.62
  732.2 7.8 copy-start.13
  732.2 7.8 copy-start.25
  732.2 8.3 copy-start.9
  732.2 9.2 copy-start.44
  741.4 12.3 copy-start.58
  741.4 21.5 %copy-start.40 = (s32[4,8,256]{2,0,1:T(4,128)S(1)}, s32[4,8,256]{2,0,1:T(4,128)}, u32[]{:S(2)}) copy-start(s32[4,8,256]{2,0,1:T(4,128)} %copy-done.39) | copy-start | bytes 98308
  774.1 83.3 %copy-start.1 = (f32[256,2048]{1,0:T(8,128)S(1)}, f32[256,2048]{1,0:T(8,128)}, u32[]{:S(2)}) copy-start(f32[256,2048]{1,0:T(8,128)} %copy-done) | copy-start | bytes 6291460
  774.1 83.3 %copy-start.47 = (f32[2048]{0:T(1024)S(1)}, f32[2048]{0:T(1024)}, u32[]{:S(2)}) copy-start(f32[2048]{0:T(1024)} %copy-done.46) | copy-start | bytes 24580
  774.1 83.3 %copy-start.68 = (f32[256]{0:T(256)S(1)}, f32[256]{0:T(256)}, u32[]{:S(2)}) copy-start(f32[256]{0:T(256)} %copy-done.67) | copy-start | bytes 3076
  857.3 4.5 copy-start.23
  857.4 6.1 copy-start.52
  860.5 81.0 %copy-start.71 = (f32[256]{0:T(256)}, f32[256]{0:T(256)S(1)}, u32[]{:S(2)}) copy-start(f32[256]{0:T(256)S(1)} %broadcast_multiply_fusion.2) | copy-start | bytes 3076
  863.5 78.1 %copy-start.38 = (bf16[4,64,2048]{2,1,0:T(8,128)(2,1)S(1)}, bf16[4,64,2048]{2,1,0:T(8,128)(2,1)}, u32[]{:S(2)}) copy-start(bf16[4,64,2048]{2,1,0:T(8,128)(2,1)} %get-tuple-element.119) | copy-start | bytes 3145732
  948.6 8.2 copy-start.5
  948.6 8.2 copy-start.7
  948.6 8.2 copy-start.18
  948.6 8.2 copy-start.50
  948.6 8.2 copy-start.60
  987.2 4.5 copy-start.32
  992.5 4.3 copy-start.27
  992.5 4.3 copy-start.33
  996.8 3.6 slice-start
  996.8 4.4 slice-start.1
  1017.0 3.5 copy-start.36
  1020.5 11.5 copy-start.34
  1020.5 11.5 copy-start.22
  1040.6 6.9 copy-start.21
  1040.6 6.9 copy-start.35
  1040.6 6.9 copy-start.37
  1178.0 4.2 copy-start.41
  1178.0 4.1 copy-start.57
  1192.6 97.1 %copy-start.10 = (bf16[2,128,2048]{2,1,0:T(8,128)(2,1)S(1)}, bf16[2,128,2048]{2,1,0:T(8,128)(2,1)}, u32[]{:S(2)}) copy-start(bf16[2,128,2048]{2,1,0:T(8,128)(2,1)} %param.13) | copy-start | bytes 3145732
  1192.6 97.1 %copy-start.45 = (f32[2048]{0:T(1024)S(1)}, f32[2048]{0:T(1024)}, u32[]{:S(2)}) copy-start(f32[2048]{0:T(1024)} %copy-done.43) | copy-start | bytes 24580
  1192.6 99.0 %copy-start.2 = (f32[256,2048]{1,0:T(8,128)S(1)}, f32[256,2048]{1,0:T(8,128)}, u32[]{:S(2)}) copy-start(f32[256,2048]{1,0:T(8,128)} %copy-done) | copy-start | bytes 6291460
  1192.6 99.0 %copy-start.48 = (f32[2048]{0:T(1024)S(1)}, f32[2048]{0:T(1024)}, u32[]{:S(2)}) copy-start(f32[2048]{0:T(1024)} %copy-done.46) | copy-start | bytes 24580
  1192.6 99.0 %copy-start.69 = (f32[256]{0:T(256)S(1)}, f32[256]{0:T(256)}, u32[]{:S(2)}) copy-start(f32[256]{0:T(256)} %copy-done.67) | copy-start | bytes 3076
  1192.6 99.0 %copy-start.72 = (f32[256]{0:T(256)S(1)}, f32[256]{0:T(256)}, u32[]{:S(2)}) copy-start(f32[256]{0:T(256)} %copy-done.71) | copy-start | bytes 3076
  1192.6 99.0 %copy-start.75 = (f32[256]{0:T(256)S(1)}, f32[256]{0:T(256)}, u32[]{:S(2)}) copy-start(f32[256]{0:T(256)} %rsqrt_bitcast_fusion) | copy-start | bytes 3076
  (24 other events, 40.4 us)
Sparse Core Ops, SparseCore 0:
  146.1 214.1 all-gather.2
  361.8 105.9 all-gather.4
  731.6 126.0 reduce-scatter.4
  860.3 261.5 reduce-scatter.2

commit v3 on v2

--- a/solution.py
+++ b/solution.py
@@ -424,14 +424,49 @@
     )(terms)
 
 
-def first_transfers(tokens, qkv_rows, proj_rows, packed, routes, collective_id):
+def rotary_tables(length):
+    half_dim = HEAD_DIM // 2
+    freqs = jnp.exp(-math.log(ROPE_BASE) * (2.0 * jnp.arange(half_dim, dtype=F32) / HEAD_DIM))
+    angles = jnp.arange(length, dtype=jnp.int32).astype(F32)[:, None] * freqs[None, :]
+    cosine, sine = jnp.cos(angles), jnp.sin(angles)
+    return jnp.concatenate([cosine, cosine], axis=1), jnp.concatenate([-sine, sine], axis=1)
+
+
+def turn_heads(values, cosine, sine):
+    return values * cosine + pltpu.roll(values, HEAD_DIM // 2, 1) * sine
+
+
+def as_columns(row):
+    return jnp.broadcast_to(row, (128, row.shape[1])).T
+
+
+def as_row(column):
+    return jnp.broadcast_to(column, (column.shape[0], 128)).T[0:1]
+
+
+def dot_rows(a, b):
+    return lax.dot_general(a, b, (((1,), (1,)), ((), ())), preferred_element_type=F32)
+
+
+def attend_first(tokens, cotangent, qkv_rows, proj_rows, packed, routes, tables, segments, n_router, collective_id):
     seq, ndp = lax.axis_size("seq"), lax.axis_size("dp")
     devices = seq * ndp
     rows, width = tokens.shape
-
-    def kernel(x_ref, qkv_ref, proj_ref, packed_ref, routes_ref, x_out, qkv_out, proj_out, packed_out, routes_out, *sems):
-        (local_sem, part_send, part_recv, own_sem, qkv_send, qkv_recv, proj_send, proj_recv, proj_fwd) = sems[:9]
-        (small_send, small_recv, routes_send, routes_recv) = sems[9:13]
+    _, _, own_rows, cols = qkv_rows.shape
+    num_seqs, length = segments.shape
+    local_len = length // seq
+    heads_here = cols // HEAD_DIM
+    tile = 256
+    per_block = 128 // own_rows
+
+    def kernel(*refs):
+        (x_ref, c_ref, qkv_ref, proj_ref, packed_ref, routes_ref, cos_ref, sin_ref, col_ref, row_ref) = refs[:10]
+        (normed_out, c_out, w_v, proj_out, packed_out, routes_out) = refs[10:16]
+        (raw_out, q_out, k_out, v_out, o_out, total_out) = refs[16:22]
+        (x_v, normed_v, gains_v, sums_v, sums_got, local_sem, normed_sem) = refs[22:29]
+        (part_send, part_recv, own_sem, qkv_send, qkv_recv, proj_send, proj_recv, proj_fwd) = refs[29:37]
+        (small_send, small_recv, routes_send, routes_recv, sums_send, sums_recv) = refs[37:43]
+        x_sems, c_sems = refs[43:47], refs[47:51]
         along, across, me, _ = seq_lines()
         x_line, core_line, dp, dp_flat = dp_lines()
         rank = dp * seq + me
@@ -449,18 +484,33 @@
         lax.fori_loop(1, devices, meet, 0)
         pl.semaphore_wait(barrier, devices - 1)
 
-        own_x = pltpu.make_async_copy(x_ref, x_out.at[me], local_sem.at[0])
-        own_qkv = pltpu.make_async_copy(qkv_ref.at[me], qkv_out.at[dp, me], own_sem)
+        def weight_rows(origin, h):
+            return w_v.at[:, pl.ds(pl.multiple_of((origin * seq + h) * own_rows, own_rows), own_rows), :]
+
+        own_x = pltpu.make_async_copy(x_ref, x_v.at[me], local_sem.at[0])
+        own_c = pltpu.make_async_copy(c_ref, c_out.at[me], local_sem.at[2])
+        own_qkv = pltpu.make_async_copy(qkv_ref.at[me], weight_rows(dp, me), own_sem)
         own_x.start()
         own_qkv.start()
 
         def part(peer, origin):
             return send_to(
-                qkv_ref.at[peer], qkv_out.at[dp, origin], part_send.at[peer], part_recv.at[origin], (dp, peer)
+                qkv_ref.at[peer], weight_rows(dp, origin), part_send.at[peer], part_recv.at[origin], (dp, peer)
             )
 
         for step in range(1, seq):
             part(lax.rem(me + step, seq), me).start()
+
+        def small(peer, origin):
+            return send_to(
+                packed_ref, packed_out.at[origin], small_send.at[peer], small_recv.at[origin], device(peer)
+            )
+
+        def small_start(step, carry):
+            small(lax.rem(rank + step, devices), rank).start()
+            return carry
+
+        lax.fori_loop(1, devices, small_start, 0)
 
         goal = lax.div(rank, ndp)
         place = lax.rem(rank, ndp)
@@ -473,17 +523,6 @@
         pl.when(stays)(own_proj.start)
         pl.when(jnp.logical_not(stays))(lambda: proj_first(place).start())
 
-        def small(peer, origin):
-            return send_to(
-                packed_ref, packed_out.at[origin], small_send.at[peer], small_recv.at[origin], device(peer)
-            )
-
-        def small_start(step, carry):
-            small(lax.rem(rank + step, devices), rank).start()
-            return carry
-
-        lax.fori_loop(1, devices, small_start, 0)
-
         def route(peer, origin):
             return send_to(
                 routes_ref, routes_out.at[origin], routes_send.at[peer], routes_recv.at[origin], (dp, peer)
@@ -494,7 +533,7 @@
         packed_out[rank] = packed_ref[...]
         routes_out[me] = routes_ref[...]
 
-        gathers = seq_gathers(x_ref, x_out, sems[13:])
+        gathers = seq_gathers(x_ref, x_v, x_sems)
         for program in gathers:
             program.start()
 
@@ -513,12 +552,16 @@
             dp,
             dp_flat,
             seq,
-            lambda h: qkv_out.at[dp, h],
-            lambda origin, h: qkv_out.at[origin, h],
+            lambda h: weight_rows(dp, h),
+            weight_rows,
             qkv_send,
             qkv_recv,
             ready,
         )
+        x_steps = sorted((s for p in gathers for s in p.steps()), key=lambda s: s[0])
+        for hops, step in x_steps:
+            if hops <= 1:
+                step()
         spread.start()
         root = lax.div(me * ndp, seq)
         root_x, root_core = lax.div(root, 2), lax.rem(root, 2)
@@ -535,6 +578,23 @@
                 proj_out.at[slot], proj_out.at[slot], proj_fwd.at[slot, way], proj_recv.at[slot], target
             )
 
+        rest = sorted(
+            [s for s in x_steps if s[0] > 1] + [(hops + 0.75, step) for hops, step in spread.steps()],
+            key=lambda s: s[0],
+        )
+        for _, step in rest:
+            step()
+
+        c_gathers = seq_gathers(c_ref, c_out, c_sems)
+        own_c.start()
+        for program in c_gathers:
+            program.start()
+        c_steps = sorted((s for p in c_gathers for s in p.steps()), key=lambda s: s[0])
+
+        def move_cotangent(hops):
+            while c_steps and c_steps[0][0] <= hops:
+                c_steps.pop(0)[1]()
+
         for slot in range(ndp):
             held = (dp == root) & (lax.rem(me * ndp + slot, seq) == me)
 
@@ -548,9 +608,113 @@
 
             for cond, target, way in ways:
                 pl.when(cond)(lambda: onward(slot, way, target).start())
-        run_steps(*gathers, spread)
-
-        for program in (*gathers, spread):
+
+        def small_end(step, carry):
+            source = lax.rem(rank + devices - step, devices)
+            small(source, source).wait_recv()
+            return carry
+
+        lax.fori_loop(1, devices, small_end, 0)
+        for block in range(width // 128):
+            total = packed_out[block * per_block, n_router : n_router + 16, :].astype(F32)
+            for i in range(1, per_block):
+                total = total + packed_out[block * per_block + i, n_router : n_router + 16, :].astype(F32)
+            gains_v[:, block * 128 : (block + 1) * 128] = total[0:8]
+        own_x.wait()
+
+        def normed_copy(src):
+            return pltpu.make_async_copy(normed_v.at[src], normed_out.at[src], normed_sem.at[src])
+
+        def project(src, carry):
+            def strip(i, inner):
+                at = pl.ds(pl.multiple_of(i * 16, 16), 16)
+                values = x_v[src, at, :].astype(F32)
+                factor = lax.rsqrt(jnp.mean(values * values, axis=-1, keepdims=True) + NORM_EPS)
+                normed_v[src, at, :] = (values * factor * gains_v[0:1, :]).astype(BF)
+                return inner
+
+            lax.fori_loop(0, rows // 16, strip, 0)
+            normed_copy(src).start()
+            at = pl.ds(pl.multiple_of(src * rows, rows), rows)
+            for j in range(2):
+                raw = jnp.dot(normed_v[src], w_v[j], preferred_element_type=F32)
+                raw_out[j, at, :] = raw
+                sums_v[pl.ds(j * seq + src, 1), :] = as_row(jnp.sum(raw * raw, axis=1, keepdims=True))
+            values = jnp.dot(normed_v[src], w_v[2], preferred_element_type=F32).astype(BF)
+            for n in range(num_seqs):
+                v_out[n, pl.ds(pl.multiple_of(src * local_len, local_len), local_len), :] = values[
+                    n * local_len : (n + 1) * local_len
+                ]
+            return carry
+
+        lax.fori_loop(0, seq // 2, project, 0)
+        move_cotangent(1)
+        lax.fori_loop(seq // 2, seq, project, 0)
+
+        def square_sums(peer, origin):
+            return send_to(sums_v, sums_got.at[origin], sums_send.at[peer], sums_recv.at[origin], (dp, peer))
+
+        for step in range(1, seq):
+            square_sums(lax.rem(me + step, seq), me).start()
+        move_cotangent(2)
+        total = sums_v[...]
+        for step in range(1, seq):
+            source = lax.rem(me + seq - step, seq)
+            square_sums(source, source).wait_recv()
+        sums_got[me] = sums_v[...]
+        total = jnp.sum(sums_got[...], axis=0)
+        for step in range(1, seq):
+            square_sums(lax.rem(me + step, seq), me).wait_send()
+        total_out[...] = total
+        sums_v[...] = lax.rsqrt(total / width + NORM_EPS)
+
+        def turn(src, carry):
+            spots = pl.ds(pl.multiple_of(src * local_len, local_len), local_len)
+            cosine, sine = cos_ref[spots, :], sin_ref[spots, :]
+            for j, out in ((0, q_out), (1, k_out)):
+                factor = as_columns(sums_v[pl.ds(j * seq + src, 1), :])
+                for h in range(heads_here):
+                    at = slice(h * HEAD_DIM, (h + 1) * HEAD_DIM)
+                    gain = gains_v[
+                        1 + j : 2 + j, pl.ds(pl.multiple_of(me * cols + h * HEAD_DIM, HEAD_DIM), HEAD_DIM)
+                    ]
+                    for n in range(num_seqs):
+                        low, high = n * local_len, (n + 1) * local_len
+                        values = raw_out[
+                            j, pl.ds(pl.multiple_of(src * rows + low, local_len), local_len), at
+                        ]
+                        values = values * factor[low:high] * gain
+                        out[n, spots, at] = turn_heads(values, cosine, sine).astype(BF)
+            return carry
+
+        lax.fori_loop(0, seq, turn, 0)
+        move_cotangent(2.5)
+
+        def attend(index, carry):
+            n = lax.div(index, heads_here)
+            head = pl.ds(pl.multiple_of(lax.rem(index, heads_here) * HEAD_DIM, HEAD_DIM), HEAD_DIM)
+            for block in range(length // tile):
+                low = block * tile
+                limit = min(length, low + 2 * tile)
+                scores = dot_rows(q_out[n, low : low + tile, head], k_out[n, 0:limit, head]) * HEAD_DIM**-0.5
+                allowed = row_ref[n, 0:1, 0:limit] <= col_ref[n, low : low + tile, :]
+                scores = jnp.where(allowed, scores, MASKED_SCORE)
+                exps = jnp.exp(scores - jnp.max(scores, axis=-1, keepdims=True))
+                probs = (exps / jnp.sum(exps, axis=-1, keepdims=True)).astype(BF)
+                result = jnp.dot(probs, v_out[n, 0:limit, head], preferred_element_type=F32).astype(BF)
+                for i in range(tile // local_len):
+                    src = low // local_len + i
+                    o_out[src, pl.ds(pl.multiple_of(n * local_len, local_len), local_len), head] = result[
+                        i * local_len : (i + 1) * local_len
+                    ]
+            return carry
+
+        lax.fori_loop(0, heads_here, attend, 0)
+        move_cotangent(3)
+        lax.fori_loop(heads_here, num_seqs * heads_here, attend, 0)
+        move_cotangent(1000)
+
+        for program in (*gathers, spread, *c_gathers):
             program.finish()
         for slot in range(ndp):
             for cond, target, way in ways:
@@ -562,30 +726,45 @@
             source = lax.rem(me + seq - step, seq)
             route(source, source).wait_recv()
 
-        def small_end(step, carry):
+        def small_sent(step, carry):
             small(lax.rem(rank + step, devices), rank).wait_send()
-            source = lax.rem(rank + devices - step, devices)
-            small(source, source).wait_recv()
             return carry
 
-        lax.fori_loop(1, devices, small_end, 0)
-        own_x.wait()
+        lax.fori_loop(1, devices, small_sent, 0)
+        for src in range(seq):
+            normed_copy(src).wait()
+        own_c.wait()
 
     dma = pltpu.SemaphoreType.DMA
     hbm, vmem = pl.BlockSpec(memory_space=pl.ANY), pl.BlockSpec(memory_space=pltpu.VMEM)
+    shaped = jax.ShapeDtypeStruct
+    outs = [
+        (shaped((seq, rows, width), BF), hbm),
+        (shaped((seq, rows, width), BF), hbm),
+        (shaped((3, width, cols), BF), vmem),
+        (shaped((ndp,) + proj_rows.shape, BF), hbm),
+        (shaped((devices,) + packed.shape, BF), vmem),
+        (shaped((seq,) + routes.shape, jnp.int32), vmem),
+        (shaped((2, seq * rows, cols), F32), vmem),
+        (shaped((num_seqs, length, cols), BF), vmem),
+        (shaped((num_seqs, length, cols), BF), vmem),
+        (shaped((num_seqs, length, cols), BF), vmem),
+        (shaped((seq, rows, cols), BF), vmem),
+        (shaped((2 * seq, rows), F32), vmem),
+    ]
     return pl.pallas_call(
         kernel,
-        out_shape=[
-            jax.ShapeDtypeStruct((seq, rows, width), BF),
-            jax.ShapeDtypeStruct((ndp,) + qkv_rows.shape, BF),
-            jax.ShapeDtypeStruct((ndp,) + proj_rows.shape, BF),
-            jax.ShapeDtypeStruct((devices,) + packed.shape, BF),
-            jax.ShapeDtypeStruct((seq,) + routes.shape, jnp.int32),
-        ],
-        in_specs=[hbm, hbm, hbm, vmem, vmem],
-        out_specs=[hbm, hbm, hbm, vmem, vmem],
+        out_shape=[shape for shape, _ in outs],
+        in_specs=[hbm] * 4 + [vmem] * 6,
+        out_specs=[spec for _, spec in outs],
         scratch_shapes=[
-            dma((2,)),
+            pltpu.VMEM((seq, rows, width), BF),
+            pltpu.VMEM((seq, rows, width), BF),
+            pltpu.VMEM((8, width), F32),
+            pltpu.VMEM((2 * seq, rows), F32),
+            pltpu.VMEM((seq, 2 * seq, rows), F32),
+            dma((3,)),
+            dma((seq,)),
             dma((seq,)),
             dma((seq,)),
             dma,
@@ -598,12 +777,27 @@
             dma((devices,)),
             dma((seq,)),
             dma((seq,)),
+            dma((seq,)),
+            dma((seq,)),
         ]
+        + gather_sems(seq, rows)
         + gather_sems(seq, rows),
-        compiler_params=pltpu.CompilerParams(collective_id=collective_id, has_side_effects=True),
-        name="first_transfers",
-        cost_estimate=cost_of(120),
-    )(tokens, qkv_rows, proj_rows, packed, routes)
+        compiler_params=pltpu.CompilerParams(
+            collective_id=collective_id, has_side_effects=True, vmem_limit_bytes=VMEM_MOST
+        ),
+        name="attend_first",
+        cost_estimate=cost_of(210),
+    )(
+        tokens,
+        cotangent,
+        qkv_rows,
+        proj_rows,
+        packed,
+        routes,
+        *tables,
+        segments[:, :, None],
+        segments[:, None, :],
+    )
 
 
 def small_exchange(arrays, axes, collective_id):
@@ -662,6 +856,194 @@
         name="small_exchange",
         cost_estimate=cost_of(8),
     )(*arrays)
+
+
+def attend_back(dz, proj_weight, o_head, query, key, value, raw, squares, gains, tables, segments, collective_id):
+    seq = lax.axis_size("seq")
+    rows, width = dz.shape
+    num_seqs, length, cols = query.shape
+    local_len = length // seq
+    heads_here = cols // HEAD_DIM
+    tile = 256
+    scale = HEAD_DIM**-0.5
+
+    def kernel(*refs):
+        (dz_ref, w_ref, o_ref, q_ref, k_ref, v_ref, raw_ref, squares_ref, gains_ref) = refs[:9]
+        (cos_ref, sin_ref, col_ref, row_ref) = refs[9:13]
+        d_out, proj_out, gain_out = refs[13:16]
+        (dz_v, do_v, turned, dk_acc, dv_acc, proj_acc, factor_v, inner_v, inner_got) = refs[16:25]
+        own_sem, inner_send, inner_recv = refs[25:28]
+        sems = refs[28:]
+        dp = lax.axis_index("dp")
+        along, across, me, _ = seq_lines()
+        barrier = pltpu.get_barrier_semaphore()
+        for step in range(1, seq):
+            pl.semaphore_signal(
+                barrier, 1, device_id=(dp, lax.rem(me + step, seq)), device_id_type=MESH
+            )
+        pl.semaphore_wait(barrier, seq - 1)
+        own = pltpu.make_async_copy(dz_ref, dz_v.at[me], own_sem)
+        own.start()
+        programs = seq_gathers(dz_ref, dz_v, sems)
+        for program in programs:
+            program.start()
+        factor_v[...] = lax.rsqrt(squares_ref[...] / width + NORM_EPS)
+        proj_acc[...] = jnp.zeros_like(proj_acc)
+        own.wait()
+        run_steps(*programs)
+
+        def project(src, carry):
+            back = dot_rows(dz_v[src], w_ref[...]).astype(BF)
+            for n in range(num_seqs):
+                do_v[n, pl.ds(pl.multiple_of(src * local_len, local_len), local_len), :] = back[
+                    n * local_len : (n + 1) * local_len
+                ]
+            proj_acc[...] += lax.dot_general(
+                o_ref[src], dz_v[src], (((0,), (0,)), ((), ())), preferred_element_type=F32
+            )
+            return carry
+
+        lax.fori_loop(0, seq, project, 0)
+        proj_out[...] = proj_acc[...].astype(BF)
+
+        def unturn(values, at):
+            return values * cos_ref[at, :] - pltpu.roll(values, HEAD_DIM // 2, 1) * sin_ref[at, :]
+
+        def attend(index, carry):
+            n = lax.div(index, heads_here)
+            head = pl.ds(pl.multiple_of(lax.rem(index, heads_here) * HEAD_DIM, HEAD_DIM), HEAD_DIM)
+            dk_acc[...] = jnp.zeros_like(dk_acc)
+            dv_acc[...] = jnp.zeros_like(dv_acc)
+            for block in range(length // tile):
+                low = block * tile
+                limit = min(length, low + 2 * tile)
+                spots = slice(low, low + tile)
+                queries, keys, grads = q_ref[n, spots, head], k_ref[n, 0:limit, head], do_v[n, spots, head]
+                scores = dot_rows(queries, keys) * scale
+                allowed = row_ref[n, 0:1, 0:limit] <= col_ref[n, spots, :]
+                scores = jnp.where(allowed, scores, MASKED_SCORE)
+                exps = jnp.exp(scores - jnp.max(scores, axis=-1, keepdims=True))
+                probs = exps / jnp.sum(exps, axis=-1, keepdims=True)
+                grad_probs = dot_rows(grads, v_ref[n, 0:limit, head])
+                inner = jnp.sum(probs * grad_probs, axis=-1, keepdims=True)
+                grad_scores = (probs * (grad_probs - inner)).astype(BF)
+                dq = jnp.dot(grad_scores, keys, preferred_element_type=F32) * scale
+                turned[0, n, spots, head] = unturn(dq, spots)
+                dk_acc[0:limit, :] += lax.dot_general(
+                    grad_scores, queries, (((0,), (0,)), ((), ())), preferred_element_type=F32
+                )
+                dv_acc[0:limit, :] += lax.dot_general(
+                    probs.astype(BF), grads, (((0,), (0,)), ((), ())), preferred_element_type=F32
+                )
+            for block in range(length // tile):
+                spots = slice(block * tile, (block + 1) * tile)
+                turned[1, n, spots, head] = unturn(dk_acc[spots, :] * scale, spots)
+            for src in range(seq):
+                d_out[2, src, pl.ds(pl.multiple_of(n * local_len, local_len), local_len), head] = dv_acc[
+                    src * local_len : (src + 1) * local_len, :
+                ].astype(BF)
+            return carry
+
+        lax.fori_loop(0, num_seqs * heads_here, attend, 0)
+
+        def pieces(j, src):
+            spots = pl.ds(pl.multiple_of(src * local_len, local_len), local_len)
+            grads = jnp.concatenate([turned[j, n, spots, :] for n in range(num_seqs)], axis=0)
+            return grads, raw_ref[j, pl.ds(pl.multiple_of(src * rows, rows), rows), :]
+
+        def wide(row):
+            return jnp.concatenate([as_columns(row)] * heads_here, axis=1)
+
+        def measure(src, carry):
+            sums = []
+            for j in range(2):
+                grads, values = pieces(j, src)
+                scaled = grads * gains_ref[j : j + 1, :]
+                inner_v[pl.ds(j * seq + src, 1), :] = as_row(
+                    jnp.sum(scaled * values, axis=1, keepdims=True)
+                )
+                factor = wide(factor_v[pl.ds(j * seq + src, 1), :])
+                sums.append(carry[j] + jnp.sum(grads * values * factor, axis=0, keepdims=True))
+            return tuple(sums)
+
+        zero = jnp.zeros((1, cols), F32)
+        gain_q, gain_k = lax.fori_loop(0, seq, measure, (zero, zero))
+        gain_out[0:1, :] = gain_q
+        gain_out[1:2, :] = gain_k
+        gain_out[2:8, :] = jnp.zeros((6, cols), F32)
+
+        def inner_copy(peer, origin):
+            return send_to(
+                inner_v, inner_got.at[origin], inner_send.at[peer], inner_recv.at[origin], (dp, peer)
+            )
+
+        for step in range(1, seq):
+            inner_copy(lax.rem(me + step, seq), me).start()
+        inner_got[me] = inner_v[...]
+        for program in programs:
+            program.finish()
+        for step in range(1, seq):
+            source = lax.rem(me + seq - step, seq)
+            inner_copy(source, source).wait_recv()
+            inner_copy(lax.rem(me + step, seq), me).wait_send()
+        inner_v[...] = jnp.sum(inner_got[...], axis=0) / width
+
+        def normalize(src, carry):
+            for j in range(2):
+                grads, values = pieces(j, src)
+                factor = wide(factor_v[pl.ds(j * seq + src, 1), :])
+                inner = wide(inner_v[pl.ds(j * seq + src, 1), :])
+                scaled = grads * gains_ref[j : j + 1, :]
+                d_out[j, src] = (factor * (scaled - values * factor * factor * inner)).astype(BF)
+            return carry
+
+        lax.fori_loop(0, seq, normalize, 0)
+
+    dma = pltpu.SemaphoreType.DMA
+    hbm, vmem = pl.BlockSpec(memory_space=pl.ANY), pl.BlockSpec(memory_space=pltpu.VMEM)
+    return pl.pallas_call(
+        kernel,
+        out_shape=[
+            jax.ShapeDtypeStruct((3, seq, rows, cols), BF),
+            jax.ShapeDtypeStruct((cols, width), BF),
+            jax.ShapeDtypeStruct((8, cols), F32),
+        ],
+        in_specs=[hbm] + [vmem] * 12,
+        out_specs=[vmem] * 3,
+        scratch_shapes=[
+            pltpu.VMEM((seq, rows, width), BF),
+            pltpu.VMEM((num_seqs, length, cols), BF),
+            pltpu.VMEM((2, num_seqs, length, cols), F32),
+            pltpu.VMEM((length, HEAD_DIM), F32),
+            pltpu.VMEM((length, HEAD_DIM), F32),
+            pltpu.VMEM((cols, width), F32),
+            pltpu.VMEM((2 * seq, rows), F32),
+            pltpu.VMEM((2 * seq, rows), F32),
+            pltpu.VMEM((seq, 2 * seq, rows), F32),
+            dma,
+            dma((seq,)),
+            dma((seq,)),
+        ]
+        + gather_sems(seq, rows),
+        compiler_params=pltpu.CompilerParams(
+            collective_id=collective_id, has_side_effects=True, vmem_limit_bytes=VMEM_MOST
+        ),
+        name="attend_back",
+        cost_estimate=cost_of(130),
+    )(
+        dz,
+        proj_weight,
+        o_head,
+        query,
+        key,
+        value,
+        raw,
+        squares,
+        gains,
+        *tables,
+        segments[:, :, None],
+        segments[:, None, :],
+    )
 
 
 def last_transfers(terms, qkv_terms, proj_terms, packed, collective_id):
@@ -848,61 +1230,6 @@
     return (factor * (scaled - values * factor * factor * inner), gain_part)
 
 
-def rotary(positions):
-    half_dim = HEAD_DIM // 2
-    freqs = jnp.exp(
-        -math.log(ROPE_BASE) * (2.0 * jnp.arange(half_dim, dtype=F32) / HEAD_DIM)
-    )
-    angles = positions.astype(F32)[:, None] * freqs[None, :]
-    return (jnp.cos(angles)[:, None, :], jnp.sin(angles)[:, None, :])
-
-
-def rotate(values, cosine, sine):
-    half_dim = values.shape[-1] // 2
-    first = values[..., :half_dim]
-    second = values[..., half_dim:]
-    return jnp.concatenate(
-        [first * cosine - second * sine, second * cosine + first * sine], axis=-1
-    )
-
-
-def attend_forward(pieces):
-    queries, key_rows, value_rows, seg_ids = pieces
-    score_scale = HEAD_DIM ** (-0.5)
-    scores = jnp.einsum("qhd,khd->hqk", queries, key_rows, preferred_element_type=F32) * score_scale
-    allowed = seg_ids[None, :] <= seg_ids[:, None]
-    scores = jnp.where(allowed[None], scores, MASKED_SCORE)
-    row_max = jnp.max(scores, axis=-1, keepdims=True)
-    exp_scores = jnp.exp(scores - row_max)
-    row_sum = jnp.sum(exp_scores, axis=-1, keepdims=True)
-    attn_probs = exp_scores / row_sum
-    attended = jnp.einsum(
-        "hqk,khd->qhd", attn_probs.astype(BF), value_rows, preferred_element_type=F32
-    )
-    return (attended.astype(BF), (row_max + jnp.log(row_sum))[..., 0])
-
-
-def attend_backward(pieces):
-    queries, key_rows, value_rows, grad_out, log_norm, seg_ids = pieces
-    score_scale = HEAD_DIM ** (-0.5)
-    scores = jnp.einsum("qhd,khd->hqk", queries, key_rows, preferred_element_type=F32) * score_scale
-    allowed = seg_ids[None, :] <= seg_ids[:, None]
-    attn_probs = jnp.where(allowed[None], jnp.exp(scores - log_norm[..., None]), 0.0)
-    grad_probs = jnp.einsum("qhd,khd->hqk", grad_out, value_rows, preferred_element_type=F32)
-    inner = jnp.sum(attn_probs * grad_probs, axis=-1, keepdims=True)
-    grad_scores = (attn_probs * (grad_probs - inner)).astype(BF)
-    grad_query = (
-        jnp.einsum("hqk,khd->qhd", grad_scores, key_rows, preferred_element_type=F32) * score_scale
-    )
-    grad_key = (
-        jnp.einsum("hqk,qhd->khd", grad_scores, queries, preferred_element_type=F32) * score_scale
-    )
-    grad_value = jnp.einsum(
-        "hqk,qhd->khd", attn_probs.astype(BF), grad_out, preferred_element_type=F32
-    )
-    return (grad_query.astype(BF), grad_key.astype(BF), grad_value.astype(BF))
-
-
 def swiglu(gate_vals, up_vals):
     return jax.nn.silu(gate_vals) * up_vals
 
@@ -923,8 +1250,7 @@
     seq, ndp = lax.axis_size("seq"), lax.axis_size("dp")
     me = lax.axis_index("seq")
     devices = seq * ndp
-    heads_here = HEADS // seq
-    cols = heads_here * HEAD_DIM
+    cols = HEADS // seq * HEAD_DIM
     tok = num_seqs * local_len
     group = tok * seq
     own_rows = attn_weight.shape[0]
@@ -934,79 +1260,54 @@
     capacity = (9 * tok * top + 8 * experts_all - 1) // (8 * experts_all)
 
     n_router, n_gain = own_rows * experts_all, 4 * own_rows
-    token_rows = tokens.reshape(tok, width)
-    x_all, qkv_got, proj_got, small_all, routes_all = first_transfers(
-        token_rows,
-        attn_weight[:, :3].reshape(own_rows, 3, seq, cols).transpose(2, 1, 0, 3),
-        attn_weight[:, 3],
-        packed_rows([router_weight.reshape(1, -1), norm_gains.reshape(1, -1)], 16)[0],
-        routes.reshape(-1, 128),
-        1,
-    )
-    expert_in, expert_out, small_all = lax.optimization_barrier((expert_in, expert_out, small_all))
+    token_rows, cot_low = tokens.reshape(tok, width), cotangent.reshape(tok, width)
+    (router_rows,) = (packed_rows([router_weight.reshape(1, -1)], 16)[0],)
+    rank = lax.axis_index("dp") * seq + me
+    gain_rows_own = lax.dynamic_update_slice(
+        jnp.zeros((16, 128), BF), norm_gains, (0, lax.rem(rank, 128 // own_rows) * own_rows)
+    )
+    tables = rotary_tables(seq_length)
+    normed_all, cot_all, qkv_weight, proj_got, small_all, routes_all, raw, query_head, key_head, value_head, o_head, sums = (
+        attend_first(
+            token_rows,
+            cot_low,
+            attn_weight[:, :3].reshape(own_rows, 3, seq, cols).transpose(2, 1, 0, 3),
+            attn_weight[:, 3],
+            jnp.concatenate([router_rows, gain_rows_own], axis=0),
+            routes.reshape(-1, 128),
+            tables,
+            segments,
+            router_rows.shape[0],
+            1,
+        )
+    )
     in_full = lax.all_gather(expert_in, "dp", axis=1, tiled=True)
     out_full = lax.all_gather(expert_out, "dp", axis=2, tiled=True)
-    small_all = small_all.reshape(devices, -1)
-    router_full = small_all[:, :n_router].reshape(width, experts_all)
+    router_full = (
+        small_all[:, : router_rows.shape[0]].reshape(devices, -1)[:, :n_router].reshape(width, experts_all)
+    )
     gain_rows = (
-        small_all[:, n_router : n_router + n_gain]
-        .reshape(devices, 4, own_rows)
+        jnp.sum(
+            small_all[:, router_rows.shape[0] : router_rows.shape[0] + 4]
+            .reshape(width // 128, 128 // own_rows, 4, 128)
+            .astype(F32),
+            axis=1,
+        )
         .transpose(1, 0, 2)
         .reshape(4, width)
-        .astype(F32)
     )
     routes_all = routes_all.reshape(seq, tok, top)
-    qkv_weight = qkv_got.transpose(2, 0, 1, 3, 4).reshape(3, width, cols)
+    normed_all = normed_all.reshape(group, width)
     proj_weight = proj_got.reshape(cols, width)
-
     resid_in = token_rows.astype(F32)
     factor_attn = rms_factor(resid_in)
-    group_in = x_all.reshape(group, width).astype(F32)
-    normed_all = (group_in * rms_factor(group_in) * gain_rows[0]).astype(BF)
-    raw = jnp.einsum("td,jde->jte", normed_all, qkv_weight, preferred_element_type=F32)
-    squares = jnp.sum(raw[:2] * raw[:2], axis=-1).reshape(1, -1, 128)
-    (sums,) = small_exchange([squares], ("seq",), 4)
-    factors = lax.rsqrt(jnp.sum(sums, axis=0).reshape(2, group, 1) / width + NORM_EPS)
-    head_gains = lax.dynamic_slice_in_dim(gain_rows, me * cols, cols, axis=1)
-
-    position = (
-        jnp.arange(seq, dtype=jnp.int32)[:, None, None] * local_len
-        + jnp.zeros((1, num_seqs, 1), jnp.int32)
-        + jnp.arange(local_len, dtype=jnp.int32)[None, None, :]
-    ).reshape(group)
-    cosine, sine = rotary(position)
-
-    def to_heads(values):
-        return values.reshape(group, heads_here, HEAD_DIM)
-
-    def by_sequence(values):
-        return (
-            values.reshape(seq, num_seqs, local_len, heads_here, HEAD_DIM)
-            .transpose(1, 0, 2, 3, 4)
-            .reshape(num_seqs, seq_length, heads_here, HEAD_DIM)
-        )
-
-    def by_source(values):
-        return (
-            values.reshape(num_seqs, seq, local_len, cols).transpose(1, 0, 2, 3).reshape(group, cols)
-        )
-
-    qn = raw[0] * factors[0] * head_gains[1]
-    kn = raw[1] * factors[1] * head_gains[2]
-    query_head = by_sequence(rotate(to_heads(qn), cosine, sine).astype(BF))
-    key_head = by_sequence(rotate(to_heads(kn), cosine, sine).astype(BF))
-    value_head = by_sequence(raw[2].astype(BF))
-    attended, log_norm = lax.map(attend_forward, (query_head, key_head, value_head, segments))
-    o_head = by_source(attended.reshape(num_seqs, seq_length, cols))
-    z_terms = jnp.dot(o_head, proj_weight, preferred_element_type=F32).astype(BF)
+    z_terms = jnp.dot(o_head.reshape(group, cols), proj_weight, preferred_element_type=F32).astype(BF)
     z = seq_reduce(z_terms.reshape(seq, tok, width), 5)
 
     middle = resid_in + z
     factor_ffn = rms_factor(middle)
     ffn_low = (middle * factor_ffn * gain_rows[3]).astype(BF)
     ffn_all = seq_gather(ffn_low, 6)
-    cot_low = cotangent.reshape(tok, width)
-    cot_all = seq_gather(cot_low, 7)
 
     logits_all = jnp.einsum("std,de->ste", ffn_all, router_full, preferred_element_type=F32)
     probs_all = jax.nn.softmax(logits_all, axis=-1)
@@ -1043,7 +1344,7 @@
         expert_res.reshape(experts, seq, capacity, width),
         preferred_element_type=F32,
     ).astype(BF)
-    mixed = seq_reduce(mixed_terms, 8)
+    mixed = lax.psum_scatter(mixed_terms, "seq", scatter_dimension=0, tiled=False).astype(F32)
     block_out = (middle + mixed).astype(BF).reshape(num_seqs, local_len, width)
 
     slot_dgate = jnp.sum(cot_rows * expert_res.astype(F32), axis=-1).reshape(experts, seq, capacity)
@@ -1083,35 +1384,27 @@
     grad_middle, gain_ffn = norm_back(middle, factor_ffn, gain_rows[3], grad_ffn)
     grad_middle = grad_middle + cot_low.astype(F32)
 
-    dz_all = seq_gather(grad_middle.astype(BF), 11).reshape(group, width)
-    grad_o = jnp.einsum("te,de->td", dz_all, proj_weight, preferred_element_type=F32).astype(BF)
-    proj_term = jnp.einsum("td,te->de", o_head, dz_all, preferred_element_type=F32).astype(BF)
-    grad_q, grad_k, grad_v = lax.map(
-        attend_backward,
-        (query_head, key_head, value_head, by_sequence(grad_o), log_norm, segments),
-    )
-    flat = (num_seqs, seq_length, cols)
-    grad_qn = rotate(to_heads(by_source(grad_q.reshape(flat)).astype(F32)), cosine, -sine).reshape(
-        group, cols
-    )
-    grad_kn = rotate(to_heads(by_source(grad_k.reshape(flat)).astype(F32)), cosine, -sine).reshape(
-        group, cols
-    )
-    grad_n = jnp.stack([grad_qn, grad_kn])
-    scaled = grad_n * head_gains[1:3, None, :]
-    inner = jnp.sum(scaled * raw[:2], axis=-1).reshape(1, -1, 128)
-    (inners,) = small_exchange([inner], ("seq",), 12)
-    inner = jnp.sum(inners, axis=0).reshape(2, group, 1) / width
-    gain_heads = jnp.sum(grad_n * raw[:2] * factors, axis=1)
-    grad_raw = factors * (scaled - raw[:2] * factors * factors * inner)
-    grad_stack = jnp.concatenate(
-        [grad_raw.astype(BF), by_source(grad_v.reshape(flat))[None]], axis=0
-    )
+    head_gains = jnp.pad(lax.dynamic_slice(gain_rows, (1, me * cols), (2, cols)), ((0, 6), (0, 0)))
+    grad_stack, proj_term, gain_heads = attend_back(
+        grad_middle.astype(BF),
+        proj_weight,
+        o_head,
+        query_head,
+        key_head,
+        value_head,
+        raw,
+        sums,
+        head_gains,
+        tables,
+        segments,
+        11,
+    )
+    grad_stack = grad_stack.reshape(3, group, cols)
     dn_terms = jnp.einsum("jte,jde->td", grad_stack, qkv_weight, preferred_element_type=F32).astype(BF)
     qkv_term = jnp.einsum("td,jte->jde", normed_all, grad_stack, preferred_element_type=F32)
     gain_attn = jnp.sum(qkv_term * qkv_weight.astype(F32), axis=(0, 2)) / gain_rows[0]
 
-    gain_heads = lax.dynamic_update_slice_in_dim(jnp.zeros((2, width), F32), gain_heads, me * cols, axis=1)
+    gain_heads = lax.dynamic_update_slice_in_dim(jnp.zeros((2, width), F32), gain_heads[:2], me * cols, axis=1)
     gain_term = jnp.concatenate([gain_attn[None], gain_heads, gain_ffn[None]], axis=0)
     gain_send = gain_term.reshape(4, devices, own_rows).transpose(1, 0, 2)
     grad_normed, qkv_out, proj_grad, total = last_transfers(

time: 1340 us -> 1170 us (0.87)
  other arithmetic: 97.6 us -> 39.1 us
  local copies, waits for them, and re-layouts: 138 us -> 79.8 us
  matrix products: 286 us -> 241 us
  waiting for transfers between devices: 1.28 us -> 23.1 us
  Pallas kernels: 790 us -> 770 us
    pallas_call x1 -> x2, Pallas kernels: 121 us -> 348 us  [the longest x1 224 us: attend_first(): pl.pallas_call(kernel, out_shape=[shape for shape, _ in outs], in_specs=[...]
    pallas_call x3 -> x1, Pallas kernels: 245 us -> 93.2 us  [seq_gather(): pl.pallas_call(kernel, out_shape=jax.ShapeDtypeStruct((seq, rows, width),...]
    pallas_call x3 -> x2, Pallas kernels: 269 us -> 191 us  [seq_reduce(): pl.pallas_call(kernel, out_shape=jax.ShapeDtypeStruct((rows, width), F32)...]
    dot_general x18 -> x1, matrix products: 62.5 us -> 8.34 us  [local(): jnp.dot(o_head.reshape(group, cols), proj_weight, preferred_element_type=...]
    convert_element_type x10 -> x2, other arithmetic: 34.1 us -> 3.55 us  [the longest x1 3.54 us: local(): grad_middle.astype(BF)]
    pallas_call x3 -> x1, Pallas kernels: 35.5 us -> 8.03 us  [small_exchange(): pl.pallas_call(kernel, out_shape=[jax.ShapeDtypeStruct((peers,) + a.shape...]
    reduce_scatter x1, waiting for transfers between devices: 0.01 us -> 22 us  [local(): lax.psum_scatter(in_term, 'dp', scatter_dimension=1, tiled=True).astype(F32)]
    convert_element_type x9 -> x0, local copies, waits for them, and re-layouts: 13.7 us -> none  [the longest x2 4.47 us: local(): by_source(grad_q.reshape(flat)).astype(F32)]
  transfers between devices with their start and end apart: 4 -> 5, of which waited for: 0 -> 1; matrix products, arithmetic and copies ran while one was open for 26% -> 26% of each run, Pallas kernels for 50% -> 66%
where the time goes in v3:
time: 1170 us
  Pallas kernels  770 us (66%)
  matrix products  241 us (21%)
  local copies, waits for them, and re-layouts  79.8 us (7%)
  other arithmetic  39.1 us (3%)
  waiting for transfers between devices  23.1 us (2%)
  between operations  14.8 us (1%)
    pallas_call x1, Pallas kernels, attend_first(): pl.pallas_call(kernel, out_shape=[shape for shape, _ in outs], in_specs=[...  224 us
    pallas_call x2, Pallas kernels, seq_reduce(): pl.pallas_call(kernel, out_shape=jax.ShapeDtypeStruct((rows, width), F32)...  191 us
    pallas_call x1, Pallas kernels, last_transfers(): pl.pallas_call(kernel, out_shape=[jax.ShapeDtypeStruct((rows, width), F32...  129 us
    pallas_call x1, Pallas kernels, attend_back(): pl.pallas_call(kernel, out_shape=[jax.ShapeDtypeStruct((3, seq, rows, col...  123 us
    pallas_call x1, Pallas kernels, seq_gather(): pl.pallas_call(kernel, out_shape=jax.ShapeDtypeStruct((seq, rows, width),...  93.2 us
    dot_general x1, matrix products, local(): jnp.einsum('erd,erjf->edjf', rows, grad_gu, preferred_element_type=F32)  35.2 us
    unnamed x56, local copies, waits for them, and re-layouts  34.1 us
    dot_general x1, matrix products, local(): jnp.einsum('erd,edjf->erjf', rows, in_full, preferred_element_type=F32)  28.8 us
  transfers between devices with their start and end apart: 5, of which 1 were waited for; matrix products, arithmetic and copies ran while one was open for 26% of the time, Pallas kernels for 66%

profile of v3, /device:TPU:0, one launch (start us, length us, event | category | flops | bytes accessed | tf_op | source)
XLA Modules:
  0.0 1167.4 jit_solution(9863509038879922219)
XLA Ops:
  7.2 9.4 copy.130
  16.7 0.7 all-gather.5.cloned.1.call-update
  17.5 0.6 broadcast_in_dim.40.refs_9_.refs_12_
  18.4 0.7 reshape.200.refs_5_
  19.8 0.9 copy.186
  20.6 1.1 reshape.238
  21.7 1.1 copy.184
  22.8 1.3 copy.123.refs_8_.refs_11_
  25.0 1.9 fusion.52
  26.9 1.3 pad_maximum_fusion.1
  28.3 224.4 %attend_first.1 = (bf16[8,256,2048]{2,1,0:T(8,128)(2,1)}, bf16[8,256,2048]{2,1,0:T(8,128)(2,1)}, bf16[3,2048,256]{2,1,0:T(8,128)(2,1)}, bf16[4,64,2048]{2,1,0:T(...) custom-call(bf16[256,2048]{1,0:T(8,128)(2,1)} %bitcast.180, ...), custom_call_target="tpu_custom_call" | custom-call | bytes 756000000 | tf_op jit(solution)/shard_map/attend_first/pallas_call | solution.py:755
  252.7 0.9 slice.43
  253.9 1.5 eq.28
  256.1 8.3 convolution_convert_fusion.2
  264.4 91.5 %seq_reduce.2 = f32[256,2048]{1,0:T(8,128)} custom-call(bf16[8,256,2048]{2,1,0:T(8,128)(2,1)} %bitcast.179), custom_call_target="tpu_custom_call" | custom-call | bytes 288000000 | tf_op jit(solution)/shard_map/seq_reduce/pallas_call | solution.py:413
  355.9 0.9 convert_reduce_fusion
  356.8 2.1 multiply_reduce_fusion.4
  359.0 1.3 fusion.63
  360.9 1.2 multiply_convert_fusion.5.x_ref
  362.1 93.2 %seq_gather.1 = bf16[8,256,2048]{2,1,0:T(8,128)(2,1)} custom-call(bf16[256,2048]{1,0:T(8,128)(2,1)} %multiply_convert_fusion.5.x_ref), custom_call_target="tpu_custom_call" | custom-call | bytes 288000000 | tf_op jit(solution)/shard_map/seq_gather/pallas_call | solution.py:231
  455.2 8.7 convert_bitcast_fusion
  463.9 9.3 copy.129
  473.2 11.3 fusion.17
  484.5 12.9 %copy.133 = f32[4,8,72,2048]{3,2,1,0:T(8,128)} copy(f32[4,8,72,2048]{3,2,0,1:T(8,128)} %fusion.17) | data formatting | bytes 37748736 | tf_op jit(solution)/shard_map/esjt,std->esjd/transpose | solution.py:1333
  497.4 6.0 fusion.64
  503.5 28.8 %fusion.66 = f32[4,576,2,1024]{3,1,2,0:T(8,128)} fusion(bf16[4,576,2048,1]{2,1,3,0:T(8,128)(2,1)} %bitcast.186, bf16[4,2048,2,1024]{3,1,2,0:T(8,128)(2,1)} %all-gather.3.cloned.1.call-done), kind=kOutput, calls=%fused_computation.121 | convolution fusion | flops 19327352832 | bytes 61865984 | tf_op jit(solution)/shard_map/erd,edjf->erjf/dot_general | solution.py:1337
  532.3 10.1 multiply_convert_fusion.2
  542.4 20.1 %multiply_reduce_fusion = (f32[4,576]{1,0:T(4,128)S(1)}, bf16[4,576,2048]{2,1,0:T(8,128)(2,1)}) fusion(f32[4,576,2048]{2,1,0:T(8,128)} %bitcast.181, bf16[4,576,1024]{2,1,0:T(8,128)(2,1)} %multiply_convert_fusion.2, bf16[4,1024,2048]{2,1,0:T(8,128)(2,1)} %all-gather.5.cloned.1.call-done), kind=kOutput, calls=%fused_computation.4 | convolution fusion | flops 9682548736 | bytes 49816576 | tf_op jit(solution)/shard_map/erf,efd->erd/dot_general | solution.py:1340
  562.6 10.5 bitcast_convert_fusion.3
  573.2 1.4 select_reduce_fusion.1
  574.8 20.4 %convolution_convert_fusion.1 = bf16[4,1024,2048]{2,1,0:T(8,128)(2,1)} fusion(bf16[4,576,1024]{2,1,0:T(8,128)(2,1)} %multiply_convert_fusion.2, f32[4,576,2048]{2,1,0:T(8,128)} %bitcast.182, f32[4,576]{1,0:T(4,128)S(1)} %mul.241), kind=kOutput, calls=%fused_computation.10 | convolution fusion | flops 9681502208 | bytes 40379392 | tf_op jit(solution)/shard_map/erf,erd->efd/dot_general | solution.py:1357
  595.1 26.3 %fusion.30 = (bf16[4,576,1,1024]{3,1,0,2:T(8,128)(2,1)}, bf16[4,576,1,1024]{3,1,0,2:T(8,128)(2,1)}) fusion(f32[4,576,2,1024]{3,1,2,0:T(8,128)} %fusion.66, bf16[4,1024,2048]{2,1,0:T(8,128)(2,1)} %all-gather.5.cloned.1.call-done, f32[4,576,2048]{2,1,0:T(8,128)} %bitcast.183, f32[4,576]{1,0:T(4,128)S(1)} %mul.241), kind=kOutput, calls=%fused_computation.40 | convolution fusion | flops 9706143744 | bytes 63972352 | tf_op jit(solution)/shard_map/erd,efd->erf/dot_general | solution.py:1353
  621.4 35.2 %convolution_convert_fusion = bf16[4,2048,2,1024]{3,1,2,0:T(8,128)(2,1)} fusion(bf16[4,576,2048,1]{2,1,3,0:T(8,128)(2,1)} %bitcast.187, bf16[4,576,1,1024]{3,1,0,2:T(8,128)(2,1)} %get-tuple-element.95, bf16[4,576,1,1024]{3,1,0,2:T(8,128)(2,1)} %get-tuple-element.94), kind=kOutput, calls=%fused_computation.2 | convolution fusion | flops 19348848640 | bytes 52428800 | tf_op jit(solution)/shard_map/erd,erjf->edjf/dot_general | solution.py:1358
  656.6 27.5 %bitcast_convert_fusion = bf16[4,576,2048]{2,1,0:T(8,128)(2,1)} fusion(bf16[4,2048,2,1024]{3,1,2,0:T(8,128)(2,1)} %all-gather.3.cloned.1.call-done, bf16[4,576,1,1024]{3,1,0,2:T(8,128)(2,1)} %get-tuple-element.95, bf16[4,576,1,1024]{3,1,0,2:T(8,128)(2,1)} %get-tuple-element.94), kind=kOutput, calls=%fused_computation.3 | convolution fusion | flops 19336790016 | bytes 52428800 | tf_op jit(solution)/shard_map/erjf,edjf->erd/dot_general | solution.py:1356
  684.9 0.8 constant_dynamic-slice_fusion
  685.7 0.6 pad.8.refs_8_
  687.1 0.6 reshape.209.refs_0_
  687.7 8.0 small_exchange.1
  695.8 0.8 reshape.210
  697.6 10.6 bitcast_convert_fusion.2.p_ref
  708.2 100.0 %seq_reduce.3 = f32[256,2048]{1,0:T(8,128)} custom-call(bf16[8,256,2048]{2,1,0:T(8,128)(2,1)} %bitcast_convert_fusion.2.p_ref), custom_call_target="tpu_custom_call" | custom-call | bytes 288000000 | tf_op jit(solution)/shard_map/seq_reduce/pallas_call | solution.py:413
  808.2 3.8 multiply_reduce_fusion.1
  812.0 3.5 fusion.61.refs_0_
  815.6 123.3 %attend_back.1 = (bf16[3,8,256,256]{3,2,1,0:T(8,128)(2,1)}, bf16[256,2048]{1,0:T(8,128)(2,1)}, f32[8,256]{1,0:T(8,128)}) custom-call(bf16[256,2048]{1,0:T(8,128)(2,1)} %fusion.61.refs_0_, bf16[256,2048]{1,0:T(8,128)(2,1)} %bitcast.191, bf16[8,256,256]{2,1,0:T(8,128)(2,1)} %get-tuple-element.29.refs_2_, bf16[2,1024,256]{2,1,0:T(8,128)(2,1)} %get-tuple-element.35.refs_3_, ...), custom_call_target="tpu_custom_call" | custom-call | bytes 468000000 | tf_op jit(solution)/shard_map/attend_back/pallas_call | solution.py:1004
  938.8 0.7 slice_dynamic-update-slice_fusion
  939.6 10.3 bitcast_convert_fusion.4
  949.9 2.1 copy.142
  952.0 1.0 copy-done.9
  953.1 0.8 fusion.22
  954.2 0.8 copy.164
  955.0 11.8 %bitcast_convert_fusion.1 = bf16[2048,2048]{1,0:T(8,128)(2,1)} fusion(bf16[3,2048,256]{2,1,0:T(8,128)(2,1)} %bitcast.213, bf16[3,2048,256]{2,1,0:T(8,128)(2,1)} %get-tuple-element.41), kind=kOutput, calls=%fused_computation.6 | convolution fusion | flops 6446645248 | bytes 14680064 | tf_op jit(solution)/shard_map/jte,jde->td/dot_general | solution.py:1403
  966.8 129.4 %last_transfers.1 = (f32[256,2048]{1,0:T(8,128)}, bf16[8,192,256]{2,1,0:T(8,128)(2,1)}, bf16[64,2048]{1,0:T(8,128)(2,1)}, f32[24,128]{1,0:T(8,128)}) custom-call(bf16[8,256,2048]{2,1,0:T(8,128)(2,1)} %bitcast.188, bf16[4,1536,256]{2,1,0:T(8,128)(2,1)} %bitcast.184, bf16[4,64,2048]{2,1,0:T(8,128)(2,1)} %bitcast.198, f32[32,24,128]{2,1,0:T(8,128)} %bitcast.197), custom_call_target="tpu_custom_call" | custom-call | bytes 360000000 | tf_op jit(solution)/shard_map/last_transfers/pallas_call | solution.py:1187
  1096.2 0.7 slice.49
  1096.9 0.7 slice.48
  1097.6 2.4 copy.185
  1100.0 2.2 reshape.222
  1102.2 0.7 reshape.224
  1102.9 0.7 copy.147
  1103.6 1.5 maximum_convert_fusion
  1105.1 2.7 copy.146
  1108.2 5.7 fusion.36
  1114.0 6.8 convert_element_type.146
  1120.7 22.0 %reduce-scatter.6.cloned.1.call-done = bf16[4,512,2,1024]{3,1,2,0:T(8,128)(2,1)} async-done(((bf16[4,2048,2,1024]{3,1,2,0:T(8,128)(2,1)}), bf16[4,512,2,1024]{3,1,2,0:T(8,128)(2,1)}) %reduce-scatter.6.cloned.1.call-update) | async-done | bytes 8388624 | tf_op jit(solution)/shard_map/reduce_scatter | solution.py:1361
  1142.7 17.7 %copy.148 = f32[4,512,2,1024]{3,2,1,0:T(2,128)} copy(bf16[4,512,2,1024]{3,1,2,0:T(8,128)(2,1)} %reduce-scatter.6.cloned.1.call-done) | data formatting | bytes 25165824
  (104 shorter events, 7.3 us)
Async XLA Ops:
  7.2 496.3 %all-gather.3.cloned.1.call-start = ((), (), s32[]{:S(2)}) async-start(), calls=%async_computation.3 | async-start | bytes 41943040 | tf_op jit(solution)/shard_map/all_gather | solution.py:1284
  16.6 0.9 copy-start.17
  16.6 1.5 copy-start.21
  16.7 1.7 copy-start.22
  16.7 2.5 copy-start.10
  16.7 7.5 copy-start.23
  16.7 525.8 %all-gather.5.cloned.1.call-start = ((), (), s32[]{:S(2)}) async-start(), calls=%async_computation.4 | async-start | bytes 20971520 | tf_op jit(solution)/shard_map/all_gather | solution.py:1285
  17.4 1090.8 %reduce-scatter.4.cloned.1.call-start = ((), (), s32[]{:S(2)}) async-start(), calls=%async_computation.5 | async-start | bytes 9437184 | tf_op jit(solution)/shard_map/reduce_scatter | solution.py:1347
  253.9 243.5 %copy-start.6 = (bf16[2048,32]{1,0:T(8,128)(2,1)}, bf16[2048,32]{1,0:T(8,128)(2,1)S(1)}, u32[]{:S(2)}) copy-start(bf16[2048,32]{1,0:T(8,128)(2,1)S(1)} %reshape_reshape.3) | copy-start | bytes 393220
  256.1 317.2 %copy-start.11 = (s32[4,8,256]{2,0,1:T(4,128)}, s32[4,8,256]{2,0,1:T(4,128)S(1)}, u32[]{:S(2)}) copy-start(s32[4,8,256]{2,0,1:T(4,128)S(1)} %copy.127) | copy-start | bytes 98308
  264.4 92.4 %copy-start.2 = (bf16[2,128,2048]{2,1,0:T(8,128)(2,1)S(1)}, bf16[2,128,2048]{2,1,0:T(8,128)(2,1)}, u32[]{:S(2)}) copy-start(bf16[2,128,2048]{2,1,0:T(8,128)(2,1)} %param.9) | copy-start | bytes 3145732
  356.8 2.1 copy-start.15
  358.9 1.3 copy-start
  358.9 1.3 copy-start.19
  360.3 0.6 copy-start.13
  573.1 540.9 %reduce-scatter.8.cloned.1.call-start = ((), (), s32[]{:S(2)}) async-start(), calls=%async_computation.7 | async-start | bytes 20971520 | tf_op jit(solution)/shard_map/reduce_scatter | solution.py:1360
  684.1 0.7 copy-start.18
  684.1 2.2 copy-start.4
  684.1 2.2 copy-start.7
  684.1 2.6 copy-start.3
  684.2 458.6 %reduce-scatter.6.cloned.1.call-start = ((), (), s32[]{:S(2)}) async-start(), calls=%async_computation.6 | async-start | bytes 41943040 | tf_op jit(solution)/shard_map/reduce_scatter | solution.py:1361
  684.7 12.8 %copy-start.12 = (s32[4,8,256]{2,0,1:T(4,128)S(1)}, s32[4,8,256]{2,0,1:T(4,128)}, u32[]{:S(2)}) copy-start(s32[4,8,256]{2,0,1:T(4,128)} %copy-done.11) | copy-start | bytes 98308
  708.1 100.0 %copy-start.1 = (f32[256,2048]{1,0:T(8,128)S(1)}, f32[256,2048]{1,0:T(8,128)}, u32[]{:S(2)}) copy-start(f32[256,2048]{1,0:T(8,128)} %copy-done) | copy-start | bytes 6291460
  708.1 100.0 %copy-start.8 = (bf16[2048,32]{1,0:T(8,128)(2,1)S(1)}, bf16[2048,32]{1,0:T(8,128)(2,1)}, u32[]{:S(2)}) copy-start(bf16[2048,32]{1,0:T(8,128)(2,1)} %copy-done.6) | copy-start | bytes 393220
  708.1 100.0 %copy-start.14 = (f32[1,16,128]{2,0,1:T(1,128)S(1)}, f32[1,16,128]{2,0,1:T(1,128)}, u32[]{:S(2)}) copy-start(f32[1,16,128]{2,0,1:T(1,128)} %copy-done.13) | copy-start | bytes 24580
  708.1 100.0 %copy-start.20 = (f32[256]{0:T(256)S(1)}, f32[256]{0:T(256)}, u32[]{:S(2)}) copy-start(f32[256]{0:T(256)} %copy-done.19) | copy-start | bytes 3076
  949.9 3.1 copy-start.9
  1096.2 11.6 copy-start.16
  1103.6 4.2 copy-start.5
Sparse Core Ops, SparseCore 0:
  16.8 230.1 all-gather.2
  248.6 110.1 all-gather.4
  573.2 165.2 reduce-scatter.3
  741.6 129.1 reduce-scatter.7
  873.3 269.3 reduce-scatter.5

commit v4 on v3

--- a/solution.py
+++ b/solution.py
@@ -241,9 +241,9 @@
 
 
 class Reduce:
-    def __init__(self, first, second, me, flat, cuts, terms, acc, out, from_first, from_second, sems):
+    def __init__(self, first, second, me, flat, cuts, terms, out, from_first, from_second, sems):
         self.first, self.second, self.me, self.flat, self.cuts = first, second, me, flat, cuts
-        self.terms, self.acc, self.out = terms, acc, out
+        self.terms, self.out = terms, out
         self.from_first, self.from_second = from_first, from_second
         self.send_sem, self.first_sem, self.second_sem = sems
         self.base = cuts[0][0]
@@ -254,7 +254,7 @@
         seq, rows, pieces = first_size * second_size, sum(r for _, r in rows_of), len(rows_of)
         lanes = 1 if first_size == 2 else 2
         return [
-            pltpu.VMEM((lanes, seq, rows, width), BF),
+            pltpu.VMEM((lanes, second_size if first_size == 2 else seq, rows, width), BF),
             pltpu.VMEM((2, second_size, rows, width), BF),
             pltpu.SemaphoreType.DMA((seq, pieces)),
             pltpu.SemaphoreType.DMA((lanes, seq, pieces)),
@@ -264,6 +264,9 @@
     def _lane(self, turn):
         return 0 if self.first.size == 2 or turn > 0 else 1
 
+    def _held(self, dest, spot):
+        return spot if self.first.size == 2 else dest
+
     def _cut(self, h):
         return pl.ds(*self.cuts[h])
 
@@ -273,7 +276,8 @@
     def _copy(self, src, dest, spot, h, line, turn):
         if line is self.first:
             lane = self._lane(turn)
-            dst, sem = self.from_first.at[lane, dest, self._inner(h)], self.first_sem.at[lane, dest, h]
+            held = self._held(dest, spot)
+            dst, sem = self.from_first.at[lane, held, self._inner(h)], self.first_sem.at[lane, dest, h]
         else:
             side = 0 if turn > 0 else 1
             dst, sem = self.from_second.at[side, spot, self._inner(h)], self.second_sem.at[side, spot, h]
@@ -325,14 +329,13 @@
             return
         behind = first.has(-turn)
         self._await(go & behind, dest, spot, h, first, turn)
-        self._add(go & behind, [self.terms.at[dest]], [self.from_first.at[self._lane(turn), dest]], self.acc.at[dest], h)
-        self._add(go & jnp.logical_not(behind), [self.terms.at[dest]], [], self.acc.at[dest], h)
-        self._send(self.acc.at[dest, self._cut(h)], dest, spot, h, first, turn, go)
+        self._add(go & behind, [self.terms.at[dest]], [self.from_first.at[self._lane(turn), dest]], self.terms.at[dest], h)
+        self._send(self.terms.at[dest, self._cut(h)], dest, spot, h, first, turn, go)
 
     def _await(self, cond, dest, spot, h, line, turn):
         @pl.when(cond)
         def _():
-            self._copy(self.acc.at[dest, self._cut(h)], dest, spot, h, line, turn).wait_recv()
+            self._copy(self.terms.at[dest, self._cut(h)], dest, spot, h, line, turn).wait_recv()
 
     def inward(self):
         for far, sign, spot, ok in self._spread():
@@ -340,12 +343,12 @@
                 yield lambda a=(far, sign, spot, ok, h): self._collect(*a)
 
     def _collect(self, far, sign, spot, ok, h):
-        first, second, acc = self.first, self.second, self.acc
+        first, second, acc = self.first, self.second, self.terms
         dest = lax.select(ok, self.flat(first.place, spot), self.me)
         for turn in (1, -1):
             self._await(ok & first.has(-turn), dest, spot, h, first, turn)
         if first.size == 2:
-            self._add(ok, [self.terms.at[dest]], [self.from_first.at[0, dest]], acc.at[dest], h)
+            self._add(ok, [self.terms.at[dest]], [self.from_first.at[0, spot]], acc.at[dest], h)
         else:
             low, high = first.has(-1), first.has(1)
             lows, highs = self.from_first.at[self._lane(1), dest], self.from_first.at[self._lane(-1), dest]
@@ -377,32 +380,31 @@
     return [entry for _, _, entry in sorted(keyed, key=lambda k: k[:2])]
 
 
-def seq_reduces(terms, acc, out, scratch):
+def seq_reduces(terms, out, scratch):
     along, across, me, flat = seq_lines()
     early, late = cuts_of(terms.shape[1], across.size)
     return [
-        Reduce(across, along, me, lambda y, z: flat(z, y), early, terms, acc, out, *scratch[0:2], scratch[2:5]),
-        Reduce(along, across, me, flat, late, terms, acc, out, *scratch[5:7], scratch[7:10]),
+        Reduce(across, along, me, lambda y, z: flat(z, y), early, terms, out, *scratch[0:2], scratch[2:5]),
+        Reduce(along, across, me, flat, late, terms, out, *scratch[5:7], scratch[7:10]),
     ]
 
 
 def reduce_scratch(seq, rows, width):
     nz, ny = grid_of(seq)
     early, late = cuts_of(rows, ny)
-    return (
-        [pltpu.VMEM((seq, rows, width), BF)]
-        + Reduce.scratch(early, ny, nz, width)
-        + Reduce.scratch(late, nz, ny, width)
-    )
+    return Reduce.scratch(early, ny, nz, width) + Reduce.scratch(late, nz, ny, width)
 
 
 def seq_reduce(terms, collective_id):
     seq, rows, width = terms.shape
 
-    def kernel(p_ref, o_ref, acc, *scratch):
+    def kernel(p_ref, o_ref, sums, load_sem, *scratch):
+        load = pltpu.make_async_copy(p_ref, sums, load_sem)
+        load.start()
         along, across, _, _ = seq_lines()
         greet_lines(along, across)
-        programs = seq_reduces(p_ref, acc, o_ref, scratch)
+        programs = seq_reduces(sums, o_ref, scratch)
+        load.wait()
         for step in woven(*[p.outward() for p in programs]):
             step()
         for step in woven(*[p.inward() for p in programs]):
@@ -413,9 +415,9 @@
     return pl.pallas_call(
         kernel,
         out_shape=jax.ShapeDtypeStruct((rows, width), F32),
-        in_specs=[pl.BlockSpec(memory_space=pltpu.VMEM)],
+        in_specs=[pl.BlockSpec(memory_space=pl.ANY)],
         out_specs=pl.BlockSpec(memory_space=pltpu.VMEM),
-        scratch_shapes=reduce_scratch(seq, rows, width),
+        scratch_shapes=[pltpu.VMEM((seq, rows, width), BF), pltpu.SemaphoreType.DMA] + reduce_scratch(seq, rows, width),
         compiler_params=pltpu.CompilerParams(
             collective_id=collective_id, has_side_effects=True, vmem_limit_bytes=VMEM_MOST
         ),
@@ -858,7 +860,83 @@
     )(*arrays)
 
 
-def attend_back(dz, proj_weight, o_head, query, key, value, raw, squares, gains, tables, segments, collective_id):
+def middle_rows(o_head, proj_weight, tokens, gain, collective_id):
+    seq, rows, cols = o_head.shape
+    width = tokens.shape[1]
+    nz, ny = grid_of(seq)
+    n_seq = 10
+
+    def kernel(*refs):
+        o_ref, w_ref, x_ref, gain_ref, middle_out, ffn_out, all_out, terms_v, own_sem = refs[:9]
+        scratch, sems = refs[9 : 9 + n_seq], refs[9 + n_seq :]
+        along, across, me, _ = seq_lines()
+        barrier = pltpu.get_barrier_semaphore()
+        count = 0
+        for line in (along, across):
+            for turn in (1, -1):
+                pl.when(line.has(turn))(
+                    lambda: pl.semaphore_signal(
+                        barrier, 1, device_id=line.device(turn), device_id_type=MESH
+                    )
+                )
+                count = count + line.has(turn).astype(jnp.int32)
+
+        def term(i, carry):
+            dest = lax.rem(i, nz) * ny + lax.rem(across.place + 1 + lax.div(i, nz), ny)
+            terms_v[dest] = jnp.dot(o_ref[dest], w_ref[...], preferred_element_type=F32).astype(BF)
+            return carry
+
+        lax.fori_loop(0, seq, term, 0)
+        pl.semaphore_wait(barrier, count)
+        reduces = seq_reduces(terms_v, middle_out, scratch)
+        for step in woven(*[p.outward() for p in reduces]):
+            step()
+        for step in woven(*[p.inward() for p in reduces]):
+            step()
+
+        def strip(i, carry):
+            at = pl.ds(pl.multiple_of(i * 16, 16), 16)
+            values = middle_out[at, :] + x_ref[at, :].astype(F32)
+            middle_out[at, :] = values
+            factor = lax.rsqrt(jnp.mean(values * values, axis=-1, keepdims=True) + NORM_EPS)
+            ffn_out[at, :] = (values * factor * gain_ref[...]).astype(BF)
+            return carry
+
+        lax.fori_loop(0, rows // 16, strip, 0)
+        own = pltpu.make_async_copy(ffn_out, all_out.at[me], own_sem)
+        own.start()
+        gathers = seq_gathers(ffn_out, all_out, sems)
+        for program in gathers:
+            program.start()
+        for program in reduces:
+            program.finish()
+        run_steps(*gathers)
+        for program in gathers:
+            program.finish()
+        own.wait()
+
+    vmem = pl.BlockSpec(memory_space=pltpu.VMEM)
+    return pl.pallas_call(
+        kernel,
+        out_shape=[
+            jax.ShapeDtypeStruct((rows, width), F32),
+            jax.ShapeDtypeStruct((rows, width), BF),
+            jax.ShapeDtypeStruct((seq, rows, width), BF),
+        ],
+        in_specs=[vmem] * 4,
+        out_specs=[vmem, vmem, pl.BlockSpec(memory_space=pl.ANY)],
+        scratch_shapes=[pltpu.VMEM((seq, rows, width), BF), pltpu.SemaphoreType.DMA]
+        + reduce_scratch(seq, rows, width)
+        + gather_sems(seq, rows),
+        compiler_params=pltpu.CompilerParams(
+            collective_id=collective_id, has_side_effects=True, vmem_limit_bytes=VMEM_MOST
+        ),
+        name="middle_rows",
+        cost_estimate=cost_of(175),
+    )(o_head, proj_weight, tokens, gain)
+
+
+def attend_back(dz, mixed_terms, proj_weight, o_head, query, key, value, raw, squares, gains, tables, segments, collective_id):
     seq = lax.axis_size("seq")
     rows, width = dz.shape
     num_seqs, length, cols = query.shape
@@ -868,12 +946,12 @@
     scale = HEAD_DIM**-0.5
 
     def kernel(*refs):
-        (dz_ref, w_ref, o_ref, q_ref, k_ref, v_ref, raw_ref, squares_ref, gains_ref) = refs[:9]
-        (cos_ref, sin_ref, col_ref, row_ref) = refs[9:13]
-        d_out, proj_out, gain_out = refs[13:16]
-        (dz_v, do_v, turned, dk_acc, dv_acc, proj_acc, factor_v, inner_v, inner_got) = refs[16:25]
-        own_sem, inner_send, inner_recv = refs[25:28]
-        sems = refs[28:]
+        (dz_ref, mixed_ref, w_ref, o_ref, q_ref, k_ref, v_ref, raw_ref, squares_ref, gains_ref) = refs[:10]
+        (cos_ref, sin_ref, col_ref, row_ref) = refs[10:14]
+        d_out, proj_out, gain_out, mixed_out = refs[14:18]
+        (dz_v, do_v, turned, dk_acc, dv_acc, proj_acc, factor_v, inner_v, inner_got, mixed_v) = refs[18:28]
+        own_sem, inner_send, inner_recv, mixed_sem = refs[28:32]
+        sems, mixed_scratch = refs[32:36], refs[36:]
         dp = lax.axis_index("dp")
         along, across, me, _ = seq_lines()
         barrier = pltpu.get_barrier_semaphore()
@@ -884,6 +962,8 @@
         pl.semaphore_wait(barrier, seq - 1)
         own = pltpu.make_async_copy(dz_ref, dz_v.at[me], own_sem)
         own.start()
+        mixed_load = pltpu.make_async_copy(mixed_ref, mixed_v, mixed_sem)
+        mixed_load.start()
         programs = seq_gathers(dz_ref, dz_v, sems)
         for program in programs:
             program.start()
@@ -891,6 +971,16 @@
         proj_acc[...] = jnp.zeros_like(proj_acc)
         own.wait()
         run_steps(*programs)
+        mixed_load.wait()
+        reduces = seq_reduces(mixed_v, mixed_out, mixed_scratch)
+        for step in woven(*[p.outward() for p in reduces]):
+            step()
+        inward = woven(*[p.inward() for p in reduces])
+        in_all = len(inward)
+
+        def move_mixed(share):
+            while inward and in_all - len(inward) < share * in_all:
+                inward.pop(0)()
 
         def project(src, carry):
             back = dot_rows(dz_v[src], w_ref[...]).astype(BF)
@@ -944,7 +1034,10 @@
                 ].astype(BF)
             return carry
 
-        lax.fori_loop(0, num_seqs * heads_here, attend, 0)
+        lax.fori_loop(0, heads_here, attend, 0)
+        move_mixed(0.3)
+        lax.fori_loop(heads_here, num_seqs * heads_here, attend, 0)
+        move_mixed(0.5)
 
         def pieces(j, src):
             spots = pl.ds(pl.multiple_of(src * local_len, local_len), local_len)
@@ -980,6 +1073,7 @@
         for step in range(1, seq):
             inner_copy(lax.rem(me + step, seq), me).start()
         inner_got[me] = inner_v[...]
+        move_mixed(0.7)
         for program in programs:
             program.finish()
         for step in range(1, seq):
@@ -998,6 +1092,9 @@
             return carry
 
         lax.fori_loop(0, seq, normalize, 0)
+        move_mixed(1.0)
+        for program in reduces:
+            program.finish()
 
     dma = pltpu.SemaphoreType.DMA
     hbm, vmem = pl.BlockSpec(memory_space=pl.ANY), pl.BlockSpec(memory_space=pltpu.VMEM)
@@ -1007,9 +1104,10 @@
             jax.ShapeDtypeStruct((3, seq, rows, cols), BF),
             jax.ShapeDtypeStruct((cols, width), BF),
             jax.ShapeDtypeStruct((8, cols), F32),
+            jax.ShapeDtypeStruct((rows, width), F32),
         ],
-        in_specs=[hbm] + [vmem] * 12,
-        out_specs=[vmem] * 3,
+        in_specs=[hbm] * 2 + [vmem] * 12,
+        out_specs=[vmem] * 4,
         scratch_shapes=[
             pltpu.VMEM((seq, rows, width), BF),
             pltpu.VMEM((num_seqs, length, cols), BF),
@@ -1020,18 +1118,22 @@
             pltpu.VMEM((2 * seq, rows), F32),
             pltpu.VMEM((2 * seq, rows), F32),
             pltpu.VMEM((seq, 2 * seq, rows), F32),
+            pltpu.VMEM((seq, rows, width), BF),
             dma,
             dma((seq,)),
             dma((seq,)),
+            dma,
         ]
-        + gather_sems(seq, rows),
+        + gather_sems(seq, rows)
+        + reduce_scratch(seq, rows, width),
         compiler_params=pltpu.CompilerParams(
             collective_id=collective_id, has_side_effects=True, vmem_limit_bytes=VMEM_MOST
         ),
         name="attend_back",
-        cost_estimate=cost_of(130),
+        cost_estimate=cost_of(180),
     )(
         dz,
+        mixed_terms,
         proj_weight,
         o_head,
         query,
@@ -1046,23 +1148,35 @@
     )
 
 
-def last_transfers(terms, qkv_terms, proj_terms, packed, collective_id):
+def last_sums(grads, normed, qkv_weight, proj_terms, router_terms, gain_heads, gain_ffn, gain_attn, collective_id):
     seq, ndp = lax.axis_size("seq"), lax.axis_size("dp")
     devices = seq * ndp
-    _, rows, width = terms.shape
-    part_rows, cols = qkv_terms.shape[1] // seq, qkv_terms.shape[2]
-    proj_rows = proj_terms.shape[1]
-    n_scratch = len(reduce_scratch(seq, rows, width))
-    n_reduce = 5
-
-    def kernel(p_ref, qkv_ref, proj_ref, packed_ref, o_ref, qkv_out, proj_out, sum_out, acc, *scratch):
-        seq_scratch, rest = scratch[: n_scratch - 1], scratch[n_scratch - 1 :]
-        qkv_acc, qkv_sum, proj_acc, proj_sum, got = rest[:5]
-        qkv_scratch, proj_scratch = rest[5 : 5 + n_reduce], rest[5 + n_reduce : 5 + 2 * n_reduce]
-        (part_send, part_recv, move_send, move_recv, small_send, small_recv, own_sem) = rest[5 + 2 * n_reduce :]
-        _, _, me, _ = seq_lines()
+    _, _, rows, cols = grads.shape
+    width = normed.shape[2]
+    nz, ny = grid_of(seq)
+    own_rows = proj_terms.shape[1]
+    part_rows = 3 * own_rows
+    n_router = router_terms.shape[1]
+    per_block = 128 // own_rows
+    n_seq = 10
+    n_dp = 5
+    block = 256
+
+    def kernel(*refs):
+        (d_ref, normed_ref, w_ref, proj_ref, router_ref, heads_ref, ffn_ref, gain_ref) = refs[:8]
+        (o_ref, qkv_out, proj_out, sum_out) = refs[8:12]
+        (terms_v, normed_v, qkv_v, qkv_sum, proj_v, proj_sum, packed_v, got, gains_v, normed_sem, proj_sem) = refs[12:23]
+        rest = refs[23:]
+        seq_scratch, rest = rest[:n_seq], rest[n_seq:]
+        qkv_scratch, proj_scratch, rest = rest[:n_dp], rest[n_dp : 2 * n_dp], rest[2 * n_dp :]
+        (part_send, part_recv, move_send, move_recv, small_send, small_recv, own_sem) = rest
+        _, across, me, _ = seq_lines()
         x_line, core_line, dp, dp_flat = dp_lines()
         rank = dp * seq + me
+        load_normed = pltpu.make_async_copy(normed_ref, normed_v, normed_sem)
+        load_normed.start()
+        load_proj = pltpu.make_async_copy(proj_ref, proj_v, proj_sem)
+        load_proj.start()
         barrier = pltpu.get_barrier_semaphore()
 
         def device(peer):
@@ -1075,11 +1189,75 @@
             return carry
 
         lax.fori_loop(1, devices, meet, 0)
+
+        def normed_term(i, carry):
+            dest = lax.rem(i, nz) * ny + lax.rem(across.place + 1 + lax.div(i, nz), ny)
+            total = dot_rows(d_ref[0, dest], w_ref[0])
+            for j in range(1, 3):
+                total = total + dot_rows(d_ref[j, dest], w_ref[j])
+            terms_v[dest] = total.astype(BF)
+            return carry
+
+        programs = seq_reduces(terms_v, o_ref, seq_scratch)
+        lax.fori_loop(0, seq - nz, normed_term, 0)
         pl.semaphore_wait(barrier, devices - 1)
-
-        programs = seq_reduces(p_ref, acc, o_ref, seq_scratch)
-
-        def over_dp(refs, total, out, buffers):
+        for step in programs[0].outward():
+            step()
+        lax.fori_loop(seq - nz, seq, normed_term, 0)
+        for step in programs[1].outward():
+            step()
+        inward = woven(*[p.inward() for p in programs])
+        in_all = len(inward)
+
+        def move_sums(share):
+            while inward and in_all - len(inward) < share * in_all:
+                inward.pop(0)()
+
+        load_normed.wait()
+        gains_v[...] = jnp.zeros_like(gains_v)
+        for j in range(2):
+            gains_v[1 + j : 2 + j, pl.ds(pl.multiple_of(me * cols, 128), cols)] = heads_ref[j : j + 1, :]
+        gains_v[3:4, :] = ffn_ref[...]
+
+        def weight_term(i, carry):
+            at = pl.ds(pl.multiple_of(i * block, block), block)
+            turned = normed_v[:, :, at].reshape(seq * rows, block).T
+            gain = jnp.zeros((block, 1), F32)
+            for j in range(3):
+                term = jnp.dot(turned, d_ref[j].reshape(seq * rows, cols), preferred_element_type=F32)
+                gain = gain + jnp.sum(term * w_ref[j, at, :].astype(F32), axis=1, keepdims=True)
+                low = term.astype(BF)
+                for piece in range(block // own_rows):
+                    owner = i * (block // own_rows) + piece
+                    spot = pl.multiple_of(lax.rem(owner, seq) * part_rows + j * own_rows, own_rows)
+                    qkv_v[lax.div(owner, seq), pl.ds(spot, own_rows), :] = low[
+                        piece * own_rows : (piece + 1) * own_rows
+                    ]
+            gains_v[0:1, at] = as_row(gain) / gain_ref[:, at]
+            return carry
+
+        blocks = width // block
+        lax.fori_loop(0, blocks // 2, weight_term, 0)
+        move_sums(0.12)
+        lax.fori_loop(blocks // 2, blocks, weight_term, 0)
+        move_sums(0.25)
+        packed_v[:, 0:n_router, :] = router_ref[...]
+        for peer in range(devices):
+            at = peer // per_block * 128
+            packed_v[peer, n_router : n_router + 8, :] = gains_v[:, at : at + 128]
+
+        def small(peer, origin):
+            return send_to(
+                packed_v.at[peer], got.at[origin], small_send.at[peer], small_recv.at[origin], device(peer)
+            )
+
+        def small_start(step, carry):
+            small(lax.rem(rank + step, devices), rank).start()
+            return carry
+
+        load_proj.wait()
+
+        def over_dp(refs, out, buffers):
             return Reduce(
                 core_line,
                 x_line,
@@ -1087,31 +1265,15 @@
                 lambda core, x: dp_flat(x, core),
                 [(0, refs.shape[1])],
                 refs,
-                total,
                 out,
                 *buffers[0:2],
                 buffers[2:5],
             )
 
-        owners = [
-            over_dp(qkv_ref, qkv_acc, qkv_sum, qkv_scratch),
-            over_dp(proj_ref, proj_acc, proj_sum, proj_scratch),
-        ]
+        owners = [over_dp(qkv_v, qkv_sum, qkv_scratch), over_dp(proj_v, proj_sum, proj_scratch)]
         for owner in owners:
             for step in owner.outward():
                 step()
-        for step in woven(*[p.outward() for p in programs]):
-            step()
-
-        def small(peer, origin):
-            return send_to(
-                packed_ref.at[peer], got.at[origin], small_send.at[peer], small_recv.at[origin], device(peer)
-            )
-
-        def small_start(step, carry):
-            small(lax.rem(rank + step, devices), rank).start()
-            return carry
-
         lax.fori_loop(1, devices, small_start, 0)
         inner = [list(owner.inward()) for owner in owners]
         for steps in inner:
@@ -1137,10 +1299,7 @@
         def move():
             return send_to(proj_sum, proj_out, move_send, move_recv, device(goal))
 
-        steps = woven(*[p.inward() for p in programs])
-        half = len(steps) // 2
-        for step in steps[:half]:
-            step()
+        move_sums(0.6)
         for owner_steps in inner:
             owner_steps[-1]()
         own_part.start()
@@ -1148,10 +1307,9 @@
             part(lax.rem(me + step, seq), me).start()
         pl.when(stays)(own_move.start)
         pl.when(jnp.logical_not(stays))(lambda: move().start())
-        for step in steps[half:]:
-            step()
-
-        got[rank] = packed_ref[rank]
+        move_sums(1.0)
+
+        got[rank] = packed_v[rank]
 
         def small_end(step, carry):
             small(lax.rem(rank + step, devices), rank).wait_send()
@@ -1179,44 +1337,293 @@
             move().wait_recv()
 
     dma = pltpu.SemaphoreType.DMA
-    vmem = pl.BlockSpec(memory_space=pltpu.VMEM)
-
-    def over_dp_scratch(array):
-        return Reduce.scratch([(0, array.shape[1])], 2, ndp // 2, array.shape[2])
-
+    hbm, vmem = pl.BlockSpec(memory_space=pl.ANY), pl.BlockSpec(memory_space=pltpu.VMEM)
     return pl.pallas_call(
         kernel,
         out_shape=[
             jax.ShapeDtypeStruct((rows, width), F32),
             jax.ShapeDtypeStruct((seq, part_rows, cols), BF),
-            jax.ShapeDtypeStruct((proj_rows, width), BF),
-            jax.ShapeDtypeStruct(packed.shape[1:], F32),
+            jax.ShapeDtypeStruct((own_rows, width), BF),
+            jax.ShapeDtypeStruct((n_router + 8, 128), F32),
         ],
-        in_specs=[vmem] * 4,
+        in_specs=[vmem, hbm, vmem, hbm] + [vmem] * 4,
         out_specs=[vmem] * 4,
-        scratch_shapes=reduce_scratch(seq, rows, width)
-        + [
-            pltpu.VMEM(qkv_terms.shape, BF),
-            pltpu.VMEM(qkv_terms.shape[1:], BF),
+        scratch_shapes=[
+            pltpu.VMEM((seq, rows, width), BF),
+            pltpu.VMEM((seq, rows, width), BF),
+            pltpu.VMEM((ndp, seq * part_rows, cols), BF),
+            pltpu.VMEM((seq * part_rows, cols), BF),
             pltpu.VMEM(proj_terms.shape, BF),
-            pltpu.VMEM(proj_terms.shape[1:], BF),
-            pltpu.VMEM(packed.shape, F32),
+            pltpu.VMEM((own_rows, width), BF),
+            pltpu.VMEM((devices, n_router + 8, 128), F32),
+            pltpu.VMEM((devices, n_router + 8, 128), F32),
+            pltpu.VMEM((8, width), F32),
+            dma,
+            dma,
         ]
-        + over_dp_scratch(qkv_terms)
-        + over_dp_scratch(proj_terms)
+        + reduce_scratch(seq, rows, width)
+        + Reduce.scratch([(0, seq * part_rows)], 2, ndp // 2, cols)
+        + Reduce.scratch([(0, own_rows)], 2, ndp // 2, width)
         + [dma((seq,)), dma((seq,)), dma, dma, dma((devices,)), dma((devices,)), dma((2,))],
         compiler_params=pltpu.CompilerParams(
             collective_id=collective_id, has_side_effects=True, vmem_limit_bytes=VMEM_MOST
         ),
-        name="last_transfers",
-        cost_estimate=cost_of(100),
-    )(terms, qkv_terms, proj_terms, packed)
+        name="last_sums",
+        cost_estimate=cost_of(110),
+    )(grads, normed, qkv_weight, proj_terms, router_terms, gain_heads, gain_ffn, gain_attn)
 
 
 def packed_rows(parts, sublanes):
     flat = jnp.concatenate(parts, axis=1)
     fill = -flat.shape[1] % (sublanes * 128)
     return jnp.pad(flat, ((0, 0), (0, fill))).reshape(flat.shape[0], -1, 128)
+
+
+def experts_dispatch(ffn_all, cot_all, routes_all, router_full, me, experts, capacity):
+    seq, rows, width = ffn_all.shape
+    experts_all, top = router_full.shape[1], routes_all.shape[2]
+
+    def kernel(me_ref, ffn_ref, cot_ref, routes_ref, router_ref, rows_out, cot_out, gate_out, slot_out, col_out):
+        first = me_ref[0] * experts
+        logits = jnp.dot(ffn_ref[0], router_ref[...], preferred_element_type=F32)
+        exps = jnp.exp(logits - jnp.max(logits, axis=-1, keepdims=True))
+        probs = exps / jnp.sum(exps, axis=-1, keepdims=True)
+        lane = lax.broadcasted_iota(jnp.int32, (rows, experts_all), 1)
+        wide_lane = lax.broadcasted_iota(jnp.int32, (rows, 128), 1)
+        hits, gates = jnp.zeros((rows, 128), F32), []
+        for e in range(experts):
+            hit = jnp.sum((routes_ref[0] == first + e).astype(F32), axis=1, keepdims=True)
+            hits = jnp.where(wide_lane == e, hit, hits)
+            gates.append(jnp.sum(jnp.where(lane == first + e, probs, 0.0), axis=1, keepdims=True))
+        below = lax.broadcasted_iota(jnp.int32, (rows, rows), 0) > lax.broadcasted_iota(
+            jnp.int32, (rows, rows), 1
+        )
+        earlier = jnp.dot(below.astype(BF), hits.astype(BF), preferred_element_type=F32)
+        slots = jnp.where(hits > 0.0, earlier, float(rows + 1))
+        slots_row = slots.T
+        number = lax.broadcasted_iota(jnp.int32, (capacity, rows), 0).astype(F32)
+        places = []
+        for e in range(experts):
+            place = slots_row[e : e + 1, :] == number
+            gate_out[e, 0] = jnp.sum(jnp.where(place, as_row(gates[e]), 0.0), axis=1, keepdims=True)
+            slot_out[0, :, e : e + 1] = slots[:, e : e + 1]
+            col_out[0, :, e : e + 1] = gates[e]
+            places.append(place.astype(BF))
+        for e in range(experts):
+            rows_out[e, 0] = jnp.dot(places[e], ffn_ref[0], preferred_element_type=F32).astype(BF)
+            cot_out[e, 0] = jnp.dot(places[e], cot_ref[0], preferred_element_type=F32).astype(BF)
+
+    def source(s, _):
+        return (s, 0, 0)
+
+    def slot(s, _):
+        return (0, s, 0, 0)
+
+    shaped = jax.ShapeDtypeStruct
+    return pl.pallas_call(
+        kernel,
+        out_shape=[
+            shaped((experts, seq, capacity, width), BF),
+            shaped((experts, seq, capacity, width), BF),
+            shaped((experts, seq, capacity, 1), F32),
+            shaped((seq, rows, experts), F32),
+            shaped((seq, rows, experts), F32),
+        ],
+        grid_spec=pltpu.PrefetchScalarGridSpec(
+            num_scalar_prefetch=1,
+            grid=(seq,),
+            in_specs=[
+                pl.BlockSpec((1, rows, width), source),
+                pl.BlockSpec((1, rows, width), source),
+                pl.BlockSpec((1, rows, top), source),
+                pl.BlockSpec((width, experts_all), lambda s, _: (0, 0)),
+            ],
+            out_specs=[
+                pl.BlockSpec((experts, 1, capacity, width), slot),
+                pl.BlockSpec((experts, 1, capacity, width), slot),
+                pl.BlockSpec((experts, 1, capacity, 1), slot),
+                pl.BlockSpec((1, rows, experts), source),
+                pl.BlockSpec((1, rows, experts), source),
+            ],
+        ),
+        compiler_params=pltpu.CompilerParams(vmem_limit_bytes=VMEM_MOST),
+        name="experts_dispatch",
+        cost_estimate=cost_of(15),
+    )(me.reshape(1), ffn_all, cot_all, routes_all, router_full)
+
+
+def experts_run(first, count, rows, cot_rows, gates, weight_in, weight_out):
+    _, slots, width = rows.shape
+    hidden_width = weight_out.shape[1]
+    step = 256
+    steps = hidden_width // step
+
+    def kernel(
+        rows_ref, cot_ref, gate_ref, in_ref, out_ref,
+        y_out, drows_out, dgate_out, in_out, outw_out,
+        gate_v, up_v, hidden_v, acc, dy_v, rows_t,
+    ):
+        phase, f = pl.program_id(1), pl.program_id(2)
+
+        def accumulate(value):
+            @pl.when(f == 0)
+            def _():
+                acc[...] = value
+
+            @pl.when(f > 0)
+            def _():
+                acc[...] += value
+
+        @pl.when(phase == 0)
+        def _():
+            @pl.when(f == 0)
+            def _():
+                rows_t[...] = rows_ref[0].T
+
+            gate = jnp.dot(rows_ref[0], in_ref[0, 0], preferred_element_type=F32)
+            up = jnp.dot(rows_ref[0], in_ref[0, 1], preferred_element_type=F32)
+            gate_v[f] = gate
+            up_v[f] = up
+            hidden = (gate / (1.0 + jnp.exp(-gate)) * up).astype(BF)
+            hidden_v[f] = hidden
+            accumulate(jnp.dot(hidden, out_ref[0], preferred_element_type=F32))
+
+            @pl.when(f == steps - 1)
+            def _():
+                result = acc[...].astype(BF)
+                y_out[0] = result
+                cot = cot_ref[0].astype(F32)
+                dgate_out[0] = jnp.sum(cot * result.astype(F32), axis=1, keepdims=True)
+                dy_v[...] = (cot * gate_ref[0]).astype(BF)
+
+        @pl.when(phase == 1)
+        def _():
+            grad = dot_rows(dy_v[...], out_ref[0])
+            gate, up = gate_v[f], up_v[f]
+            sig = 1.0 / (1.0 + jnp.exp(-gate))
+            dgate = (grad * up * sig * (1.0 + gate * (1.0 - sig))).astype(BF)
+            dup = (grad * gate * sig).astype(BF)
+            outw_out[0] = lax.dot_general(
+                hidden_v[f], dy_v[...], (((0,), (0,)), ((), ())), preferred_element_type=F32
+            ).astype(BF)
+            in_out[0, 0] = jnp.dot(rows_t[...], dgate, preferred_element_type=F32).astype(BF)
+            in_out[0, 1] = jnp.dot(rows_t[...], dup, preferred_element_type=F32).astype(BF)
+            accumulate(dot_rows(dgate, in_ref[0, 0]) + dot_rows(dup, in_ref[0, 1]))
+
+            @pl.when(f == steps - 1)
+            def _():
+                drows_out[0] = acc[...].astype(BF)
+
+    shaped = jax.ShapeDtypeStruct
+    by_expert = pl.BlockSpec((1, slots, width), lambda e, p, f: (first + e, 0, 0))
+    whole = pl.BlockSpec((1, slots, width), lambda e, p, f: (e, 0, 0))
+    flops = 18 * count * slots * width * hidden_width
+    return pl.pallas_call(
+        kernel,
+        grid=(count, 2, steps),
+        out_shape=[
+            shaped((count, slots, width), BF),
+            shaped((count, slots, width), BF),
+            shaped((count, slots, 1), F32),
+            shaped((count, 2, width, hidden_width), BF),
+            shaped((count, hidden_width, width), BF),
+        ],
+        in_specs=[
+            by_expert,
+            by_expert,
+            pl.BlockSpec((1, slots, 1), lambda e, p, f: (first + e, 0, 0)),
+            pl.BlockSpec((1, 2, width, step), lambda e, p, f: (first + e, 0, 0, f)),
+            pl.BlockSpec((1, step, width), lambda e, p, f: (first + e, f, 0)),
+        ],
+        out_specs=[
+            whole,
+            whole,
+            pl.BlockSpec((1, slots, 1), lambda e, p, f: (e, 0, 0)),
+            pl.BlockSpec((1, 2, width, step), lambda e, p, f: (e, 0, 0, f * p)),
+            pl.BlockSpec((1, step, width), lambda e, p, f: (e, f * p, 0)),
+        ],
+        scratch_shapes=[
+            pltpu.VMEM((steps, slots, step), F32),
+            pltpu.VMEM((steps, slots, step), F32),
+            pltpu.VMEM((steps, slots, step), BF),
+            pltpu.VMEM((slots, width), F32),
+            pltpu.VMEM((slots, width), BF),
+            pltpu.VMEM((width, slots), BF),
+        ],
+        compiler_params=pltpu.CompilerParams(vmem_limit_bytes=VMEM_MOST),
+        name="experts_run",
+        cost_estimate=pl.CostEstimate(
+            flops=flops, bytes_accessed=50_000_000, transcendentals=2 * count * slots * hidden_width
+        ),
+    )(rows, cot_rows, gates, weight_in, weight_out)
+
+
+def experts_combine(outputs, drows, dgates, slot_cols, gate_cols, capacity):
+    seq, rows, experts = slot_cols.shape
+    parts = len(outputs)
+    per = experts // parts
+    width = outputs[0].shape[-1]
+
+    def kernel(*refs):
+        y_refs, d_refs, g_refs = refs[:parts], refs[parts : 2 * parts], refs[2 * parts : 3 * parts]
+        slot_ref, gate_ref, mixed_out, dffn_out, dprob_out, y_v, d_v = refs[3 * parts :]
+        slots = slot_ref[0]
+        number = lax.broadcasted_iota(jnp.int32, (rows, capacity), 1).astype(F32)
+        number_rows = lax.broadcasted_iota(jnp.int32, (capacity, rows), 0).astype(F32)
+        gated, plain = [], []
+        for e in range(experts):
+            part, at = e // per, e % per
+            place = slots[:, e : e + 1] == number
+            gated.append(jnp.where(place, gate_ref[0, :, e : e + 1], 0.0).astype(BF))
+            plain.append(place.astype(BF))
+            cut = slice(e * capacity, (e + 1) * capacity)
+            y_v[cut, :] = y_refs[part][at, 0]
+            d_v[cut, :] = d_refs[part][at, 0]
+            across = as_row(slots[:, e : e + 1]) == number_rows
+            dprob_out[0, e : e + 1, :] = jnp.sum(
+                jnp.where(across, g_refs[part][at, 0], 0.0), axis=0, keepdims=True
+            )
+        mixed_out[0] = jnp.dot(
+            jnp.concatenate(gated, axis=1), y_v[...], preferred_element_type=F32
+        ).astype(BF)
+        dffn_out[0] = jnp.dot(
+            jnp.concatenate(plain, axis=1), d_v[...], preferred_element_type=F32
+        ).astype(BF)
+
+    def source(s):
+        return (s, 0, 0)
+
+    slot_rows = pl.BlockSpec((per, 1, capacity, width), lambda s: (0, s, 0, 0))
+    slot_ones = pl.BlockSpec((per, 1, capacity, 1), lambda s: (0, s, 0, 0))
+
+    def split(arrays):
+        return [a.reshape(per, seq, capacity, a.shape[-1]) for a in arrays]
+
+    shaped = jax.ShapeDtypeStruct
+    return pl.pallas_call(
+        kernel,
+        grid=(seq,),
+        out_shape=[
+            shaped((seq, rows, width), BF),
+            shaped((seq, rows, width), BF),
+            shaped((seq, experts, rows), F32),
+        ],
+        in_specs=[slot_rows] * (2 * parts)
+        + [slot_ones] * parts
+        + [pl.BlockSpec((1, rows, experts), source)] * 2,
+        out_specs=[
+            pl.BlockSpec((1, rows, width), source),
+            pl.BlockSpec((1, rows, width), source),
+            pl.BlockSpec((1, experts, rows), source),
+        ],
+        scratch_shapes=[
+            pltpu.VMEM((experts * capacity, width), BF),
+            pltpu.VMEM((experts * capacity, width), BF),
+        ],
+        compiler_params=pltpu.CompilerParams(vmem_limit_bytes=VMEM_MOST),
+        name="experts_combine",
+        cost_estimate=cost_of(15),
+    )(*split(outputs), *split(drows), *split(dgates), slot_cols, gate_cols)
 
 
 def rms_factor(values):
@@ -1228,10 +1635,6 @@
     gain_part = jnp.sum(incoming * values * factor, axis=0)
     inner = jnp.mean(scaled * values, axis=-1, keepdims=True)
     return (factor * (scaled - values * factor * factor * inner), gain_part)
-
-
-def swiglu(gate_vals, up_vals):
-    return jax.nn.silu(gate_vals) * up_vals
 
 
 def local(
@@ -1259,7 +1662,7 @@
     top = routes.shape[-1]
     capacity = (9 * tok * top + 8 * experts_all - 1) // (8 * experts_all)
 
-    n_router, n_gain = own_rows * experts_all, 4 * own_rows
+    n_router = own_rows * experts_all
     token_rows, cot_low = tokens.reshape(tok, width), cotangent.reshape(tok, width)
     (router_rows,) = (packed_rows([router_weight.reshape(1, -1)], 16)[0],)
     rank = lax.axis_index("dp") * seq + me
@@ -1297,77 +1700,38 @@
         .reshape(4, width)
     )
     routes_all = routes_all.reshape(seq, tok, top)
-    normed_all = normed_all.reshape(group, width)
     proj_weight = proj_got.reshape(cols, width)
     resid_in = token_rows.astype(F32)
     factor_attn = rms_factor(resid_in)
-    z_terms = jnp.dot(o_head.reshape(group, cols), proj_weight, preferred_element_type=F32).astype(BF)
-    z = seq_reduce(z_terms.reshape(seq, tok, width), 5)
-
-    middle = resid_in + z
+    middle, ffn_low, ffn_all = middle_rows(o_head, proj_weight, token_rows, gain_rows[3:4], 5)
     factor_ffn = rms_factor(middle)
-    ffn_low = (middle * factor_ffn * gain_rows[3]).astype(BF)
-    ffn_all = seq_gather(ffn_low, 6)
-
-    logits_all = jnp.einsum("std,de->ste", ffn_all, router_full, preferred_element_type=F32)
-    probs_all = jax.nn.softmax(logits_all, axis=-1)
-    here = me * experts + jnp.arange(experts, dtype=jnp.int32)
-    hits = jnp.any(routes_all[:, :, :, None] == here, axis=2)
-    token_ids = jnp.arange(tok, dtype=jnp.int32)
-    earlier = (token_ids[:, None] > token_ids[None, :]).astype(BF)
-    slot = jnp.einsum("tu,sue->ste", earlier, hits.astype(BF), preferred_element_type=F32)
-    slot = jnp.where(hits, slot, float(tok + 1)).astype(jnp.int32)
-    place = slot.transpose(2, 0, 1)[:, :, None, :] == jnp.arange(capacity, dtype=jnp.int32)[
-        None, None, :, None
+
+    slots = seq * capacity
+    rows, cot_rows, gates, slot_cols, gate_cols = experts_dispatch(
+        ffn_all, cot_all, routes_all, router_full, me, experts, capacity
+    )
+    rows, cot_rows = rows.reshape(experts, slots, width), cot_rows.reshape(experts, slots, width)
+    gates = gates.reshape(experts, slots, 1)
+    halves = 1
+    count = experts // halves
+    runs = [
+        experts_run(half * count, count, rows, cot_rows, gates, in_full.transpose(0, 2, 1, 3), out_full)
+        for half in range(halves)
     ]
-    place_low = place.astype(BF)
-    probs_here = lax.dynamic_slice_in_dim(probs_all, me * experts, experts, axis=2).transpose(2, 0, 1)
-    place_gate = jnp.where(place, probs_here[:, :, None, :], 0.0)
-    slot_gate = jnp.sum(place_gate, axis=-1)
-    slots = seq * capacity
-    rows = (
-        jnp.einsum("esjt,std->esjd", place_low, ffn_all, preferred_element_type=F32)
-        .astype(BF)
-        .reshape(experts, slots, width)
+    in_grads = [
+        lax.psum_scatter(run[3].transpose(0, 2, 1, 3), "dp", scatter_dimension=1, tiled=True) for run in runs
+    ]
+    out_grads = [
+        lax.psum_scatter(run[4], "dp", scatter_dimension=2, tiled=True) for run in runs
+    ]
+    expert_in_grad = jnp.concatenate(in_grads).astype(F32)
+    expert_out_grad = jnp.concatenate(out_grads).astype(F32)
+    mixed_terms, dffn_terms, grad_prob_here = experts_combine(
+        [run[0] for run in runs], [run[1] for run in runs], [run[2] for run in runs], slot_cols, gate_cols, capacity
     )
-    cot_rows = jnp.einsum("esjt,std->esjd", place_low, cot_all, preferred_element_type=F32).reshape(
-        experts, slots, width
-    )
-
-    gate_up = jnp.einsum("erd,edjf->erjf", rows, in_full, preferred_element_type=F32)
-    hidden_f, swiglu_pull = jax.vjp(swiglu, gate_up[:, :, 0], gate_up[:, :, 1])
-    hidden = hidden_f.astype(BF)
-    expert_res = jnp.einsum("erf,efd->erd", hidden, out_full, preferred_element_type=F32).astype(BF)
-    mixed_terms = jnp.einsum(
-        "esjt,esjd->std",
-        place_gate.astype(BF),
-        expert_res.reshape(experts, seq, capacity, width),
-        preferred_element_type=F32,
-    ).astype(BF)
-    mixed = lax.psum_scatter(mixed_terms, "seq", scatter_dimension=0, tiled=False).astype(F32)
-    block_out = (middle + mixed).astype(BF).reshape(num_seqs, local_len, width)
-
-    slot_dgate = jnp.sum(cot_rows * expert_res.astype(F32), axis=-1).reshape(experts, seq, capacity)
-    grad_prob_here = jnp.sum(jnp.where(place, slot_dgate[..., None], 0.0), axis=2)
-    grad_res = (cot_rows * slot_gate.reshape(experts, slots, 1)).astype(BF)
-    grad_hidden = jnp.einsum("erd,efd->erf", grad_res, out_full, preferred_element_type=F32)
-    grad_gatev, grad_upv = swiglu_pull(grad_hidden)
-    grad_gu = jnp.stack([grad_gatev, grad_upv], axis=2).astype(BF)
-    grad_rows = jnp.einsum("erjf,edjf->erd", grad_gu, in_full, preferred_element_type=F32).astype(BF)
-    out_term = jnp.einsum("erf,erd->efd", hidden, grad_res, preferred_element_type=F32).astype(BF)
-    in_term = jnp.einsum("erd,erjf->edjf", rows, grad_gu, preferred_element_type=F32).astype(BF)
-    out_term, in_term, grad_rows = lax.optimization_barrier((out_term, in_term, grad_rows))
-    expert_out_grad = lax.psum_scatter(out_term, "dp", scatter_dimension=2, tiled=True).astype(F32)
-    expert_in_grad = lax.psum_scatter(in_term, "dp", scatter_dimension=1, tiled=True).astype(F32)
-    dffn_terms = jnp.einsum(
-        "esjt,esjd->std",
-        place_low,
-        grad_rows.reshape(experts, seq, capacity, width),
-        preferred_element_type=F32,
-    ).astype(BF)
     grad_ffn = seq_reduce(dffn_terms, 9)
     (grad_prob,) = small_exchange(
-        [grad_prob_here.transpose(1, 0, 2).reshape(seq, -1, 128)], ("seq",), 10
+        [grad_prob_here.reshape(seq, -1, 128)], ("seq",), 10
     )
     grad_prob = grad_prob.reshape(experts_all, tok).T
 
@@ -1385,8 +1749,9 @@
     grad_middle = grad_middle + cot_low.astype(F32)
 
     head_gains = jnp.pad(lax.dynamic_slice(gain_rows, (1, me * cols), (2, cols)), ((0, 6), (0, 0)))
-    grad_stack, proj_term, gain_heads = attend_back(
+    grad_heads, proj_term, gain_heads, mixed = attend_back(
         grad_middle.astype(BF),
+        mixed_terms,
         proj_weight,
         o_head,
         query_head,
@@ -1399,31 +1764,28 @@
         segments,
         11,
     )
-    grad_stack = grad_stack.reshape(3, group, cols)
-    dn_terms = jnp.einsum("jte,jde->td", grad_stack, qkv_weight, preferred_element_type=F32).astype(BF)
-    qkv_term = jnp.einsum("td,jte->jde", normed_all, grad_stack, preferred_element_type=F32)
-    gain_attn = jnp.sum(qkv_term * qkv_weight.astype(F32), axis=(0, 2)) / gain_rows[0]
-
-    gain_heads = lax.dynamic_update_slice_in_dim(jnp.zeros((2, width), F32), gain_heads[:2], me * cols, axis=1)
-    gain_term = jnp.concatenate([gain_attn[None], gain_heads, gain_ffn[None]], axis=0)
-    gain_send = gain_term.reshape(4, devices, own_rows).transpose(1, 0, 2)
-    grad_normed, qkv_out, proj_grad, total = last_transfers(
-        dn_terms.reshape(seq, tok, width),
-        qkv_term.astype(BF)
-        .reshape(3, ndp, seq, own_rows, cols)
-        .transpose(1, 2, 0, 3, 4)
-        .reshape(ndp, seq * 3 * own_rows, cols),
+    block_out = (middle + mixed).astype(BF).reshape(num_seqs, local_len, width)
+
+    grad_normed, qkv_out, proj_grad, total = last_sums(
+        grad_heads,
+        normed_all,
+        qkv_weight,
         proj_term.reshape(ndp, own_rows, width),
-        packed_rows([router_term.reshape(devices, -1), gain_send.reshape(devices, -1)], 8),
+        packed_rows([router_term.reshape(devices, -1)], 8),
+        gain_heads,
+        gain_ffn[None],
+        gain_rows[0:1],
         14,
     )
     grad_resid, _ = norm_back(resid_in, factor_attn, gain_rows[0], grad_normed)
     input_grad = (grad_resid + grad_middle).reshape(num_seqs, local_len, width)
     qkv_grad = qkv_out.reshape(seq, 3, own_rows, cols).transpose(2, 1, 0, 3).reshape(own_rows, 3, width)
     attn_grad = jnp.concatenate([qkv_grad, proj_grad[:, None, :]], axis=1).astype(F32)
-    total = total.reshape(-1)
-    router_grad = total[:n_router].reshape(own_rows, experts_all)
-    gain_grad = total[n_router : n_router + n_gain].reshape(4, own_rows)
+    gain_at = total.shape[0] - 8
+    router_grad = total[:gain_at].reshape(-1)[:n_router].reshape(own_rows, experts_all)
+    gain_grad = lax.dynamic_slice(
+        total, (gain_at, lax.rem(rank, 128 // own_rows) * own_rows), (4, own_rows)
+    )
     return (
         block_out,
         input_grad,

time: 1170 us -> 1100 us (0.940)
  matrix products: 241 us -> 7.77 us
  Pallas kernels: 770 us -> 1000 us
  local copies, waits for them, and re-layouts: 79.8 us -> 53 us
  waiting for transfers between devices: 23.1 us -> 1.24 us
  other arithmetic: 39.1 us -> 22.5 us
    pallas_call x2 -> x5, Pallas kernels: 223 us -> 513 us  [the longest x1 175 us: middle_rows(): pl.pallas_call(kernel, out_shape=[jax.ShapeDtypeStruct((rows, width), F32...]
    dot_general x15 -> x0, matrix products: 236 us -> none  [the longest x1 35.2 us: local(): jnp.einsum('erd,erjf->edjf', rows, grad_gu, preferred_element_type=F32)]
    pallas_call x2 -> x1, Pallas kernels: 191 us -> 82.8 us  [seq_reduce(): pl.pallas_call(kernel, out_shape=jax.ShapeDtypeStruct((rows, width), F32)...]
    pallas_call x1, Pallas kernels: 123 us -> 175 us  [attend_back(): pl.pallas_call(kernel, out_shape=[jax.ShapeDtypeStruct((3, seq, rows, col...]
    reduce_scatter x3 -> x2, waiting for transfers between devices: 22 us -> 0.01 us  [the longest x1 0.01 us: local(): lax.psum_scatter(run[4], 'dp', scatter_dimension=2, tiled=True)]
    transpose x2 -> x0, local copies, waits for them, and re-layouts: 13 us -> none  [the longest x1 12.9 us: local(): jnp.einsum('esjt,std->esjd', place_low, cot_all, preferred_element_type=F32)]
    pallas_call x1, Pallas kernels: 224 us -> 212 us  [attend_first(): pl.pallas_call(kernel, out_shape=[shape for shape, _ in outs], in_specs=[...]
    unnamed x56 -> x35, local copies, waits for them, and re-layouts: 34.1 us -> 32.8 us
  transfers between devices with their start and end apart: 5 -> 4, of which waited for: 1 -> 0; matrix products, arithmetic and copies ran while one was open for 26% -> 6% of each run, Pallas kernels for 66% -> 78%
where the time goes in v4:
time: 1100 us
  Pallas kernels  1000 us (91%)
  local copies, waits for them, and re-layouts  53 us (5%)
  other arithmetic  22.5 us (2%)
  between operations  14.3 us (1%)
    pallas_call x1, Pallas kernels, attend_first(): pl.pallas_call(kernel, out_shape=[shape for shape, _ in outs], in_specs=[...  212 us
    pallas_call x1, Pallas kernels, middle_rows(): pl.pallas_call(kernel, out_shape=[jax.ShapeDtypeStruct((rows, width), F32...  175 us
    pallas_call x1, Pallas kernels, attend_back(): pl.pallas_call(kernel, out_shape=[jax.ShapeDtypeStruct((3, seq, rows, col...  175 us
    pallas_call x1, Pallas kernels, last_sums(): pl.pallas_call(kernel, out_shape=[jax.ShapeDtypeStruct((rows, width), F32...  157 us
    pallas_call x1, Pallas kernels, experts_run(): pl.pallas_call(kernel, grid=(count, 2, steps), out_shape=[shaped((count,...  140 us
    pallas_call x1, Pallas kernels, seq_reduce(): pl.pallas_call(kernel, out_shape=jax.ShapeDtypeStruct((rows, width), F32)...  82.8 us
    unnamed x35, local copies, waits for them, and re-layouts  32.8 us
    pallas_call x1, Pallas kernels, experts_dispatch(): pl.pallas_call(kernel, out_shape=[shaped((experts, seq, capacity, width),...  22.5 us
  transfers between devices with their start and end apart: 4, of which 0 were waited for; matrix products, arithmetic and copies ran while one was open for 6% of the time, Pallas kernels for 78%

profile of v4, /device:TPU:0, one launch (start us, length us, event | category | flops | bytes accessed | tf_op | source)
XLA Modules:
  0.0 1099.5 jit_solution(2755039921877758357)
XLA Ops:
  7.2 0.0 all-gather.5.cloned.1.call-start
  7.2 0.7 all-gather.5.cloned.1.call-update
  7.9 0.0 all-gather.3.cloned.1.call-start
  7.9 9.5 copy.44
  17.4 0.0 all-gather.3.cloned.1.call-update
  17.4 0.2 reduce-scatter.5.cloned.1.call-start
  17.7 1.1 copy-done.6
  18.8 0.6 slice.30
  19.4 0.0 copy-start.11
  19.4 0.0 copy-start.12
  19.4 0.9 reshape.159
  20.4 0.0 copy-start.13
  20.4 1.1 copy.58
  21.4 0.9 copy.60
  22.3 0.1 copy.41
  22.4 0.1 squeeze_reshape.3
  22.5 0.1 copy.42
  22.6 0.7 reshape.139.refs_5_
  23.4 0.6 broadcast_in_dim.12.refs_9_.refs_13_
  24.0 1.3 copy.43.refs_8_.refs_12_
  25.3 0.3 dynamic_update_slice.3
  25.6 0.6 pad_maximum_fusion.2.refs_4_
  26.2 1.9 fusion.6
  28.1 1.3 pad_maximum_fusion
  29.4 212.2 %attend_first.1 = (bf16[8,256,2048]{2,1,0:T(8,128)(2,1)}, bf16[8,256,2048]{2,1,0:T(8,128)(2,1)}, bf16[3,2048,256]{2,1,0:T(8,128)(2,1)}, bf16[4,64,2048]{2,1,0:T(...) custom-call(bf16[256,2048]{1,0:T(8,128)(2,1)} %bitcast.70, ...), custom_call_target="tpu_custom_call" | custom-call | bytes 756000000 | tf_op jit(solution)/shard_map/attend_first/pallas_call | solution.py:757
  241.6 2.4 reshape.142.routes_ref
  244.0 0.9 slice.34
  244.9 1.0 reshape_reshape.6.router_ref
  246.0 0.9 convert_reduce_fusion
  246.9 0.6 fusion.13
  247.5 175.2 %middle_rows.1 = (f32[256,2048]{1,0:T(8,128)}, bf16[256,2048]{1,0:T(8,128)(2,1)}, bf16[8,256,2048]{2,1,0:T(8,128)(2,1)}) custom-call(bf16[8,256,256]{2,1,0:T(8,128)(2,1)} %get-tuple-element.43.refs_0_.refs_3_, bf16[256,2048]{1,0:T(8,128)(2,1)} %bitcast.75, bf16[256,2048]{1,0:T(8,128)(2,1)} %bitcast.71, f32[1,2048]{1,0:T(1,128)} %get-tuple-element.105.refs_3_), custom_call_target="tpu_custom_call" | custom-call | bytes 630000000 | tf_op jit(solution)/shard_map/middle_rows/pallas_call | solution.py:919
  422.7 22.5 %experts_dispatch.1 = (bf16[4,8,72,2048]{3,2,1,0:T(8,128)(2,1)}, bf16[4,8,72,2048]{3,2,1,0:T(8,128)(2,1)}, f32[4,8,72,1]{3,2,1,0:T(8,128)}, f32[8,256,4]{2,1,0:T(8,128)}, f32[8,256,4]{2,1,0:T(8,128)}) custom-call(s32[1]{0:T(128)} %bitcast.9.me_ref, bf16[8,256,2048]{2,1,0:T(8,128)(2,1)} %get-tuple-element.47.ffn_ref, ...), custom_call_target="tpu_custom_call" | custom-call | bytes 54000000 | tf_op jit(solution)/shard_map/experts_dispatch/pallas_call | solution.py:1423
  445.2 0.0 all-gather.3.cloned.1.call-done
  445.2 140.2 %experts_run.1 = (bf16[4,576,2048]{2,1,0:T(8,128)(2,1)}, bf16[4,576,2048]{2,1,0:T(8,128)(2,1)}, f32[4,576,1]{2,1,0:T(8,128)}, bf16[4,2,2048,1024]{3,2,1,0:T(8,128)(2,1)}, bf16[4,1024,2048]{2,1,0:T(8,128)(2,1)}) custom-call(bf16[4,576,2048]{2,1,0:T(8,128)(2,1)} %bitcast.97, bf16[4,576,2048]{2,1,0:T(8,128)(2,1)} %bitcast.98, f32[4,576,1]{2,1,0:T(8,128)} %bitcast.99, ...), custom_call_target="tpu_custom_call" | custom-call | flops 86973087744 | bytes 50000000 | tf_op jit(solution)/shard_map/experts_run/pallas_call | solution.py:1521
  585.4 0.0 reduce-scatter.5.cloned.1.call-update
  585.5 0.0 reduce-scatter.3.cloned.1.call-start
  585.5 0.5 reduce-scatter.3.cloned.1.call-update
  586.1 0.1 constant_dynamic-slice_fusion.1
  586.1 0.6 pad.4.refs_9_
  586.7 1.8 fusion.14
  588.6 0.3 multiply_reduce_fusion.1
  588.9 0.2 multiply_reduce_fusion.3
  589.1 17.8 %experts_combine.1 = (bf16[8,256,2048]{2,1,0:T(8,128)(2,1)}, bf16[8,256,2048]{2,1,0:T(8,128)(2,1)}, f32[8,4,256]{2,1,0:T(4,128)}) custom-call(bf16[4,8,72,2048]{3,2,1,0:T(8,128)(2,1)} %bitcast.73, bf16[4,8,72,2048]{3,2,1,0:T(8,128)(2,1)} %bitcast.74, f32[4,8,72,1]{3,2,1,0:T(8,128)} %bitcast.81, f32[8,256,4]{2,1,0:T(8,128)} %get-tuple-element.56.refs_3_, ...), custom_call_target="tpu_custom_call" | custom-call | bytes 54000000 | tf_op jit(solution)/shard_map/experts_combine/pallas_call | solution.py:1603
  606.9 82.8 %seq_reduce.1 = f32[256,2048]{1,0:T(8,128)} custom-call(bf16[8,256,2048]{2,1,0:T(8,128)(2,1)} %get-tuple-element.58.p_ref), custom_call_target="tpu_custom_call" | custom-call | bytes 288000000 | tf_op jit(solution)/shard_map/seq_reduce/pallas_call | solution.py:415
  689.7 0.6 reshape.149.refs_0_
  690.4 17.3 %small_exchange.1 = f32[8,8,128]{2,1,0:T(8,128)} custom-call(f32[8,8,128]{2,1,0:T(8,128)} %reshape.149.refs_0_), custom_call_target="tpu_custom_call" | custom-call | bytes 28800000 | tf_op jit(solution)/shard_map/small_exchange/pallas_call | solution.py:848
  707.7 0.8 reshape.150
  708.5 2.7 fusion.15
  711.2 2.2 reshape.154.refs_4_
  713.4 3.3 multiply_reduce_fusion
  716.7 1.7 fusion.12.refs_0_
  718.4 175.1 %attend_back.1 = (bf16[3,8,256,256]{3,2,1,0:T(8,128)(2,1)}, bf16[256,2048]{1,0:T(8,128)(2,1)}, f32[8,256]{1,0:T(8,128)}, f32[256,2048]{1,0:T(8,128)}) custom-call(bf16[256,2048]{1,0:T(8,128)(2,1)} %fusion.12.refs_0_, bf16[8,256,2048]{2,1,0:T(8,128)(2,1)} %get-tuple-element.61.refs_1_, bf16[256,2048]{1,0:T(8,128)(2,1)} %bitcast.76, ...), custom_call_target="tpu_custom_call" | custom-call | bytes 648000000 | tf_op jit(solution)/shard_map/attend_back/pallas_call | solution.py:1101
  893.5 157.2 %last_sums.1 = (f32[256,2048]{1,0:T(8,128)}, bf16[8,192,256]{2,1,0:T(8,128)(2,1)}, bf16[64,2048]{1,0:T(8,128)(2,1)}, f32[24,128]{1,0:T(8,128)}) custom-call(bf16[3,8,256,256]{3,2,1,0:T(8,128)(2,1)} %get-tuple-element.68.refs_0_, bf16[8,256,2048]{2,1,0:T(8,128)(2,1)} %get-tuple-element.69.refs_1_, bf16[3,2048,256]{2,1,0:T(8,128)(2,1)} %get-tuple-element.70.refs_2_, ...), custom_call_target="tpu_custom_call" | custom-call | bytes 396000000 | tf_op jit(solution)/shard_map/last_sums/pallas_call | solution.py:1341
  1050.7 2.5 copy.59
  1053.2 2.2 reshape.157
  1055.4 1.3 maximum_convert_fusion
  1056.7 2.7 copy.48
  1059.3 0.1 reshape_reshape.7
  1059.4 0.7 copy.49
  1060.1 0.6 constant_dynamic-slice_fusion
  1060.8 2.2 fusion.5
  1063.0 5.2 fusion.4
  1068.2 6.8 convert_element_type.59
  1075.0 17.7 %copy.50 = f32[4,512,2,1024]{3,2,1,0:T(2,128)} copy(bf16[4,512,2,1024]{3,1,2,0:T(8,128)(2,1)} %reduce-scatter.3.cloned.1.call-done) | data formatting | bytes 25165824
  (38 shorter events, 0.2 us)
Async XLA Ops:
  7.2 438.1 %all-gather.5.cloned.1.call-start = ((), (), s32[]{:S(2)}) async-start(), calls=%async_computation.3 | async-start | bytes 20971520 | tf_op jit(solution)/shard_map/all_gather | solution.py:1688
  7.9 437.3 %all-gather.3.cloned.1.call-start = ((), (), s32[]{:S(2)}) async-start(), calls=%async_computation.2 | async-start | bytes 41943040 | tf_op jit(solution)/shard_map/all_gather | solution.py:1687
  17.4 1.4 copy-start.6
  17.4 1050.8 %reduce-scatter.5.cloned.1.call-start = ((), (), s32[]{:S(2)}) async-start(), calls=%async_computation.5 | async-start | bytes 20971520 | tf_op jit(solution)/shard_map/reduce_scatter | solution.py:1725
  19.4 2.9 copy-start.11
  19.4 3.1 copy-start.12
  19.4 3.9 copy-start.8
  20.4 4.9 copy-start.13
  585.5 489.6 %reduce-scatter.3.cloned.1.call-start = ((), (), s32[]{:S(2)}) async-start(), calls=%async_computation.4 | async-start | bytes 41943040 | tf_op jit(solution)/shard_map/reduce_scatter | solution.py:1722
  585.5 3.1 copy-start.1
  586.0 2.8 copy-start
  606.9 82.8 %copy-start.9 = (f32[8,4,256]{2,1,0:T(4,128)S(1)}, f32[8,4,256]{2,1,0:T(4,128)}, u32[]{:S(2)}) copy-start(f32[8,4,256]{2,1,0:T(4,128)} %get-tuple-element.60) | copy-start | bytes 98308
  713.4 3.3 copy-start.4
  716.7 1.7 copy-start.2
  1050.7 4.7 copy-start.7
  1056.7 2.7 copy-start.10
  1060.1 2.9 copy-start.3
  1060.1 2.9 copy-start.5
Sparse Core Ops, SparseCore 0:
  9.6 128.2 all-gather.4
  140.0 203.9 all-gather.2
  585.6 145.0 reduce-scatter.4
  733.2 244.2 reduce-scatter.2

commit v5 on v4

--- a/solution.py
+++ b/solution.py
@@ -95,42 +95,51 @@
         self.first, self.second, self.me, self.flat = first, second, me, flat
         self.pieces, self.own, self.slot = pieces, own, slot
         self.send_sem, self.recv_sem, self.ready = send_sem, recv_sem, ready
-        self.sent = []
-
-    def _copy(self, src, origin, h, line, turn):
+        self.opening = [
+            (line.has(turn), h, line, turn)
+            for h in range(pieces)
+            for line in (first, second)
+            for turn in (1, -1)
+        ]
+        self.sent = [(ok, me, h, line, turn) for ok, h, line, turn in self.opening]
+
+    def _source(self, origin, h):
+        return self.own(h) if origin is self.me else self.slot(origin, h)
+
+    def _copy(self, origin, h, line, turn):
         way = (0 if line is self.first else 2) + (turn > 0)
         return send_to(
-            src,
+            self._source(origin, h),
             self.slot(origin, h),
             self.send_sem.at[origin, h, way],
             self.recv_sem.at[origin, h],
             line.device(turn),
         )
 
-    def _send(self, src, origin, h, line, turn, cond):
-        ok = cond & line.has(turn)
-        pl.when(ok)(lambda: self._copy(src, origin, h, line, turn).start())
-        self.sent.append((ok, src, origin, h, line, turn))
-
     def start(self):
         for h in range(self.pieces):
             if self.ready is not None:
                 self.ready(h)
-            for line in (self.first, self.second):
-                for turn in (1, -1):
-                    self._send(self.own(h), self.me, h, line, turn, self.me >= 0)
-
-    def _arrive(self, place, side, h, sends):
+            for ok, piece, line, turn in self.opening:
+                if piece == h:
+                    pl.when(ok)(lambda: self._copy(self.me, h, line, turn).start())
+
+    def _arrival(self, place, side, h, sends):
         first, second = self.first, self.second
         cond = first.inside(place) & second.inside(side)
         origin = lax.select(cond, self.flat(place, side), self.me)
-
-        @pl.when(cond)
-        def _():
-            self._copy(self.slot(origin, h), origin, h, first, 1).wait_recv()
-
-        for line, turn in sends:
-            self._send(self.slot(origin, h), origin, h, line, turn, cond)
+        onward = [(cond & line.has(turn), origin, h, line, turn) for line, turn in sends]
+        self.sent += onward
+
+        def thunk():
+            @pl.when(cond)
+            def _():
+                self._copy(origin, h, first, 1).wait_recv()
+
+            for ok, *way in onward:
+                pl.when(ok)(lambda: self._copy(*way).start())
+
+        return thunk
 
     def steps(self):
         first, second = self.first, self.second
@@ -141,7 +150,7 @@
                     listed.append(
                         (
                             far,
-                            lambda far=far, h=h, sign=sign: self._arrive(
+                            self._arrival(
                                 first.place - sign * far,
                                 second.place,
                                 h,
@@ -157,7 +166,7 @@
                             listed.append(
                                 (
                                     far + step + 0.5,
-                                    lambda far=far, step=step, h=h, sign=sign, turn=turn: self._arrive(
+                                    self._arrival(
                                         first.place - sign * far,
                                         second.place - turn * step,
                                         h,
@@ -168,8 +177,8 @@
         return listed
 
     def finish(self):
-        for ok, src, origin, h, line, turn in self.sent:
-            pl.when(ok)(lambda: self._copy(src, origin, h, line, turn).wait_send())
+        for ok, *way in self.sent:
+            pl.when(ok)(lambda: self._copy(*way).wait_send())
 
 
 def run_steps(*programs):
@@ -255,7 +264,7 @@
         lanes = 1 if first_size == 2 else 2
         return [
             pltpu.VMEM((lanes, second_size if first_size == 2 else seq, rows, width), BF),
-            pltpu.VMEM((2, second_size, rows, width), BF),
+            pltpu.VMEM((2, max(1, second_size - 1), rows, width), BF),
             pltpu.SemaphoreType.DMA((seq, pieces)),
             pltpu.SemaphoreType.DMA((lanes, seq, pieces)),
             pltpu.SemaphoreType.DMA((2, second_size, pieces)),
@@ -267,25 +276,30 @@
     def _held(self, dest, spot):
         return spot if self.first.size == 2 else dest
 
+    def _passed(self, spot, side):
+        return lax.max(spot - 1, 0) if side == 0 else lax.min(spot, max(0, self.second.size - 2))
+
     def _cut(self, h):
         return pl.ds(*self.cuts[h])
 
     def _inner(self, h):
         return pl.ds(self.cuts[h][0] - self.base, self.cuts[h][1])
 
-    def _copy(self, src, dest, spot, h, line, turn):
+    def _copy(self, dest, spot, h, line, turn):
         if line is self.first:
             lane = self._lane(turn)
             held = self._held(dest, spot)
             dst, sem = self.from_first.at[lane, held, self._inner(h)], self.first_sem.at[lane, dest, h]
         else:
             side = 0 if turn > 0 else 1
-            dst, sem = self.from_second.at[side, spot, self._inner(h)], self.second_sem.at[side, spot, h]
-        return send_to(src, dst, self.send_sem.at[dest, h], sem, line.device(turn))
-
-    def _send(self, src, dest, spot, h, line, turn, ok):
-        pl.when(ok)(lambda: self._copy(src, dest, spot, h, line, turn).start())
-        self.sent.append((ok, src, dest, spot, h, line, turn))
+            dst = self.from_second.at[side, self._passed(spot, side), self._inner(h)]
+            sem = self.second_sem.at[side, spot, h]
+        return send_to(
+            self.terms.at[dest, self._cut(h)], dst, self.send_sem.at[dest, h], sem, line.device(turn)
+        )
+
+    def _send(self, ok, *way):
+        pl.when(ok)(lambda: self._copy(*way).start())
 
     def _add(self, cond, whole, parts, out, h):
         first, count = self.cuts[h]
@@ -317,34 +331,35 @@
             for far, sign, spot, ok in self._spread():
                 for h in range(len(self.cuts)):
                     for turn in (1, -1):
-                        yield lambda a=(step, spot, ok, h, turn): self._pass_on(*a)
-
-    def _pass_on(self, step, spot, ok, h, turn):
-        first = self.first
-        goal = first.place + turn * step
-        go = ok & first.inside(goal)
-        dest = lax.select(go, self.flat(goal, spot), self.me)
-        if first.size == 2:
-            self._send(self.terms.at[dest, self._cut(h)], dest, spot, h, first, turn, go)
-            return
-        behind = first.has(-turn)
-        self._await(go & behind, dest, spot, h, first, turn)
-        self._add(go & behind, [self.terms.at[dest]], [self.from_first.at[self._lane(turn), dest]], self.terms.at[dest], h)
-        self._send(self.terms.at[dest, self._cut(h)], dest, spot, h, first, turn, go)
+                        goal = first.place + turn * step
+                        go = ok & first.inside(goal)
+                        dest = lax.select(go, self.flat(goal, spot), self.me)
+                        way = (dest, spot, h, first, turn)
+                        self.sent.append((go, *way))
+                        yield lambda go=go, way=way: self._pass_on(go, *way)
+
+    def _pass_on(self, go, dest, spot, h, first, turn):
+        if first.size > 2:
+            behind = go & first.has(-turn)
+            self._await(behind, dest, spot, h, first, turn)
+            self._add(behind, [self.terms.at[dest]], [self.from_first.at[self._lane(turn), dest]], self.terms.at[dest], h)
+        self._send(go, dest, spot, h, first, turn)
 
     def _await(self, cond, dest, spot, h, line, turn):
         @pl.when(cond)
         def _():
-            self._copy(self.terms.at[dest, self._cut(h)], dest, spot, h, line, turn).wait_recv()
+            self._copy(dest, spot, h, line, turn).wait_recv()
 
     def inward(self):
         for far, sign, spot, ok in self._spread():
+            dest = lax.select(ok, self.flat(self.first.place, spot), self.me)
             for h in range(len(self.cuts)):
-                yield lambda a=(far, sign, spot, ok, h): self._collect(*a)
-
-    def _collect(self, far, sign, spot, ok, h):
+                if far:
+                    self.sent.append((ok, dest, spot, h, self.second, sign))
+                yield lambda a=(far, sign, spot, ok, dest, h): self._collect(*a)
+
+    def _collect(self, far, sign, spot, ok, dest, h):
         first, second, acc = self.first, self.second, self.terms
-        dest = lax.select(ok, self.flat(first.place, spot), self.me)
         for turn in (1, -1):
             self._await(ok & first.has(-turn), dest, spot, h, first, turn)
         if first.size == 2:
@@ -359,20 +374,23 @@
             behind = second.has(-sign)
             side = 0 if sign > 0 else 1
             self._await(ok & behind, dest, spot, h, second, sign)
-            self._add(ok & behind, [acc.at[dest]], [self.from_second.at[side, spot]], acc.at[dest], h)
-            self._send(acc.at[dest, self._cut(h)], dest, spot, h, second, sign, ok)
+            self._add(
+                ok & behind, [acc.at[dest]], [self.from_second.at[side, self._passed(spot, side)]], acc.at[dest], h
+            )
+            self._send(ok, dest, spot, h, second, sign)
             return
         low, high = second.has(-1), second.has(1)
         self._await(low, dest, spot, h, second, 1)
         self._await(high, dest, spot, h, second, -1)
-        lows, highs = self.from_second.at[0, spot], self.from_second.at[1, spot]
+        lows = self.from_second.at[0, self._passed(spot, 0)]
+        highs = self.from_second.at[1, self._passed(spot, 1)]
         self._add(low & high, [acc.at[dest]], [lows, highs], self.out, h)
         self._add(low & jnp.logical_not(high), [acc.at[dest]], [lows], self.out, h)
         self._add(high & jnp.logical_not(low), [acc.at[dest]], [highs], self.out, h)
 
     def finish(self):
-        for ok, src, dest, spot, h, line, turn in self.sent:
-            pl.when(ok)(lambda: self._copy(src, dest, spot, h, line, turn).wait_send())
+        for ok, *way in self.sent:
+            pl.when(ok)(lambda: self._copy(*way).wait_send())
 
 
 def woven(*lists):
@@ -460,6 +478,7 @@
     heads_here = cols // HEAD_DIM
     tile = 256
     per_block = 128 // own_rows
+    ahead = cotangent.shape[0]
 
     def kernel(*refs):
         (x_ref, c_ref, qkv_ref, proj_ref, packed_ref, routes_ref, cos_ref, sin_ref, col_ref, row_ref) = refs[:10]
@@ -635,7 +654,7 @@
                 normed_v[src, at, :] = (values * factor * gains_v[0:1, :]).astype(BF)
                 return inner
 
-            lax.fori_loop(0, rows // 16, strip, 0)
+            lax.fori_loop(0, rows // 16, strip, 0, unroll=4)
             normed_copy(src).start()
             at = pl.ds(pl.multiple_of(src * rows, rows), rows)
             for j in range(2):
@@ -742,7 +761,7 @@
     shaped = jax.ShapeDtypeStruct
     outs = [
         (shaped((seq, rows, width), BF), hbm),
-        (shaped((seq, rows, width), BF), hbm),
+        (shaped((seq, ahead, width), BF), hbm),
         (shaped((3, width, cols), BF), vmem),
         (shaped((ndp,) + proj_rows.shape, BF), hbm),
         (shaped((devices,) + packed.shape, BF), vmem),
@@ -783,7 +802,7 @@
             dma((seq,)),
         ]
         + gather_sems(seq, rows)
-        + gather_sems(seq, rows),
+        + gather_sems(seq, ahead),
         compiler_params=pltpu.CompilerParams(
             collective_id=collective_id, has_side_effects=True, vmem_limit_bytes=VMEM_MOST
         ),
@@ -902,7 +921,7 @@
             ffn_out[at, :] = (values * factor * gain_ref[...]).astype(BF)
             return carry
 
-        lax.fori_loop(0, rows // 16, strip, 0)
+        lax.fori_loop(0, rows // 16, strip, 0, unroll=4)
         own = pltpu.make_async_copy(ffn_out, all_out.at[me], own_sem)
         own.start()
         gathers = seq_gathers(ffn_out, all_out, sems)
@@ -936,7 +955,7 @@
     )(o_head, proj_weight, tokens, gain)
 
 
-def attend_back(dz, mixed_terms, proj_weight, o_head, query, key, value, raw, squares, gains, tables, segments, collective_id):
+def attend_back(dz, proj_weight, o_head, query, key, value, raw, squares, gains, tables, segments, collective_id):
     seq = lax.axis_size("seq")
     rows, width = dz.shape
     num_seqs, length, cols = query.shape
@@ -946,12 +965,12 @@
     scale = HEAD_DIM**-0.5
 
     def kernel(*refs):
-        (dz_ref, mixed_ref, w_ref, o_ref, q_ref, k_ref, v_ref, raw_ref, squares_ref, gains_ref) = refs[:10]
-        (cos_ref, sin_ref, col_ref, row_ref) = refs[10:14]
-        d_out, proj_out, gain_out, mixed_out = refs[14:18]
-        (dz_v, do_v, turned, dk_acc, dv_acc, proj_acc, factor_v, inner_v, inner_got, mixed_v) = refs[18:28]
-        own_sem, inner_send, inner_recv, mixed_sem = refs[28:32]
-        sems, mixed_scratch = refs[32:36], refs[36:]
+        (dz_ref, w_ref, o_ref, q_ref, k_ref, v_ref, raw_ref, squares_ref, gains_ref) = refs[:9]
+        (cos_ref, sin_ref, col_ref, row_ref) = refs[9:13]
+        d_out, proj_out, gain_out = refs[13:16]
+        (dz_v, do_v, turned, dk_acc, dv_acc, proj_acc, factor_v, inner_v, inner_got) = refs[16:25]
+        own_sem, inner_send, inner_recv = refs[25:28]
+        sems = refs[28:]
         dp = lax.axis_index("dp")
         along, across, me, _ = seq_lines()
         barrier = pltpu.get_barrier_semaphore()
@@ -962,8 +981,6 @@
         pl.semaphore_wait(barrier, seq - 1)
         own = pltpu.make_async_copy(dz_ref, dz_v.at[me], own_sem)
         own.start()
-        mixed_load = pltpu.make_async_copy(mixed_ref, mixed_v, mixed_sem)
-        mixed_load.start()
         programs = seq_gathers(dz_ref, dz_v, sems)
         for program in programs:
             program.start()
@@ -971,16 +988,6 @@
         proj_acc[...] = jnp.zeros_like(proj_acc)
         own.wait()
         run_steps(*programs)
-        mixed_load.wait()
-        reduces = seq_reduces(mixed_v, mixed_out, mixed_scratch)
-        for step in woven(*[p.outward() for p in reduces]):
-            step()
-        inward = woven(*[p.inward() for p in reduces])
-        in_all = len(inward)
-
-        def move_mixed(share):
-            while inward and in_all - len(inward) < share * in_all:
-                inward.pop(0)()
 
         def project(src, carry):
             back = dot_rows(dz_v[src], w_ref[...]).astype(BF)
@@ -1034,10 +1041,7 @@
                 ].astype(BF)
             return carry
 
-        lax.fori_loop(0, heads_here, attend, 0)
-        move_mixed(0.3)
-        lax.fori_loop(heads_here, num_seqs * heads_here, attend, 0)
-        move_mixed(0.5)
+        lax.fori_loop(0, num_seqs * heads_here, attend, 0)
 
         def pieces(j, src):
             spots = pl.ds(pl.multiple_of(src * local_len, local_len), local_len)
@@ -1073,7 +1077,6 @@
         for step in range(1, seq):
             inner_copy(lax.rem(me + step, seq), me).start()
         inner_got[me] = inner_v[...]
-        move_mixed(0.7)
         for program in programs:
             program.finish()
         for step in range(1, seq):
@@ -1092,9 +1095,6 @@
             return carry
 
         lax.fori_loop(0, seq, normalize, 0)
-        move_mixed(1.0)
-        for program in reduces:
-            program.finish()
 
     dma = pltpu.SemaphoreType.DMA
     hbm, vmem = pl.BlockSpec(memory_space=pl.ANY), pl.BlockSpec(memory_space=pltpu.VMEM)
@@ -1104,10 +1104,9 @@
             jax.ShapeDtypeStruct((3, seq, rows, cols), BF),
             jax.ShapeDtypeStruct((cols, width), BF),
             jax.ShapeDtypeStruct((8, cols), F32),
-            jax.ShapeDtypeStruct((rows, width), F32),
         ],
-        in_specs=[hbm] * 2 + [vmem] * 12,
-        out_specs=[vmem] * 4,
+        in_specs=[hbm] + [vmem] * 12,
+        out_specs=[vmem] * 3,
         scratch_shapes=[
             pltpu.VMEM((seq, rows, width), BF),
             pltpu.VMEM((num_seqs, length, cols), BF),
@@ -1118,22 +1117,18 @@
             pltpu.VMEM((2 * seq, rows), F32),
             pltpu.VMEM((2 * seq, rows), F32),
             pltpu.VMEM((seq, 2 * seq, rows), F32),
-            pltpu.VMEM((seq, rows, width), BF),
             dma,
             dma((seq,)),
             dma((seq,)),
-            dma,
         ]
-        + gather_sems(seq, rows)
-        + reduce_scratch(seq, rows, width),
+        + gather_sems(seq, rows),
         compiler_params=pltpu.CompilerParams(
             collective_id=collective_id, has_side_effects=True, vmem_limit_bytes=VMEM_MOST
         ),
         name="attend_back",
-        cost_estimate=cost_of(180),
+        cost_estimate=cost_of(130),
     )(
         dz,
-        mixed_terms,
         proj_weight,
         o_head,
         query,
@@ -1146,6 +1141,11 @@
         segments[:, :, None],
         segments[:, None, :],
     )
+
+
+def dp_cuts(rows):
+    pieces = max(n for n in (8, 4, 2, 1) if rows % (16 * n) == 0)
+    return [(i * (rows // pieces), rows // pieces) for i in range(pieces)]
 
 
 def last_sums(grads, normed, qkv_weight, proj_terms, router_terms, gain_heads, gain_ffn, gain_attn, collective_id):
@@ -1198,21 +1198,6 @@
             terms_v[dest] = total.astype(BF)
             return carry
 
-        programs = seq_reduces(terms_v, o_ref, seq_scratch)
-        lax.fori_loop(0, seq - nz, normed_term, 0)
-        pl.semaphore_wait(barrier, devices - 1)
-        for step in programs[0].outward():
-            step()
-        lax.fori_loop(seq - nz, seq, normed_term, 0)
-        for step in programs[1].outward():
-            step()
-        inward = woven(*[p.inward() for p in programs])
-        in_all = len(inward)
-
-        def move_sums(share):
-            while inward and in_all - len(inward) < share * in_all:
-                inward.pop(0)()
-
         load_normed.wait()
         gains_v[...] = jnp.zeros_like(gains_v)
         for j in range(2):
@@ -1237,23 +1222,10 @@
             return carry
 
         blocks = width // block
-        lax.fori_loop(0, blocks // 2, weight_term, 0)
-        move_sums(0.12)
-        lax.fori_loop(blocks // 2, blocks, weight_term, 0)
-        move_sums(0.25)
-        packed_v[:, 0:n_router, :] = router_ref[...]
-        for peer in range(devices):
-            at = peer // per_block * 128
-            packed_v[peer, n_router : n_router + 8, :] = gains_v[:, at : at + 128]
-
-        def small(peer, origin):
-            return send_to(
-                packed_v.at[peer], got.at[origin], small_send.at[peer], small_recv.at[origin], device(peer)
-            )
-
-        def small_start(step, carry):
-            small(lax.rem(rank + step, devices), rank).start()
-            return carry
+        near = blocks // x_line.size
+
+        def rotated(i, carry):
+            return weight_term(lax.rem((x_line.place + 1) * near + i, blocks), carry)
 
         load_proj.wait()
 
@@ -1263,7 +1235,7 @@
                 x_line,
                 dp,
                 lambda core, x: dp_flat(x, core),
-                [(0, refs.shape[1])],
+                dp_cuts(refs.shape[1]),
                 refs,
                 out,
                 *buffers[0:2],
@@ -1271,14 +1243,51 @@
             )
 
         owners = [over_dp(qkv_v, qkv_sum, qkv_scratch), over_dp(proj_v, proj_sum, proj_scratch)]
-        for owner in owners:
-            for step in owner.outward():
+        out_lists = [(list(owner.outward()), 2 * len(owner.cuts)) for owner in owners]
+        in_lists = [(list(owner.inward()), len(owner.cuts)) for owner in owners]
+        programs = seq_reduces(terms_v, o_ref, seq_scratch)
+
+        lax.fori_loop(0, seq - nz, normed_term, 0)
+        pl.semaphore_wait(barrier, devices - 1)
+        for step in programs[0].outward():
+            step()
+        lax.fori_loop(0, blocks - near, rotated, 0)
+        for steps, kept in out_lists:
+            for step in steps[:-kept]:
                 step()
+        lax.fori_loop(seq - nz, seq, normed_term, 0)
+        for step in programs[1].outward():
+            step()
+        for steps, kept in in_lists:
+            for step in steps[:-kept]:
+                step()
+        inward = woven(*[p.inward() for p in programs])
+        in_all = len(inward)
+
+        def move_sums(share):
+            while inward and in_all - len(inward) < share * in_all:
+                inward.pop(0)()
+
+        lax.fori_loop(blocks - near, blocks, rotated, 0)
+        for steps, kept in out_lists:
+            for step in steps[-kept:]:
+                step()
+        move_sums(0.25)
+        packed_v[:, 0:n_router, :] = router_ref[...]
+        for peer in range(devices):
+            at = peer // per_block * 128
+            packed_v[peer, n_router : n_router + 8, :] = gains_v[:, at : at + 128]
+
+        def small(peer, origin):
+            return send_to(
+                packed_v.at[peer], got.at[origin], small_send.at[peer], small_recv.at[origin], device(peer)
+            )
+
+        def small_start(step, carry):
+            small(lax.rem(rank + step, devices), rank).start()
+            return carry
+
         lax.fori_loop(1, devices, small_start, 0)
-        inner = [list(owner.inward()) for owner in owners]
-        for steps in inner:
-            for step in steps[:-1]:
-                step()
 
         def part(peer, origin):
             return send_to(
@@ -1299,9 +1308,10 @@
         def move():
             return send_to(proj_sum, proj_out, move_send, move_recv, device(goal))
 
-        move_sums(0.6)
-        for owner_steps in inner:
-            owner_steps[-1]()
+        move_sums(0.8)
+        for steps, kept in in_lists:
+            for step in steps[-kept:]:
+                step()
         own_part.start()
         for step in range(1, seq):
             part(lax.rem(me + step, seq), me).start()
@@ -1362,8 +1372,8 @@
             dma,
         ]
         + reduce_scratch(seq, rows, width)
-        + Reduce.scratch([(0, seq * part_rows)], 2, ndp // 2, cols)
-        + Reduce.scratch([(0, own_rows)], 2, ndp // 2, width)
+        + Reduce.scratch(dp_cuts(seq * part_rows), 2, ndp // 2, cols)
+        + Reduce.scratch(dp_cuts(own_rows), 2, ndp // 2, width)
         + [dma((seq,)), dma((seq,)), dma, dma, dma((devices,)), dma((devices,)), dma((2,))],
         compiler_params=pltpu.CompilerParams(
             collective_id=collective_id, has_side_effects=True, vmem_limit_bytes=VMEM_MOST
@@ -1379,11 +1389,17 @@
     return jnp.pad(flat, ((0, 0), (0, fill))).reshape(flat.shape[0], -1, 128)
 
 
-def experts_dispatch(ffn_all, cot_all, routes_all, router_full, me, experts, capacity):
+def slot_places(slots, capacity):
+    rows, experts = slots.shape
+    number = lax.broadcasted_iota(jnp.int32, (capacity, rows), 0).astype(F32)
+    return [as_row(slots[:, e : e + 1]) == number for e in range(experts)]
+
+
+def experts_dispatch(ffn_all, routes_all, router_full, me, experts, capacity):
     seq, rows, width = ffn_all.shape
     experts_all, top = router_full.shape[1], routes_all.shape[2]
 
-    def kernel(me_ref, ffn_ref, cot_ref, routes_ref, router_ref, rows_out, cot_out, gate_out, slot_out, col_out):
+    def kernel(me_ref, ffn_ref, routes_ref, router_ref, rows_out, gate_out, slot_out, col_out):
         first = me_ref[0] * experts
         logits = jnp.dot(ffn_ref[0], router_ref[...], preferred_element_type=F32)
         exps = jnp.exp(logits - jnp.max(logits, axis=-1, keepdims=True))
@@ -1399,19 +1415,16 @@
             jnp.int32, (rows, rows), 1
         )
         earlier = jnp.dot(below.astype(BF), hits.astype(BF), preferred_element_type=F32)
-        slots = jnp.where(hits > 0.0, earlier, float(rows + 1))
-        slots_row = slots.T
-        number = lax.broadcasted_iota(jnp.int32, (capacity, rows), 0).astype(F32)
-        places = []
+        slots = jnp.where(hits > 0.0, earlier, float(rows + 1))[:, 0:experts]
+        places = slot_places(slots, capacity)
+        slot_out[0] = slots
         for e in range(experts):
-            place = slots_row[e : e + 1, :] == number
-            gate_out[e, 0] = jnp.sum(jnp.where(place, as_row(gates[e]), 0.0), axis=1, keepdims=True)
-            slot_out[0, :, e : e + 1] = slots[:, e : e + 1]
+            gate_out[e, 0] = jnp.sum(jnp.where(places[e], as_row(gates[e]), 0.0), axis=1, keepdims=True)
             col_out[0, :, e : e + 1] = gates[e]
-            places.append(place.astype(BF))
         for e in range(experts):
-            rows_out[e, 0] = jnp.dot(places[e], ffn_ref[0], preferred_element_type=F32).astype(BF)
-            cot_out[e, 0] = jnp.dot(places[e], cot_ref[0], preferred_element_type=F32).astype(BF)
+            rows_out[e, 0] = jnp.dot(
+                places[e].astype(BF), ffn_ref[0], preferred_element_type=F32
+            ).astype(BF)
 
     def source(s, _):
         return (s, 0, 0)
@@ -1423,7 +1436,6 @@
     return pl.pallas_call(
         kernel,
         out_shape=[
-            shaped((experts, seq, capacity, width), BF),
             shaped((experts, seq, capacity, width), BF),
             shaped((experts, seq, capacity, 1), F32),
             shaped((seq, rows, experts), F32),
@@ -1434,12 +1446,10 @@
             grid=(seq,),
             in_specs=[
                 pl.BlockSpec((1, rows, width), source),
-                pl.BlockSpec((1, rows, width), source),
                 pl.BlockSpec((1, rows, top), source),
                 pl.BlockSpec((width, experts_all), lambda s, _: (0, 0)),
             ],
             out_specs=[
-                pl.BlockSpec((experts, 1, capacity, width), slot),
                 pl.BlockSpec((experts, 1, capacity, width), slot),
                 pl.BlockSpec((experts, 1, capacity, 1), slot),
                 pl.BlockSpec((1, rows, experts), source),
@@ -1448,156 +1458,148 @@
         ),
         compiler_params=pltpu.CompilerParams(vmem_limit_bytes=VMEM_MOST),
         name="experts_dispatch",
-        cost_estimate=cost_of(15),
-    )(me.reshape(1), ffn_all, cot_all, routes_all, router_full)
-
-
-def experts_run(first, count, rows, cot_rows, gates, weight_in, weight_out):
-    _, slots, width = rows.shape
+        cost_estimate=cost_of(12),
+    )(me.reshape(1), ffn_all, routes_all, router_full)
+
+
+EXPERT_STEP = 512
+
+
+def server(now, places, thunks):
+    per_step, steps = places
+    spots = [min(per_step * steps - 1, int(per_step * steps * share)) for share, _ in thunks]
+
+    def serve(point):
+        for mark in sorted(set(spots)):
+            if mark % per_step != point:
+                continue
+            group = [thunk for spot, (_, thunk) in zip(spots, thunks) if spot == mark]
+
+            @pl.when(now == mark // per_step)
+            def _():
+                for thunk in group:
+                    thunk()
+
+    return serve
+
+
+def experts_forward(rows, weight_in, weight_out, cot_rows, collective_id):
+    experts, slots, width = rows.shape
     hidden_width = weight_out.shape[1]
-    step = 256
+    step = EXPERT_STEP
     steps = hidden_width // step
-
-    def kernel(
-        rows_ref, cot_ref, gate_ref, in_ref, out_ref,
-        y_out, drows_out, dgate_out, in_out, outw_out,
-        gate_v, up_v, hidden_v, acc, dy_v, rows_t,
-    ):
-        phase, f = pl.program_id(1), pl.program_id(2)
-
-        def accumulate(value):
-            @pl.when(f == 0)
-            def _():
-                acc[...] = value
-
-            @pl.when(f > 0)
-            def _():
-                acc[...] += value
-
-        @pl.when(phase == 0)
+    seq = lax.axis_size("seq")
+    part = cot_rows.shape[0]
+    last = experts * steps - 1
+
+    def kernel(rows_ref, in_ref, out_ref, c_ref, y_out, gate_out, up_out, hidden_out, c_out, acc, own_sem, *sems):
+        f = pl.program_id(1)
+        now = pl.program_id(0) * steps + f
+        along, across, me, _ = seq_lines()
+        gathers = seq_gathers(c_ref, c_out, sems)
+        moves = sorted((s for p in gathers for s in p.steps()), key=lambda s: s[0])
+        most = max(hops for hops, _ in moves)
+        serve = server(now, (2, last + 1), [(0.1 + 0.85 * hops / most, thunk) for hops, thunk in moves])
+        own = pltpu.make_async_copy(c_ref, c_out.at[me], own_sem)
+
+        @pl.when(now == 0)
         def _():
-            @pl.when(f == 0)
-            def _():
-                rows_t[...] = rows_ref[0].T
-
-            gate = jnp.dot(rows_ref[0], in_ref[0, 0], preferred_element_type=F32)
-            up = jnp.dot(rows_ref[0], in_ref[0, 1], preferred_element_type=F32)
-            gate_v[f] = gate
-            up_v[f] = up
-            hidden = (gate / (1.0 + jnp.exp(-gate)) * up).astype(BF)
-            hidden_v[f] = hidden
-            accumulate(jnp.dot(hidden, out_ref[0], preferred_element_type=F32))
-
-            @pl.when(f == steps - 1)
-            def _():
-                result = acc[...].astype(BF)
-                y_out[0] = result
-                cot = cot_ref[0].astype(F32)
-                dgate_out[0] = jnp.sum(cot * result.astype(F32), axis=1, keepdims=True)
-                dy_v[...] = (cot * gate_ref[0]).astype(BF)
-
-        @pl.when(phase == 1)
+            greet_lines(along, across)
+            own.start()
+            for program in gathers:
+                program.start()
+
+        gate = jnp.dot(rows_ref[0], in_ref[0, 0], preferred_element_type=F32)
+        up = jnp.dot(rows_ref[0], in_ref[0, 1], preferred_element_type=F32)
+        gate_out[0] = gate.astype(BF)
+        up_out[0] = up.astype(BF)
+        hidden = (gate / (1.0 + jnp.exp(-gate)) * up).astype(BF)
+        hidden_out[0] = hidden
+        serve(0)
+        value = jnp.dot(hidden, out_ref[0], preferred_element_type=F32)
+
+        @pl.when(f == 0)
         def _():
-            grad = dot_rows(dy_v[...], out_ref[0])
-            gate, up = gate_v[f], up_v[f]
-            sig = 1.0 / (1.0 + jnp.exp(-gate))
-            dgate = (grad * up * sig * (1.0 + gate * (1.0 - sig))).astype(BF)
-            dup = (grad * gate * sig).astype(BF)
-            outw_out[0] = lax.dot_general(
-                hidden_v[f], dy_v[...], (((0,), (0,)), ((), ())), preferred_element_type=F32
-            ).astype(BF)
-            in_out[0, 0] = jnp.dot(rows_t[...], dgate, preferred_element_type=F32).astype(BF)
-            in_out[0, 1] = jnp.dot(rows_t[...], dup, preferred_element_type=F32).astype(BF)
-            accumulate(dot_rows(dgate, in_ref[0, 0]) + dot_rows(dup, in_ref[0, 1]))
-
-            @pl.when(f == steps - 1)
-            def _():
-                drows_out[0] = acc[...].astype(BF)
+            acc[...] = value
+
+        @pl.when(f > 0)
+        def _():
+            acc[...] += value
+
+        @pl.when(f == steps - 1)
+        def _():
+            y_out[0] = acc[...].astype(BF)
+
+        serve(1)
+
+        @pl.when(now == last)
+        def _():
+            for program in gathers:
+                program.finish()
+            own.wait()
 
     shaped = jax.ShapeDtypeStruct
-    by_expert = pl.BlockSpec((1, slots, width), lambda e, p, f: (first + e, 0, 0))
-    whole = pl.BlockSpec((1, slots, width), lambda e, p, f: (e, 0, 0))
-    flops = 18 * count * slots * width * hidden_width
+    hbm = pl.BlockSpec(memory_space=pl.ANY)
+    by_expert = pl.BlockSpec((1, slots, width), lambda e, f: (e, 0, 0))
+    hidden_block = pl.BlockSpec((1, slots, step), lambda e, f: (e, 0, f))
     return pl.pallas_call(
         kernel,
-        grid=(count, 2, steps),
+        grid=(experts, steps),
         out_shape=[
-            shaped((count, slots, width), BF),
-            shaped((count, slots, width), BF),
-            shaped((count, slots, 1), F32),
-            shaped((count, 2, width, hidden_width), BF),
-            shaped((count, hidden_width, width), BF),
+            shaped((experts, slots, width), BF),
+            shaped((experts, slots, hidden_width), BF),
+            shaped((experts, slots, hidden_width), BF),
+            shaped((experts, slots, hidden_width), BF),
+            shaped((seq, part, width), BF),
         ],
         in_specs=[
             by_expert,
-            by_expert,
-            pl.BlockSpec((1, slots, 1), lambda e, p, f: (first + e, 0, 0)),
-            pl.BlockSpec((1, 2, width, step), lambda e, p, f: (first + e, 0, 0, f)),
-            pl.BlockSpec((1, step, width), lambda e, p, f: (first + e, f, 0)),
+            pl.BlockSpec((1, 2, width, step), lambda e, f: (e, 0, 0, f)),
+            pl.BlockSpec((1, step, width), lambda e, f: (e, f, 0)),
+            hbm,
         ],
-        out_specs=[
-            whole,
-            whole,
-            pl.BlockSpec((1, slots, 1), lambda e, p, f: (e, 0, 0)),
-            pl.BlockSpec((1, 2, width, step), lambda e, p, f: (e, 0, 0, f * p)),
-            pl.BlockSpec((1, step, width), lambda e, p, f: (e, f * p, 0)),
-        ],
-        scratch_shapes=[
-            pltpu.VMEM((steps, slots, step), F32),
-            pltpu.VMEM((steps, slots, step), F32),
-            pltpu.VMEM((steps, slots, step), BF),
-            pltpu.VMEM((slots, width), F32),
-            pltpu.VMEM((slots, width), BF),
-            pltpu.VMEM((width, slots), BF),
-        ],
-        compiler_params=pltpu.CompilerParams(vmem_limit_bytes=VMEM_MOST),
-        name="experts_run",
-        cost_estimate=pl.CostEstimate(
-            flops=flops, bytes_accessed=50_000_000, transcendentals=2 * count * slots * hidden_width
+        out_specs=[by_expert, hidden_block, hidden_block, hidden_block, hbm],
+        scratch_shapes=[pltpu.VMEM((slots, width), F32), pltpu.SemaphoreType.DMA] + gather_sems(seq, part),
+        compiler_params=pltpu.CompilerParams(
+            collective_id=collective_id, has_side_effects=True, vmem_limit_bytes=VMEM_MOST
         ),
-    )(rows, cot_rows, gates, weight_in, weight_out)
-
-
-def experts_combine(outputs, drows, dgates, slot_cols, gate_cols, capacity):
-    seq, rows, experts = slot_cols.shape
-    parts = len(outputs)
-    per = experts // parts
-    width = outputs[0].shape[-1]
-
-    def kernel(*refs):
-        y_refs, d_refs, g_refs = refs[:parts], refs[parts : 2 * parts], refs[2 * parts : 3 * parts]
-        slot_ref, gate_ref, mixed_out, dffn_out, dprob_out, y_v, d_v = refs[3 * parts :]
-        slots = slot_ref[0]
+        name="experts_forward",
+        cost_estimate=cost_of(65),
+    )(rows, weight_in, weight_out, cot_rows)
+
+
+def experts_mix(outputs, cot_first, cot_rest, gates, slot_cols, gate_cols):
+    experts, slots, width = outputs.shape
+    seq, rows, _ = slot_cols.shape
+    capacity = slots // seq
+    ahead = cot_first.shape[1]
+
+    def kernel(y_ref, a_ref, b_ref, gate_ref, slot_ref, col_ref, mixed_out, dy_out, dprob_out, y_v, c_v):
+        slot_cols = slot_ref[0]
+        c_v[0:ahead, :] = a_ref[0]
+        c_v[ahead:rows, :] = b_ref[0]
         number = lax.broadcasted_iota(jnp.int32, (rows, capacity), 1).astype(F32)
-        number_rows = lax.broadcasted_iota(jnp.int32, (capacity, rows), 0).astype(F32)
-        gated, plain = [], []
+        places = slot_places(slot_cols, capacity)
+        gated = []
         for e in range(experts):
-            part, at = e // per, e % per
-            place = slots[:, e : e + 1] == number
-            gated.append(jnp.where(place, gate_ref[0, :, e : e + 1], 0.0).astype(BF))
-            plain.append(place.astype(BF))
-            cut = slice(e * capacity, (e + 1) * capacity)
-            y_v[cut, :] = y_refs[part][at, 0]
-            d_v[cut, :] = d_refs[part][at, 0]
-            across = as_row(slots[:, e : e + 1]) == number_rows
-            dprob_out[0, e : e + 1, :] = jnp.sum(
-                jnp.where(across, g_refs[part][at, 0], 0.0), axis=0, keepdims=True
+            value = y_ref[e, 0]
+            y_v[e * capacity : (e + 1) * capacity, :] = value
+            gated.append(
+                jnp.where(slot_cols[:, e : e + 1] == number, col_ref[0, :, e : e + 1], 0.0).astype(BF)
             )
+            cot = jnp.dot(places[e].astype(BF), c_v[...], preferred_element_type=F32)
+            dy_out[e, 0] = (cot * gate_ref[e, 0]).astype(BF)
+            dgate = jnp.sum(cot * value.astype(F32), axis=1, keepdims=True)
+            dprob_out[0, e : e + 1, :] = jnp.sum(jnp.where(places[e], dgate, 0.0), axis=0, keepdims=True)
         mixed_out[0] = jnp.dot(
             jnp.concatenate(gated, axis=1), y_v[...], preferred_element_type=F32
         ).astype(BF)
-        dffn_out[0] = jnp.dot(
-            jnp.concatenate(plain, axis=1), d_v[...], preferred_element_type=F32
-        ).astype(BF)
 
     def source(s):
         return (s, 0, 0)
 
-    slot_rows = pl.BlockSpec((per, 1, capacity, width), lambda s: (0, s, 0, 0))
-    slot_ones = pl.BlockSpec((per, 1, capacity, 1), lambda s: (0, s, 0, 0))
-
-    def split(arrays):
-        return [a.reshape(per, seq, capacity, a.shape[-1]) for a in arrays]
+    def slot(s):
+        return (0, s, 0, 0)
 
     shaped = jax.ShapeDtypeStruct
     return pl.pallas_call(
@@ -1605,25 +1607,227 @@
         grid=(seq,),
         out_shape=[
             shaped((seq, rows, width), BF),
-            shaped((seq, rows, width), BF),
+            shaped((experts, seq, capacity, width), BF),
             shaped((seq, experts, rows), F32),
         ],
-        in_specs=[slot_rows] * (2 * parts)
-        + [slot_ones] * parts
-        + [pl.BlockSpec((1, rows, experts), source)] * 2,
+        in_specs=[
+            pl.BlockSpec((experts, 1, capacity, width), slot),
+            pl.BlockSpec((1, ahead, width), source),
+            pl.BlockSpec((1, rows - ahead, width), source),
+            pl.BlockSpec((experts, 1, capacity, 1), slot),
+            pl.BlockSpec((1, rows, experts), source),
+            pl.BlockSpec((1, rows, experts), source),
+        ],
         out_specs=[
             pl.BlockSpec((1, rows, width), source),
-            pl.BlockSpec((1, rows, width), source),
+            pl.BlockSpec((experts, 1, capacity, width), slot),
             pl.BlockSpec((1, experts, rows), source),
         ],
+        scratch_shapes=[pltpu.VMEM((experts * capacity, width), BF), pltpu.VMEM((rows, width), BF)],
+        compiler_params=pltpu.CompilerParams(vmem_limit_bytes=VMEM_MOST),
+        name="experts_mix",
+        cost_estimate=cost_of(15),
+    )(outputs.reshape(experts, seq, capacity, width), cot_first, cot_rest, gates, slot_cols, gate_cols)
+
+
+def experts_out_terms(hidden, grads):
+    experts, slots, width = grads.shape
+    hidden_width = hidden.shape[2]
+    step = hidden_width
+
+    def kernel(hidden_ref, dy_ref, out_ref):
+        out_ref[0] = lax.dot_general(
+            hidden_ref[0], dy_ref[0], (((0,), (0,)), ((), ())), preferred_element_type=F32
+        ).astype(BF)
+
+    return pl.pallas_call(
+        kernel,
+        grid=(experts, hidden_width // step),
+        out_shape=jax.ShapeDtypeStruct((experts, hidden_width, width), BF),
+        in_specs=[
+            pl.BlockSpec((1, slots, step), lambda e, f: (e, 0, f)),
+            pl.BlockSpec((1, slots, width), lambda e, f: (e, 0, 0)),
+        ],
+        out_specs=pl.BlockSpec((1, step, width), lambda e, f: (e, f, 0)),
+        compiler_params=pltpu.CompilerParams(vmem_limit_bytes=VMEM_MOST),
+        name="experts_out_terms",
+        cost_estimate=cost_of(15),
+    )(hidden, grads)
+
+
+def experts_back(rows, grads, gate_in, up_in, weight_in, weight_out, mixed_terms, collective_id):
+    experts, slots, width = rows.shape
+    hidden_width = weight_out.shape[1]
+    step = EXPERT_STEP
+    steps = hidden_width // step
+    seq, tok, _ = mixed_terms.shape
+    last = experts * steps - 1
+
+    def kernel(
+        rows_ref, dy_ref, gate_ref, up_ref, in_ref, out_ref, mixed_ref,
+        drows_out, in_out, mixed_out,
+        rows_t, mixed_v, load_sem, *scratch,
+    ):
+        f = pl.program_id(1)
+        now = pl.program_id(0) * steps + f
+        along, across, _, _ = seq_lines()
+        reduces = seq_reduces(mixed_v, mixed_out, scratch)
+        outward, late = (list(p.outward()) for p in reduces)
+        early_in, late_in = (list(p.inward()) for p in reduces)
+        nz = along.size
+        rank = 2 * len(reduces[0].cuts)
+        thunks = [(0.06 + 0.18 * i / len(late), thunk) for i, thunk in enumerate(late)]
+        thunks += [(0.07 + (i // rank + 1) / nz, thunk) for i, thunk in enumerate(early_in)]
+        thunks += [((i + 1.5) / (len(late_in) + 0.5), thunk) for i, thunk in enumerate(late_in)]
+        serve = server(now, (4, last + 1), sorted(thunks, key=lambda t: t[0]))
+        load = pltpu.make_async_copy(mixed_ref, mixed_v, load_sem)
+
+        @pl.when(now == 0)
+        def _():
+            load.start()
+            greet_lines(along, across)
+            load.wait()
+            for thunk in outward:
+                thunk()
+
+        @pl.when(f == 0)
+        def _():
+            rows_t[...] = rows_ref[0].T
+
+        grad = dot_rows(dy_ref[0], out_ref[0])
+        serve(0)
+        gate, up = gate_ref[0].astype(F32), up_ref[0].astype(F32)
+        sig = 1.0 / (1.0 + jnp.exp(-gate))
+        silu = gate * sig
+        dgate = (grad * up * sig * (1.0 + gate * (1.0 - sig))).astype(BF)
+        dup = (grad * silu).astype(BF)
+        in_out[0, 0] = jnp.dot(rows_t[...], dgate, preferred_element_type=F32).astype(BF)
+        serve(1)
+        in_out[0, 1] = jnp.dot(rows_t[...], dup, preferred_element_type=F32).astype(BF)
+        serve(2)
+        value = dot_rows(dgate, in_ref[0, 0]) + dot_rows(dup, in_ref[0, 1])
+
+        @pl.when(f == 0)
+        def _():
+            drows_out[0] = value.astype(BF)
+
+        @pl.when(f > 0)
+        def _():
+            drows_out[0] = (drows_out[0].astype(F32) + value).astype(BF)
+
+        serve(3)
+
+        @pl.when(now == last)
+        def _():
+            for program in reduces:
+                program.finish()
+
+    shaped = jax.ShapeDtypeStruct
+    hbm = pl.BlockSpec(memory_space=pl.ANY)
+    by_expert = pl.BlockSpec((1, slots, width), lambda e, f: (e, 0, 0))
+    once = pl.BlockSpec((1, slots, width), lambda e, f: (e, 0, 0), pipeline_mode=pl.Buffered(1))
+    hidden_block = pl.BlockSpec((1, slots, step), lambda e, f: (e, 0, f))
+    in_block = pl.BlockSpec((1, 2, width, step), lambda e, f: (e, 0, 0, f))
+    out_block = pl.BlockSpec((1, step, width), lambda e, f: (e, f, 0))
+    return pl.pallas_call(
+        kernel,
+        grid=(experts, steps),
+        out_shape=[
+            shaped((experts, slots, width), BF),
+            shaped((experts, 2, width, hidden_width), BF),
+            shaped((tok, width), F32),
+        ],
+        in_specs=[once, once, hidden_block, hidden_block, in_block, out_block, hbm],
+        out_specs=[by_expert, in_block, pl.BlockSpec(memory_space=pltpu.VMEM)],
         scratch_shapes=[
+            pltpu.VMEM((width, slots), BF),
+            pltpu.VMEM((seq, tok, width), BF),
+            pltpu.SemaphoreType.DMA,
+        ]
+        + reduce_scratch(seq, tok, width),
+        compiler_params=pltpu.CompilerParams(
+            collective_id=collective_id, has_side_effects=True, vmem_limit_bytes=VMEM_MOST
+        ),
+        name="experts_back",
+        cost_estimate=cost_of(95),
+    )(rows, grads, gate_in, up_in, weight_in, weight_out, mixed_terms)
+
+
+def rows_back(drows, slot_cols, prob_grads, collective_id):
+    seq, rows, experts = slot_cols.shape
+    width = drows.shape[-1]
+    capacity = drows.shape[1] // seq
+    nz, ny = grid_of(seq)
+
+    def kernel(d_ref, slot_ref, prob_ref, o_ref, prob_out, terms_v, d_v, prob_send, prob_recv, *scratch):
+        dp = lax.axis_index("dp")
+        _, across, me, _ = seq_lines()
+        barrier = pltpu.get_barrier_semaphore()
+        for step in range(1, seq):
+            pl.semaphore_signal(
+                barrier, 1, device_id=(dp, lax.rem(me + step, seq)), device_id_type=MESH
+            )
+        number = lax.broadcasted_iota(jnp.int32, (rows, capacity), 1).astype(F32)
+
+        def term(i, carry):
+            dest = lax.rem(i, nz) * ny + lax.rem(across.place + 1 + lax.div(i, nz), ny)
+            places = []
+            for e in range(experts):
+                d_v[e * capacity : (e + 1) * capacity, :] = d_ref[e, dest]
+                places.append((slot_ref[dest, :, e : e + 1] == number).astype(BF))
+            terms_v[dest] = jnp.dot(
+                jnp.concatenate(places, axis=1), d_v[...], preferred_element_type=F32
+            ).astype(BF)
+            return carry
+
+        def prob_copy(peer, origin):
+            return send_to(
+                prob_ref.at[peer], prob_out.at[origin], prob_send.at[peer], prob_recv.at[origin], (dp, peer)
+            )
+
+        reduces = seq_reduces(terms_v, o_ref, scratch)
+        lax.fori_loop(0, seq - nz, term, 0)
+        pl.semaphore_wait(barrier, seq - 1)
+        for step in range(1, seq):
+            prob_copy(lax.rem(me + step, seq), me).start()
+        for thunk in reduces[0].outward():
+            thunk()
+        lax.fori_loop(seq - nz, seq, term, 0)
+        for thunk in reduces[1].outward():
+            thunk()
+        prob_out[me] = prob_ref[me]
+        for thunk in woven(*[p.inward() for p in reduces]):
+            thunk()
+        for program in reduces:
+            program.finish()
+        for step in range(1, seq):
+            prob_copy(lax.rem(me + step, seq), me).wait_send()
+            source = lax.rem(me + seq - step, seq)
+            prob_copy(source, source).wait_recv()
+
+    vmem = pl.BlockSpec(memory_space=pltpu.VMEM)
+    dma = pltpu.SemaphoreType.DMA
+    return pl.pallas_call(
+        kernel,
+        out_shape=[
+            jax.ShapeDtypeStruct((rows, width), F32),
+            jax.ShapeDtypeStruct(prob_grads.shape, F32),
+        ],
+        in_specs=[vmem] * 3,
+        out_specs=[vmem] * 2,
+        scratch_shapes=[
+            pltpu.VMEM((seq, rows, width), BF),
             pltpu.VMEM((experts * capacity, width), BF),
-            pltpu.VMEM((experts * capacity, width), BF),
-        ],
-        compiler_params=pltpu.CompilerParams(vmem_limit_bytes=VMEM_MOST),
-        name="experts_combine",
-        cost_estimate=cost_of(15),
-    )(*split(outputs), *split(drows), *split(dgates), slot_cols, gate_cols)
+            dma((seq,)),
+            dma((seq,)),
+        ]
+        + reduce_scratch(seq, rows, width),
+        compiler_params=pltpu.CompilerParams(
+            collective_id=collective_id, has_side_effects=True, vmem_limit_bytes=VMEM_MOST
+        ),
+        name="rows_back",
+        cost_estimate=cost_of(90),
+    )(drows.reshape(experts, seq, capacity, width), slot_cols, prob_grads)
 
 
 def rms_factor(values):
@@ -1670,10 +1874,11 @@
         jnp.zeros((16, 128), BF), norm_gains, (0, lax.rem(rank, 128 // own_rows) * own_rows)
     )
     tables = rotary_tables(seq_length)
+    ahead = tok * 10 // 256 * 16
     normed_all, cot_all, qkv_weight, proj_got, small_all, routes_all, raw, query_head, key_head, value_head, o_head, sums = (
         attend_first(
             token_rows,
-            cot_low,
+            cot_low[:ahead],
             attn_weight[:, :3].reshape(own_rows, 3, seq, cols).transpose(2, 1, 0, 3),
             attn_weight[:, 3],
             jnp.concatenate([router_rows, gain_rows_own], axis=0),
@@ -1707,32 +1912,34 @@
     factor_ffn = rms_factor(middle)
 
     slots = seq * capacity
-    rows, cot_rows, gates, slot_cols, gate_cols = experts_dispatch(
-        ffn_all, cot_all, routes_all, router_full, me, experts, capacity
+    in_weight = in_full.transpose(0, 2, 1, 3)
+    rows, gates, slot_cols, gate_cols = experts_dispatch(
+        ffn_all, routes_all, router_full, me, experts, capacity
     )
-    rows, cot_rows = rows.reshape(experts, slots, width), cot_rows.reshape(experts, slots, width)
-    gates = gates.reshape(experts, slots, 1)
-    halves = 1
-    count = experts // halves
-    runs = [
-        experts_run(half * count, count, rows, cot_rows, gates, in_full.transpose(0, 2, 1, 3), out_full)
-        for half in range(halves)
-    ]
-    in_grads = [
-        lax.psum_scatter(run[3].transpose(0, 2, 1, 3), "dp", scatter_dimension=1, tiled=True) for run in runs
-    ]
-    out_grads = [
-        lax.psum_scatter(run[4], "dp", scatter_dimension=2, tiled=True) for run in runs
-    ]
-    expert_in_grad = jnp.concatenate(in_grads).astype(F32)
-    expert_out_grad = jnp.concatenate(out_grads).astype(F32)
-    mixed_terms, dffn_terms, grad_prob_here = experts_combine(
-        [run[0] for run in runs], [run[1] for run in runs], [run[2] for run in runs], slot_cols, gate_cols, capacity
+    rows = rows.reshape(experts, slots, width)
+    outputs, gate_in, up_in, hidden, cot_rest = experts_forward(rows, in_weight, out_full, cot_low[ahead:], 7)
+    mixed_terms, output_grads, prob_grads = experts_mix(
+        outputs, cot_all, cot_rest, gates, slot_cols, gate_cols
     )
-    grad_ffn = seq_reduce(dffn_terms, 9)
-    (grad_prob,) = small_exchange(
-        [grad_prob_here.reshape(seq, -1, 128)], ("seq",), 10
+    output_grads = output_grads.reshape(experts, slots, width)
+    out_term = experts_out_terms(hidden, output_grads)
+    expert_out_grad = lax.psum_scatter(out_term, "dp", scatter_dimension=2, tiled=True).astype(F32)
+    out_term, output_grads = lax.optimization_barrier((out_term, output_grads))
+    drows, in_term, mixed = experts_back(
+        rows,
+        output_grads,
+        gate_in,
+        up_in,
+        in_weight,
+        out_full,
+        mixed_terms,
+        8,
     )
+    block_out = (middle + mixed).astype(BF).reshape(num_seqs, local_len, width)
+    expert_in_grad = lax.psum_scatter(
+        in_term.transpose(0, 2, 1, 3), "dp", scatter_dimension=1, tiled=True
+    ).astype(F32)
+    grad_ffn, grad_prob = rows_back(drows, slot_cols, prob_grads, 9)
     grad_prob = grad_prob.reshape(experts_all, tok).T
 
     route_probs = jax.nn.softmax(
@@ -1749,9 +1956,8 @@
     grad_middle = grad_middle + cot_low.astype(F32)
 
     head_gains = jnp.pad(lax.dynamic_slice(gain_rows, (1, me * cols), (2, cols)), ((0, 6), (0, 0)))
-    grad_heads, proj_term, gain_heads, mixed = attend_back(
+    grad_heads, proj_term, gain_heads = attend_back(
         grad_middle.astype(BF),
-        mixed_terms,
         proj_weight,
         o_head,
         query_head,
@@ -1764,7 +1970,6 @@
         segments,
         11,
     )
-    block_out = (middle + mixed).astype(BF).reshape(num_seqs, local_len, width)
 
     grad_normed, qkv_out, proj_grad, total = last_sums(
         grad_heads,

time: 1100 us -> 1060 us (0.964)
  Pallas kernels: 1000 us -> 954 us
    pallas_call x1, Pallas kernels: 175 us -> 114 us  [attend_back(): pl.pallas_call(kernel, out_shape=[jax.ShapeDtypeStruct((3, seq, rows, col...]
    pallas_call x4 -> x5, Pallas kernels: 258 us -> 292 us  [the longest x1 110 us: experts_back(): pl.pallas_call(kernel, grid=(experts, steps), out_shape=[shaped((experts,...]
    pallas_call x1, Pallas kernels: 212 us -> 188 us  [attend_first(): pl.pallas_call(kernel, out_shape=[shape for shape, _ in outs], in_specs=[...]
    pallas_call x1, Pallas kernels: 157 us -> 170 us  [last_sums(): pl.pallas_call(kernel, out_shape=[jax.ShapeDtypeStruct((rows, width), F32...]
  transfers between devices with their start and end apart: 4 -> 4, of which waited for: 0 -> 0; matrix products, arithmetic and copies ran while one was open for 6% -> 6% of each run, Pallas kernels for 78% -> 82%
where the time goes in v5:
time: 1060 us; the launch traced here: 1050 us
  Pallas kernels  954 us (90%)
  local copies, waits for them, and re-layouts  53.6 us (5%)
  other arithmetic  22.5 us (2%)
  between operations  14.2 us (1%)
    pallas_call x1, Pallas kernels, attend_first(): pl.pallas_call(kernel, out_shape=[shape for shape, _ in outs], in_specs=[...  188 us
    pallas_call x1, Pallas kernels, middle_rows(): pl.pallas_call(kernel, out_shape=[jax.ShapeDtypeStruct((rows, width), F32...  173 us
    pallas_call x1, Pallas kernels, last_sums(): pl.pallas_call(kernel, out_shape=[jax.ShapeDtypeStruct((rows, width), F32...  170 us
    pallas_call x1, Pallas kernels, attend_back(): pl.pallas_call(kernel, out_shape=[jax.ShapeDtypeStruct((3, seq, rows, col...  114 us
    pallas_call x1, Pallas kernels, experts_back(): pl.pallas_call(kernel, grid=(experts, steps), out_shape=[shaped((experts,...  110 us
    pallas_call x1, Pallas kernels, rows_back(): pl.pallas_call(kernel, out_shape=[jax.ShapeDtypeStruct((rows, width), F32...  90.6 us
    pallas_call x1, Pallas kernels, experts_forward(): pl.pallas_call(kernel, grid=(experts, steps), out_shape=[shaped((experts,...  54.6 us
    unnamed x35, local copies, waits for them, and re-layouts  32.4 us
  transfers between devices with their start and end apart: 4, of which 0 were waited for; matrix products, arithmetic and copies ran while one was open for 6% of the time, Pallas kernels for 82%

profile of v5, /device:TPU:0, one launch (start us, length us, event | category | flops | bytes accessed | tf_op | source)
XLA Modules:
  0.0 1054.6 jit_solution(13706560689298537518)
XLA Ops:
  7.2 0.0 all-gather.5.cloned.1.call-start
  7.2 0.7 all-gather.5.cloned.1.call-update
  7.9 0.0 all-gather.3.cloned.1.call-start
  7.9 9.5 copy.44
  17.4 0.0 all-gather.3.cloned.1.call-update
  17.5 0.0 copy-start.7
  17.5 0.6 reduce-scatter.5.cloned.1.call-start
  18.1 0.8 copy-done.4
  18.8 0.9 slice.46.refs_1_
  19.7 0.8 slice.48.c_ref
  20.5 0.1 copy.41
  20.6 0.1 squeeze_reshape.3
  20.7 0.6 broadcast_in_dim.12.refs_9_.refs_12_
  21.3 1.3 copy.43.refs_8_.refs_11_
  22.6 0.6 slice.37
  23.2 0.9 reshape.147
  24.2 1.1 copy.58
  25.2 0.9 copy.60
  26.1 0.1 copy.42
  26.2 0.7 reshape.130.refs_5_
  26.9 0.3 dynamic_update_slice.3
  27.2 0.6 pad_maximum_fusion.2.refs_4_
  27.8 1.9 fusion.6
  29.7 1.3 pad_maximum_fusion
  31.1 187.7 %attend_first.1 = (bf16[8,256,2048]{2,1,0:T(8,128)(2,1)}, bf16[8,160,2048]{2,1,0:T(8,128)(2,1)}, bf16[3,2048,256]{2,1,0:T(8,128)(2,1)}, bf16[4,64,2048]{2,1,0:T(...) custom-call(bf16[256,2048]{1,0:T(8,128)(2,1)} %bitcast.74, ...), custom_call_target="tpu_custom_call" | custom-call | bytes 756000000 | tf_op jit(solution)/shard_map/attend_first/pallas_call | solution.py:776
  218.7 0.9 slice.41
  219.6 1.0 reshape_reshape.6.router_ref
  220.7 2.4 reshape.133.routes_ref
  223.1 0.9 convert_reduce_fusion
  223.9 0.6 fusion.13
  224.6 172.8 %middle_rows.1 = (f32[256,2048]{1,0:T(8,128)}, bf16[256,2048]{1,0:T(8,128)(2,1)}, bf16[8,256,2048]{2,1,0:T(8,128)(2,1)}) custom-call(bf16[8,256,256]{2,1,0:T(8,128)(2,1)} %get-tuple-element.47.refs_0_.refs_2_, bf16[256,2048]{1,0:T(8,128)(2,1)} %bitcast.80, bf16[256,2048]{1,0:T(8,128)(2,1)} %bitcast.75, f32[1,2048]{1,0:T(1,128)} %get-tuple-element.113.refs_3_), custom_call_target="tpu_custom_call" | custom-call | bytes 630000000 | tf_op jit(solution)/shard_map/middle_rows/pallas_call | solution.py:938
  397.4 17.8 %experts_dispatch.1 = (bf16[4,8,72,2048]{3,2,1,0:T(8,128)(2,1)}, f32[4,8,72,1]{3,2,1,0:T(8,128)}, f32[8,256,4]{2,1,0:T(8,128)}, f32[8,256,4]{2,1,0:T(8,128)}) custom-call(s32[1]{0:T(128)} %bitcast.9.me_ref, bf16[8,256,2048]{2,1,0:T(8,128)(2,1)} %get-tuple-element.51.ffn_ref, s32[8,256,8]{2,1,0:T(8,128)} %reshape.133.routes_ref, ...), custom_call_target="tpu_custom_call" | custom-call | bytes 43200000 | tf_op jit(solution)/shard_map/experts_dispatch/pallas_call | solution.py:1436
  415.2 0.0 all-gather.3.cloned.1.call-done
  415.2 54.6 %experts_forward.1 = (bf16[4,576,2048]{2,1,0:T(8,128)(2,1)}, bf16[4,576,1024]{2,1,0:T(8,128)(2,1)}, bf16[4,576,1024]{2,1,0:T(8,128)(2,1)}, bf16[4,576,1024]{2,1,0:T(8,128)(2,1)}, bf16[8,96,2048]{2,1,0:T(8,128)(2,1)}) custom-call(bf16[4,576,2048]{2,1,0:T(8,128)(2,1)} %bitcast.69, bf16[4,2,2048,1024]{3,2,1,0:T(8,128)(2,1)} %bitcast.67, ...), custom_call_target="tpu_custom_call" | custom-call | bytes 234000000 | tf_op jit(solution)/shard_map/experts_forward/pallas_call | solution.py:1545
  469.8 19.2 %experts_mix.1 = (bf16[8,256,2048]{2,1,0:T(8,128)(2,1)}, bf16[4,8,72,2048]{3,2,1,0:T(8,128)(2,1)}, f32[8,4,256]{2,1,0:T(4,128)}) custom-call(bf16[4,8,72,2048]{3,2,1,0:T(8,128)(2,1)} %bitcast.79, bf16[8,160,2048]{2,1,0:T(8,128)(2,1)} %get-tuple-element.56.a_ref, bf16[8,96,2048]{2,1,0:T(8,128)(2,1)} %get-tuple-element.57.b_ref, ...), custom_call_target="tpu_custom_call" | custom-call | bytes 54000000 | tf_op jit(solution)/shard_map/experts_mix/pallas_call | solution.py:1605
  489.1 18.0 %experts_out_terms.1 = bf16[4,1024,2048]{2,1,0:T(8,128)(2,1)} custom-call(bf16[4,576,1024]{2,1,0:T(8,128)(2,1)} %get-tuple-element.54.hidden_ref, bf16[4,576,2048]{2,1,0:T(8,128)(2,1)} %bitcast.71), custom_call_target="tpu_custom_call" | custom-call | bytes 54000000 | tf_op jit(solution)/shard_map/experts_out_terms/pallas_call | solution.py:1643
  507.0 0.0 reduce-scatter.5.cloned.1.call-update
  507.1 0.0 reduce-scatter.3.cloned.1.call-start
  507.1 109.8 %experts_back.1 = (bf16[4,576,2048]{2,1,0:T(8,128)(2,1)}, bf16[4,2,2048,1024]{3,2,1,0:T(8,128)(2,1)}, f32[256,2048]{1,0:T(8,128)}) custom-call(bf16[4,576,2048]{2,1,0:T(8,128)(2,1)} %bitcast.70, bf16[4,576,2048]{2,1,0:T(8,128)(2,1)} %bitcast.72, bf16[4,576,1024]{2,1,0:T(8,128)(2,1)} %get-tuple-element.63.gate_ref, ...), custom_call_target="tpu_custom_call" | custom-call | bytes 342000000 | tf_op jit(solution)/shard_map/experts_back/pallas_call | solution.py:1732
  616.9 0.0 reduce-scatter.3.cloned.1.call-update
  617.0 0.1 constant_dynamic-slice_fusion.1
  617.0 0.6 pad.4.refs_8_
  617.6 2.1 fusion.14
  619.8 0.3 multiply_reduce_fusion.3
  620.1 0.2 multiply_reduce_fusion.2
  620.3 90.6 %rows_back.1 = (f32[256,2048]{1,0:T(8,128)}, f32[8,4,256]{2,1,0:T(4,128)}) custom-call(bf16[4,8,72,2048]{3,2,1,0:T(8,128)(2,1)} %bitcast.76, f32[8,256,4]{2,1,0:T(8,128)} %get-tuple-element.59.slot_ref, f32[8,4,256]{2,1,0:T(4,128)} %get-tuple-element.68.prob_ref), custom_call_target="tpu_custom_call" | custom-call | bytes 324000000 | tf_op jit(solution)/shard_map/rows_back/pallas_call | solution.py:1810
  711.0 0.8 reshape.139
  711.8 3.0 fusion.15
  714.8 2.2 reshape.142.refs_4_
  717.0 3.2 multiply_reduce_fusion
  720.2 1.7 fusion.12.refs_0_
  721.9 113.6 %attend_back.1 = (bf16[3,8,256,256]{3,2,1,0:T(8,128)(2,1)}, bf16[256,2048]{1,0:T(8,128)(2,1)}, f32[8,256]{1,0:T(8,128)}) custom-call(bf16[256,2048]{1,0:T(8,128)(2,1)} %fusion.12.refs_0_, bf16[256,2048]{1,0:T(8,128)(2,1)} %bitcast.81, bf16[8,256,256]{2,1,0:T(8,128)(2,1)} %get-tuple-element.47.refs_0_.refs_2_, ...), custom_call_target="tpu_custom_call" | custom-call | bytes 468000000 | tf_op jit(solution)/shard_map/attend_back/pallas_call | solution.py:1101
  835.5 170.4 %last_sums.1 = (f32[256,2048]{1,0:T(8,128)}, bf16[8,192,256]{2,1,0:T(8,128)(2,1)}, bf16[64,2048]{1,0:T(8,128)(2,1)}, f32[24,128]{1,0:T(8,128)}) custom-call(bf16[3,8,256,256]{3,2,1,0:T(8,128)(2,1)} %get-tuple-element.77.refs_0_, bf16[8,256,2048]{2,1,0:T(8,128)(2,1)} %get-tuple-element.78.refs_1_, bf16[3,2048,256]{2,1,0:T(8,128)(2,1)} %get-tuple-element.79.refs_2_, ...), custom_call_target="tpu_custom_call" | custom-call | bytes 396000000 | tf_op jit(solution)/shard_map/last_sums/pallas_call | solution.py:1351
  1005.9 2.5 copy.59
  1008.4 2.2 reshape.145
  1010.5 1.3 maximum_convert_fusion
  1011.8 2.7 copy.48
  1014.5 0.1 reshape_reshape.7
  1014.6 0.7 copy.49
  1015.3 0.6 constant_dynamic-slice_fusion
  1015.9 2.2 fusion.5
  1018.2 5.2 fusion.4
  1023.4 6.8 convert_element_type.59
  1030.2 17.7 %copy.50 = f32[4,512,2,1024]{3,2,1,0:T(2,128)} copy(bf16[4,512,2,1024]{3,1,2,0:T(8,128)(2,1)} %reduce-scatter.3.cloned.1.call-done) | data formatting | bytes 25165824
  (40 shorter events, 0.2 us)
Async XLA Ops:
  7.2 408.0 %all-gather.5.cloned.1.call-start = ((), (), s32[]{:S(2)}) async-start(), calls=%async_computation.3 | async-start | bytes 20971520 | tf_op jit(solution)/shard_map/all_gather | solution.py:1893
  7.9 407.3 %all-gather.3.cloned.1.call-start = ((), (), s32[]{:S(2)}) async-start(), calls=%async_computation.2 | async-start | bytes 41943040 | tf_op jit(solution)/shard_map/all_gather | solution.py:1892
  17.4 1.4 copy-start.4
  17.4 3.0 copy-start.11
  17.5 3.2 copy-start.9
  17.5 5.1 copy-start.7
  17.5 1005.9 %reduce-scatter.5.cloned.1.call-start = ((), (), s32[]{:S(2)}) async-start(), calls=%async_computation.5 | async-start | bytes 20971520 | tf_op jit(solution)/shard_map/reduce_scatter | solution.py:1926
  23.2 2.9 copy-start.12
  23.2 3.7 copy-start.13
  507.1 523.1 %reduce-scatter.3.cloned.1.call-start = ((), (), s32[]{:S(2)}) async-start(), calls=%async_computation.4 | async-start | bytes 41943040 | tf_op jit(solution)/shard_map/reduce_scatter | solution.py:1939
  616.9 2.9 copy-start.1
  617.0 3.1 copy-start
  717.0 3.2 copy-start.5
  720.2 1.7 copy-start.2
  1005.9 4.7 copy-start.8
  1011.8 2.7 copy-start.10
  1015.3 2.9 copy-start.3
  1015.3 2.9 copy-start.6
Sparse Core Ops, SparseCore 0:
  9.6 128.2 all-gather.4
  140.0 205.5 all-gather.2
  507.2 150.8 reduce-scatter.4
  660.7 236.1 reduce-scatter.2

commit v6 on v5

--- a/solution.py
+++ b/solution.py
@@ -1889,6 +1889,7 @@
             1,
         )
     )
+    expert_in, sums = lax.optimization_barrier((expert_in, sums))
     in_full = lax.all_gather(expert_in, "dp", axis=1, tiled=True)
     out_full = lax.all_gather(expert_out, "dp", axis=2, tiled=True)
     router_full = (

time: 1060 us -> 1050 us (level)
  Pallas kernels: 954 us -> 928 us
  waiting for transfers between devices: 0.75 us -> 15.3 us
    pallas_call x1, Pallas kernels: 170 us -> 131 us  [last_sums(): pl.pallas_call(kernel, out_shape=[jax.ShapeDtypeStruct((rows, width), F32...]
    all_gather x1, waiting for transfers between devices: 0.01 us -> 14.6 us  [local(): in_full = lax.all_gather(expert_in, 'dp', axis=1, tiled=True)]
    unnamed x35 -> x38, local copies, waits for them, and re-layouts: 32.4 us -> 22.3 us
  transfers between devices with their start and end apart: 4 -> 4, of which waited for: 0 -> 1; matrix products, arithmetic and copies ran while one was open for 6% -> 6% of each run, Pallas kernels for 82% -> 81%
where the time goes in v6:
time: 1050 us; the launch traced here: 1040 us
  Pallas kernels  928 us (88%)
  local copies, waits for them, and re-layouts  51.3 us (5%)
  other arithmetic  21.7 us (2%)
  waiting for transfers between devices  15.3 us (1%)
  between operations  14.2 us (1%)
    pallas_call x1, Pallas kernels, attend_first(): pl.pallas_call(kernel, out_shape=[shape for shape, _ in outs], in_specs=[...  187 us
    pallas_call x1, Pallas kernels, middle_rows(): pl.pallas_call(kernel, out_shape=[jax.ShapeDtypeStruct((rows, width), F32...  174 us
    pallas_call x1, Pallas kernels, last_sums(): pl.pallas_call(kernel, out_shape=[jax.ShapeDtypeStruct((rows, width), F32...  131 us
    pallas_call x1, Pallas kernels, attend_back(): pl.pallas_call(kernel, out_shape=[jax.ShapeDtypeStruct((3, seq, rows, col...  122 us
    pallas_call x1, Pallas kernels, experts_back(): pl.pallas_call(kernel, grid=(experts, steps), out_shape=[shaped((experts,...  115 us
    pallas_call x1, Pallas kernels, rows_back(): pl.pallas_call(kernel, out_shape=[jax.ShapeDtypeStruct((rows, width), F32...  91.4 us
    pallas_call x1, Pallas kernels, experts_forward(): pl.pallas_call(kernel, grid=(experts, steps), out_shape=[shaped((experts,...  52.6 us
    unnamed x38, local copies, waits for them, and re-layouts  22.3 us
  transfers between devices with their start and end apart: 4, of which 1 were waited for; matrix products, arithmetic and copies ran while one was open for 6% of the time, Pallas kernels for 81%

profile of v6, /device:TPU:0, one launch (start us, length us, event | category | flops | bytes accessed | tf_op | source)
XLA Modules:
  0.0 1039.2 jit_solution(9562108608178000344)
XLA Ops:
  7.2 0.0 copy-start.4
  7.2 0.0 all-gather.5.cloned.1.call-start
  7.2 0.7 all-gather.5.cloned.1.call-update
  7.9 0.0 all-gather.3.cloned.1.call-start
  8.0 0.1 copy.41
  8.1 0.1 squeeze_reshape.3
  8.2 0.6 broadcast_in_dim.12.refs_9_.refs_12_
  8.8 1.3 copy.43.refs_8_.refs_11_
  10.2 0.9 slice.46.refs_1_
  11.0 0.6 slice.37
  11.6 0.0 copy-start.14
  11.6 0.0 copy-start.15
  11.7 0.9 reshape.147
  12.6 1.1 copy.58
  13.7 0.9 copy.60
  14.5 0.1 copy.42
  14.6 0.7 reshape.130.refs_5_
  15.4 0.3 dynamic_update_slice.3
  15.7 0.6 pad_maximum_fusion.2.refs_4_
  16.3 1.9 fusion.6
  18.2 1.3 pad_maximum_fusion
  19.5 187.2 %attend_first.1 = (bf16[8,256,2048]{2,1,0:T(8,128)(2,1)}, bf16[8,160,2048]{2,1,0:T(8,128)(2,1)}, bf16[3,2048,256]{2,1,0:T(8,128)(2,1)}, bf16[4,64,2048]{2,1,0:T(...) custom-call(bf16[256,2048]{1,0:T(8,128)(2,1)} %bitcast.74, ...), custom_call_target="tpu_custom_call" | custom-call | bytes 756000000 | tf_op jit(solution)/shard_map/attend_first/pallas_call | solution.py:776
  206.7 9.5 copy.44
  216.1 0.0 all-gather.3.cloned.1.call-update
  216.2 0.0 reduce-scatter.5.cloned.1.call-start
  216.2 0.8 slice.48.c_ref
  217.0 0.1 copy-done.9
  217.1 1.1 reshape_reshape.6.router_ref
  218.1 1.6 reshape.133.routes_ref
  219.7 0.6 fusion.13
  220.3 174.3 %middle_rows.1 = (f32[256,2048]{1,0:T(8,128)}, bf16[256,2048]{1,0:T(8,128)(2,1)}, bf16[8,256,2048]{2,1,0:T(8,128)(2,1)}) custom-call(bf16[8,256,256]{2,1,0:T(8,128)(2,1)} %get-tuple-element.49.refs_0_.refs_2_, bf16[256,2048]{1,0:T(8,128)(2,1)} %bitcast.80, bf16[256,2048]{1,0:T(8,128)(2,1)} %bitcast.75, f32[1,2048]{1,0:T(1,128)} %get-tuple-element.117.refs_3_), custom_call_target="tpu_custom_call" | custom-call | bytes 630000000 | tf_op jit(solution)/shard_map/middle_rows/pallas_call | solution.py:938
  394.6 17.8 %experts_dispatch.1 = (bf16[4,8,72,2048]{3,2,1,0:T(8,128)(2,1)}, f32[4,8,72,1]{3,2,1,0:T(8,128)}, f32[8,256,4]{2,1,0:T(8,128)}, f32[8,256,4]{2,1,0:T(8,128)}) custom-call(s32[1]{0:T(128)} %bitcast.9.me_ref, bf16[8,256,2048]{2,1,0:T(8,128)(2,1)} %get-tuple-element.53.ffn_ref, s32[8,256,8]{2,1,0:T(8,128)} %reshape.133.routes_ref, ...), custom_call_target="tpu_custom_call" | custom-call | bytes 43200000 | tf_op jit(solution)/shard_map/experts_dispatch/pallas_call | solution.py:1436
  412.5 14.6 %all-gather.3.cloned.1.call-done = bf16[4,2048,2,1024]{3,1,2,0:T(8,128)(2,1)} async-done(((bf16[4,512,2,1024]{3,1,2,0:T(8,128)(2,1)}), bf16[4,2048,2,1024]{3,1,2,0:T(8,128)(2,1)}) %all-gather.3.cloned.1.call-update) | async-done | bytes 33554448 | tf_op jit(solution)/shard_map/all_gather | solution.py:1893
  427.1 52.6 %experts_forward.1 = (bf16[4,576,2048]{2,1,0:T(8,128)(2,1)}, bf16[4,576,1024]{2,1,0:T(8,128)(2,1)}, bf16[4,576,1024]{2,1,0:T(8,128)(2,1)}, bf16[4,576,1024]{2,1,0:T(8,128)(2,1)}, bf16[8,96,2048]{2,1,0:T(8,128)(2,1)}) custom-call(bf16[4,576,2048]{2,1,0:T(8,128)(2,1)} %bitcast.69, bf16[4,2,2048,1024]{3,2,1,0:T(8,128)(2,1)} %bitcast.67, ...), custom_call_target="tpu_custom_call" | custom-call | bytes 234000000 | tf_op jit(solution)/shard_map/experts_forward/pallas_call | solution.py:1545
  479.7 19.2 %experts_mix.1 = (bf16[8,256,2048]{2,1,0:T(8,128)(2,1)}, bf16[4,8,72,2048]{3,2,1,0:T(8,128)(2,1)}, f32[8,4,256]{2,1,0:T(4,128)}) custom-call(bf16[4,8,72,2048]{3,2,1,0:T(8,128)(2,1)} %bitcast.79, bf16[8,160,2048]{2,1,0:T(8,128)(2,1)} %get-tuple-element.60.a_ref, bf16[8,96,2048]{2,1,0:T(8,128)(2,1)} %get-tuple-element.61.b_ref, ...), custom_call_target="tpu_custom_call" | custom-call | bytes 54000000 | tf_op jit(solution)/shard_map/experts_mix/pallas_call | solution.py:1605
  499.0 18.0 %experts_out_terms.1 = bf16[4,1024,2048]{2,1,0:T(8,128)(2,1)} custom-call(bf16[4,576,1024]{2,1,0:T(8,128)(2,1)} %get-tuple-element.58.hidden_ref, bf16[4,576,2048]{2,1,0:T(8,128)(2,1)} %bitcast.71), custom_call_target="tpu_custom_call" | custom-call | bytes 54000000 | tf_op jit(solution)/shard_map/experts_out_terms/pallas_call | solution.py:1643
  517.0 0.0 reduce-scatter.5.cloned.1.call-update
  517.0 0.0 reduce-scatter.3.cloned.1.call-start
  517.0 115.2 %experts_back.1 = (bf16[4,576,2048]{2,1,0:T(8,128)(2,1)}, bf16[4,2,2048,1024]{3,2,1,0:T(8,128)(2,1)}, f32[256,2048]{1,0:T(8,128)}) custom-call(bf16[4,576,2048]{2,1,0:T(8,128)(2,1)} %bitcast.70, bf16[4,576,2048]{2,1,0:T(8,128)(2,1)} %bitcast.72, bf16[4,576,1024]{2,1,0:T(8,128)(2,1)} %get-tuple-element.67.gate_ref, ...), custom_call_target="tpu_custom_call" | custom-call | bytes 342000000 | tf_op jit(solution)/shard_map/experts_back/pallas_call | solution.py:1732
  632.2 0.0 reduce-scatter.3.cloned.1.call-update
  632.2 0.1 constant_dynamic-slice_fusion.1
  632.3 0.6 pad.4.refs_8_
  632.9 2.0 fusion.14
  635.0 0.3 multiply_reduce_fusion.3
  635.3 0.2 multiply_reduce_fusion.2
  635.5 91.4 %rows_back.1 = (f32[256,2048]{1,0:T(8,128)}, f32[8,4,256]{2,1,0:T(4,128)}) custom-call(bf16[4,8,72,2048]{3,2,1,0:T(8,128)(2,1)} %bitcast.76, f32[8,256,4]{2,1,0:T(8,128)} %get-tuple-element.63.slot_ref, f32[8,4,256]{2,1,0:T(4,128)} %get-tuple-element.72.prob_ref), custom_call_target="tpu_custom_call" | custom-call | bytes 324000000 | tf_op jit(solution)/shard_map/rows_back/pallas_call | solution.py:1810
  726.9 0.8 reshape.139
  727.8 2.8 fusion.15
  730.5 2.2 reshape.142.refs_4_
  732.8 3.5 multiply_reduce_fusion
  736.2 1.7 fusion.12.refs_0_
  737.9 121.9 %attend_back.1 = (bf16[3,8,256,256]{3,2,1,0:T(8,128)(2,1)}, bf16[256,2048]{1,0:T(8,128)(2,1)}, f32[8,256]{1,0:T(8,128)}) custom-call(bf16[256,2048]{1,0:T(8,128)(2,1)} %fusion.12.refs_0_, bf16[256,2048]{1,0:T(8,128)(2,1)} %bitcast.81, bf16[8,256,256]{2,1,0:T(8,128)(2,1)} %get-tuple-element.49.refs_0_.refs_2_, ...), custom_call_target="tpu_custom_call" | custom-call | bytes 468000000 | tf_op jit(solution)/shard_map/attend_back/pallas_call | solution.py:1101
  859.8 130.7 %last_sums.1 = (f32[256,2048]{1,0:T(8,128)}, bf16[8,192,256]{2,1,0:T(8,128)(2,1)}, bf16[64,2048]{1,0:T(8,128)(2,1)}, f32[24,128]{1,0:T(8,128)}) custom-call(bf16[3,8,256,256]{3,2,1,0:T(8,128)(2,1)} %get-tuple-element.81.refs_0_, bf16[8,256,2048]{2,1,0:T(8,128)(2,1)} %get-tuple-element.82.refs_1_, bf16[3,2048,256]{2,1,0:T(8,128)(2,1)} %get-tuple-element.83.refs_2_, ...), custom_call_target="tpu_custom_call" | custom-call | bytes 396000000 | tf_op jit(solution)/shard_map/last_sums/pallas_call | solution.py:1351
  990.5 2.5 copy.59
  993.0 2.2 reshape.145
  995.2 1.3 maximum_convert_fusion
  996.4 2.7 copy.48
  999.1 0.1 reshape_reshape.7
  999.2 0.7 copy.49
  999.9 0.6 constant_dynamic-slice_fusion
  1000.5 2.2 fusion.5
  1002.8 5.2 fusion.4
  1008.0 6.8 convert_element_type.59
  1014.8 17.7 %copy.50 = f32[4,512,2,1024]{3,2,1,0:T(2,128)} copy(bf16[4,512,2,1024]{3,1,2,0:T(8,128)(2,1)} %reduce-scatter.3.cloned.1.call-done) | data formatting | bytes 25165824
  (44 shorter events, 0.2 us)
Async XLA Ops:
  7.2 0.8 copy-start.13
  7.2 1.0 copy-start.11
  7.2 3.0 copy-start.4
  7.2 405.3 %all-gather.5.cloned.1.call-start = ((), (), s32[]{:S(2)}) async-start(), calls=%async_computation.3 | async-start | bytes 20971520 | tf_op jit(solution)/shard_map/all_gather | solution.py:1894
  7.9 3.1 copy-start.7
  7.9 419.1 %all-gather.3.cloned.1.call-start = ((), (), s32[]{:S(2)}) async-start(), calls=%async_computation.2 | async-start | bytes 41943040 | tf_op jit(solution)/shard_map/all_gather | solution.py:1893
  11.6 2.9 copy-start.14
  11.6 3.7 copy-start.15
  216.1 0.9 copy-start.9
  216.1 2.0 copy-start.10
  216.2 791.9 %reduce-scatter.5.cloned.1.call-start = ((), (), s32[]{:S(2)}) async-start(), calls=%async_computation.5 | async-start | bytes 20971520 | tf_op jit(solution)/shard_map/reduce_scatter | solution.py:1927
  517.0 497.8 %reduce-scatter.3.cloned.1.call-start = ((), (), s32[]{:S(2)}) async-start(), calls=%async_computation.4 | async-start | bytes 41943040 | tf_op jit(solution)/shard_map/reduce_scatter | solution.py:1940
  632.2 2.8 copy-start.1
  632.2 3.0 copy-start
  732.8 3.5 copy-start.5
  736.2 1.7 copy-start.2
  990.5 4.7 copy-start.8
  996.4 2.7 copy-start.12
  999.9 2.9 copy-start.3
  999.9 2.9 copy-start.6
Sparse Core Ops, SparseCore 0:
  9.6 128.2 all-gather.4
  216.3 210.7 all-gather.2
  517.1 125.1 reduce-scatter.4
  644.9 235.0 reduce-scatter.2
